TPU v7x, 256 devices: a whole 4x4x8 slice. The times are simulated.
256 devices in a mesh: row: 32 (over y, x, core), col: 8 (over z).
Axes of the slice: x: 4, y: 4, z: 8, core: 2. Of those that a mesh axis runs over, the one named last changes fastest.
Arguments:
- matrix: float32 [20480, 16384], P('row', 'col'), may hold values from -100 to 100
- pivots: int32 [256], replicated, may hold values from 0 to 16383, as said below
- sketch: float32 [264, 16384], P(None, ('col', 'row')), may hold values from -6 to 6
Outputs:
- upper_rows: float32 [256, 16384], P(None, ('col', 'row'))
- trailing: float32 [20480, 16384], P('row', 'col')
- new_sketch: float32 [264, 16384], P(None, ('col', 'row'))
Inputs may be any that keep to these rules, and one draw needn't show every extreme that they name: `pivots`: 256 distinct column indices.
All inputs are finite; a program needn't handle non-finite values.
Results may differ from a plain program's by a relative error of at most 0.0003.
Values sent between devices are 32-bit elements; how exact they have to be, the bound alone decides.
No kernel may reach another device: no remote copies, remote signals or barrier semaphores. Data moves between devices by JAX's collectives and lax.ppermute only.
A program may use at most 128 MiB of HBM per device.

v0:
```python
import functools

import jax
import jax.numpy as jnp
from jax import lax
from jax.experimental import pallas as pl
from jax.experimental.pallas import tpu as pltpu
from jax.sharding import Mesh
from jax.sharding import PartitionSpec as P

ROW = ("row_0", "row_1", "row_2")
CHIPS = ("row_0", "row_1")
COL_ROW = ("col", "row_0", "row_1", "row_2")

f32, bf16, i32 = jnp.float32, jnp.bfloat16, jnp.int32
highest = lax.Precision.HIGHEST
NN = (((1,), (0,)), ((), ()))
NT = (((1,), (1,)), ((), ()))
TN = (((0,), (0,)), ((), ()))


def iota(shape, dim):
    return lax.broadcasted_iota(i32, shape, dim)


def dot(a, b, dims=NN, precision=None):
    return lax.dot_general(a, b, dims, precision=precision, preferred_element_type=f32)


def split(a, pieces):
    out = []
    for _ in range(pieces - 1):
        top = a.astype(bf16)
        out.append(top)
        a = a - top.astype(f32)
    return (*out, a.astype(bf16))


def picked(a, onehot, dims=NN):
    hi, mid, lo = split(a, 3)
    return dot(hi, onehot, dims) + dot(mid, onehot, dims) + dot(lo, onehot, dims)


def partners(prow, pcol):
    n = prow.shape[1]
    drow, dcol = iota((1, n), 1), iota((n, 1), 0)
    gone_col = jnp.max(jnp.where(prow == dcol, 1, 0), axis=1, keepdims=True)
    gone_row = jnp.max(jnp.where(pcol == drow, 1, 0), axis=0, keepdims=True)
    rank_d = jnp.sum(jnp.where(drow < dcol, 1 - gone_row, 0), axis=1, keepdims=True)
    rank_v = jnp.sum(jnp.where((pcol < prow) & (pcol >= n), 1, 0), axis=0, keepdims=True)
    match = (rank_d == rank_v) & (gone_col == 0) & (prow >= n)
    return jnp.sum(jnp.where(match, dcol + 1, 0), axis=0, keepdims=True) - 1


def wanted(prow, partner, c, columns):
    n = prow.shape[1]
    off = c * columns
    own = (prow >= off) & (prow < off + columns)
    sel = jnp.where(own, prow - off, jnp.where(c == 0, partner, -1))
    own_disp = jnp.where(own & (prow >= n) & (c == 0), partner, -1)
    return own, sel, own_disp


def extract_kernel(c_ref, prow_ref, pcol_ref, a_ref, m_ref, d_ref, e_ref, e2_ref):
    columns = a_ref.shape[1]
    n = prow_ref.shape[1]

    @pl.when(pl.program_id(0) == 0)
    def _():
        prow = prow_ref[...]
        _, sel, disp = wanted(prow, partners(prow, pcol_ref[...]), c_ref[0], columns)
        for s in range(0, columns, n):
            e_ref[s : s + n, :] = jnp.where(iota((n, n), 0) + s == sel, 1.0, 0.0).astype(bf16)
        e2_ref[...] = jnp.where(iota((n, n), 0) == disp, 1.0, 0.0).astype(bf16)

    a = a_ref[...]
    m_ref[...] = picked(a, e_ref[...])
    d_ref[...] = picked(a[:, :n], e2_ref[...])


def extract(c, prow, pcol, a):
    rows, columns = a.shape
    n = prow.shape[1]
    tm = 128
    small = lambda shape: pl.BlockSpec(shape, lambda i, *_: (0, 0))
    return pl.pallas_call(
        extract_kernel,
        out_shape=(jax.ShapeDtypeStruct((rows, n), f32),) * 2,
        grid_spec=pltpu.PrefetchScalarGridSpec(
            num_scalar_prefetch=1,
            grid=(rows // tm,),
            in_specs=[small((1, n)), small((n, 1)), pl.BlockSpec((tm, columns), lambda i, *_: (i, 0))],
            out_specs=(pl.BlockSpec((tm, n), lambda i, *_: (i, 0)),) * 2,
            scratch_shapes=[pltpu.VMEM((columns, n), bf16), pltpu.VMEM((n, n), bf16)],
        ),
        name="extract",
    )(c, prow, pcol, a)


def holder_kernel(columns, prow_ref, r_ref, o_ref):
    peers = r_ref.shape[0]
    prow = prow_ref[...]
    owns = [(prow >= s * columns) & (prow < (s + 1) * columns) for s in range(peers)]
    panel = jnp.zeros(r_ref.shape[1:], f32)
    for s in range(peers):
        panel = jnp.where(owns[s], r_ref[s], panel)
    o_ref[0] = panel
    for s in range(1, peers):
        o_ref[s] = jnp.where(owns[s], r_ref[0], panel)


def holder(prow, received, columns):
    return pl.pallas_call(
        functools.partial(holder_kernel, columns),
        out_shape=jax.ShapeDtypeStruct(received.shape, f32),
        name="holder",
    )(prow, received)


def gram_kernel(columns, c_ref, prow_ref, x_ref, m_ref, d0_ref, p_ref, d_ref, g_ref, dp_ref):
    c = c_ref[0]
    prow = prow_ref[...]
    own = (prow >= c * columns) & (prow < (c + 1) * columns)
    x = x_ref[...]
    panel = jnp.where(own, m_ref[...], x)
    moved = jnp.where(c == 0, d0_ref[...], jnp.where(own, x, 0.0))
    p_ref[...] = panel
    d_ref[...] = moved
    g_ref[...] = dot(panel, panel, TN, highest)
    dp_ref[...] = dot(moved, panel, TN, highest)


def gram(c, prow, x, m, d0, columns):
    rows, n = x.shape
    whole = lambda s: pl.BlockSpec(s, lambda *_: (0, 0))
    return pl.pallas_call(
        functools.partial(gram_kernel, columns),
        out_shape=tuple(jax.ShapeDtypeStruct(s, f32) for s in ((rows, n), (rows, n), (n, n), (n, n))),
        grid_spec=pltpu.PrefetchScalarGridSpec(
            num_scalar_prefetch=1,
            grid=(1,),
            in_specs=[whole((1, n))] + [whole((rows, n))] * 3,
            out_specs=tuple(whole(s) for s in ((rows, n), (rows, n), (n, n), (n, n))),
        ),
        name="gram",
    )(c, prow, x, m, d0)


def product_kernel(columns, ck_ref, prow_ref, a_ref, p_ref, g_ref, dp_ref, keep_ref, send_ref, r_ref):
    c, k = ck_ref[0], ck_ref[1]
    b = pl.program_id(0)
    tn = a_ref.shape[1]
    half = tn // 2
    n = prow_ref.shape[1]
    place = c * columns + b * tn + iota((tn, 1), 0)
    onehot = jnp.where(place == prow_ref[...], 1.0, 0.0)
    stays = 1.0 - jnp.max(onehot, axis=1, keepdims=True)
    stays = jnp.where(place < n, 0.0, stays)
    r = dot(a_ref[...], p_ref[...], TN, highest) * stays + dot(onehot, dp_ref[...], NN, highest)
    r_ref[...] = r

    @pl.when((c == 0) & (b < n // tn))
    def _():
        r_ref[...] = g_ref[pl.ds(jnp.minimum(b, n // tn - 1) * tn, tn), :]

    keep_ref[0] = r_ref[pl.ds(k * half, half), :]
    send_ref[0] = r_ref[pl.ds((1 - k) * half, half), :]


def product(ck, prow, a, p, g, dp):
    rows, columns = a.shape
    n = prow.shape[1]
    tn = 128
    whole = lambda s: pl.BlockSpec(s, lambda *_: (0, 0))
    return pl.pallas_call(
        functools.partial(product_kernel, columns),
        out_shape=(jax.ShapeDtypeStruct((columns // tn, tn // 2, n), f32),) * 2,
        grid_spec=pltpu.PrefetchScalarGridSpec(
            num_scalar_prefetch=1,
            grid=(columns // tn,),
            in_specs=[
                whole((1, n)),
                pl.BlockSpec((rows, tn), lambda b, *_: (0, b)),
                whole((rows, n)),
                whole((n, n)),
                whole((n, n)),
            ],
            out_specs=(pl.BlockSpec((1, tn // 2, n), lambda b, *_: (b, 0, 0)),) * 2,
            scratch_shapes=[pltpu.VMEM((tn, n), f32)],
        ),
        name="product",
    )(ck, prow, a, p, g, dp)


def permute_kernel(columns, c_ref, prow_ref, pcol_ref, a_ref, p_ref, d_ref, o_ref):
    c = c_ref[0]
    b = pl.program_id(0)
    tn = a_ref.shape[1]
    n = prow_ref.shape[1]
    start = c * columns + b * tn
    onehot = jnp.where(start + iota((tn, 1), 0) == prow_ref[...], 1.0, 0.0).astype(bf16)
    here = jnp.max(jnp.where(pcol_ref[...] == start + iota((1, tn), 1), 1, 0), axis=0, keepdims=True)
    o_ref[...] = jnp.where(here > 0, picked(d_ref[...], onehot, NT), a_ref[...])
    for s in range(n // tn):

        @pl.when((c == 0) & (b == s))
        def _():
            o_ref[...] = p_ref[:, s * tn : (s + 1) * tn]


def permute(c, prow, pcol, a, p, d):
    rows, columns = a.shape
    n = prow.shape[1]
    tn = 128
    whole = lambda s: pl.BlockSpec(s, lambda *_: (0, 0))
    return pl.pallas_call(
        functools.partial(permute_kernel, columns),
        out_shape=jax.ShapeDtypeStruct(a.shape, f32),
        grid_spec=pltpu.PrefetchScalarGridSpec(
            num_scalar_prefetch=1,
            grid=(columns // tn,),
            in_specs=[
                whole((1, n)),
                whole((n, 1)),
                pl.BlockSpec((rows, tn), lambda b, *_: (0, b)),
                whole((rows, n)),
                whole((rows, n)),
            ],
            out_specs=pl.BlockSpec((rows, tn), lambda b, *_: (0, b)),
        ),
        name="permute",
    )(c, prow, pcol, a, p, d)


def factor_kernel(g_ref, o_ref, t_ref):
    n = g_ref.shape[0]
    nb = 64
    t_ref[:, :n] = g_ref[...]
    t_ref[:, n:] = jnp.where(iota((n, n), 0) == iota((n, n), 1), 1.0, 0.0)
    eye = jnp.where(iota((nb, nb), 0) == iota((nb, nb), 1), 1.0, 0.0)
    below = iota((nb, 1), 0)
    for s in range(0, n, nb):
        t = jnp.concatenate([t_ref[s : s + nb, s : s + nb], eye], axis=1)
        scale = jnp.zeros((nb, 1), f32)
        for j in range(nb):
            row = t[j : j + 1, :]
            pivot = row[:, j : j + 1]
            scale = jnp.where(below == j, lax.rsqrt(pivot), scale)
            if j + 1 < nb:
                scaled = row * (1.0 / pivot)
                mult = jnp.where(below > j, t[:, j : j + 1], 0.0)
                t = t - mult * scaled
        inv = t[:, nb:] * scale
        y = dot(inv, t_ref[s : s + nb, :], NN, highest)
        o_ref[s : s + nb, :] = y[:, n:]
        if s + nb < n:
            t_ref[s + nb :, :] = t_ref[s + nb :, :] - dot(y[:, s + nb : n], y, TN, highest)


def factor(g):
    n = g.shape[0]
    return pl.pallas_call(
        factor_kernel,
        out_shape=jax.ShapeDtypeStruct((n, n), f32),
        scratch_shapes=[pltpu.VMEM((n, 2 * n), f32)],
        name="factor",
    )(g)


def basis_kernel(p_ref, inv_ref, hi_ref, lo_ref):
    hi_ref[...], lo_ref[...] = split(dot(p_ref[...], inv_ref[...], NT, highest), 2)


def basis_of(p, inverse):
    return pl.pallas_call(
        basis_kernel,
        out_shape=(jax.ShapeDtypeStruct(p.shape, bf16),) * 2,
        name="basis",
    )(p, inverse)


def trailing_kernel(k_ref, a_ref, hi_ref, lo_ref, inv_ref, mine_ref, other_ref, o_ref, s_ref):
    k = k_ref[0]
    half = mine_ref.shape[1]
    s_ref[pl.ds(k * half, half), :] = mine_ref[0]
    s_ref[pl.ds((1 - k) * half, half), :] = other_ref[0]
    u_hi, u_lo = split(dot(s_ref[...], inv_ref[...], NT, highest), 2)
    hi, lo = hi_ref[...], lo_ref[...]
    o_ref[...] = a_ref[...] - (dot(hi, u_hi, NT) + (dot(hi, u_lo, NT) + dot(lo, u_hi, NT)))


def trail(k, a, hi, lo, inverse, mine, other):
    rows, columns = a.shape
    blocks, half, n = mine.shape
    tn = 2 * half
    whole = lambda s: pl.BlockSpec(s, lambda *_: (0, 0))
    share = pl.BlockSpec((1, half, n), lambda b, *_: (b, 0, 0))
    return pl.pallas_call(
        trailing_kernel,
        out_shape=jax.ShapeDtypeStruct(a.shape, f32),
        grid_spec=pltpu.PrefetchScalarGridSpec(
            num_scalar_prefetch=1,
            grid=(blocks,),
            in_specs=[
                pl.BlockSpec((rows, tn), lambda b, *_: (0, b)),
                whole((rows, n)),
                whole((rows, n)),
                whole((n, n)),
                share,
                share,
            ],
            out_specs=pl.BlockSpec((rows, tn), lambda b, *_: (0, b)),
            scratch_shapes=[pltpu.VMEM((tn, n), f32)],
        ),
        name="trailing",
    )(k, a, hi, lo, inverse, mine, other)


def exchange(pieces, axis):
    return lax.all_to_all(pieces, axis, split_axis=0, concat_axis=0, tiled=True)


def to_all(piece, axis):
    return exchange(jnp.broadcast_to(piece[None], (lax.axis_size(axis), *piece.shape)), axis)


def per_device(matrix, pivots, sketch):
    c = lax.axis_index("col")
    r = lax.axis_index(ROW)
    k = lax.axis_index("row_2")
    cols, lanes = lax.axis_size("col"), lax.axis_size(ROW)
    rows, columns = matrix.shape
    n = pivots.shape[0]
    prow, pcol = pivots.reshape(1, n), pivots.reshape(n, 1)
    c1 = c.reshape(1).astype(i32)
    k1 = k.reshape(1).astype(i32)
    ck = jnp.stack([c, k]).astype(i32)

    mine, inside = extract(c1, prow, pcol, matrix)
    arrived = exchange(mine.reshape(cols, rows // cols, n), "col")
    x = exchange(holder(prow, arrived, columns), "col").reshape(rows, n)
    panel, displaced, gram_part, moved_part = gram(c1, prow, x, mine, inside, columns)

    gram_own = exchange(gram_part.reshape(lanes, n // lanes, n), ROW).sum(axis=0)
    keep, send = product(ck, prow, matrix, panel, gram_part, moved_part)
    swap = [(0, 1), (1, 0)]
    half = keep + lax.ppermute(send, "row_2", swap)
    share = exchange(half, CHIPS).sum(axis=0)
    own_all = to_all(share, CHIPS)
    gram_all = to_all(gram_own, ROW).reshape(n, n)
    permuted = permute(c1, prow, pcol, matrix, panel, displaced)
    other_all = lax.ppermute(own_all, "row_2", swap)
    inverse = factor(gram_all)
    hi, lo = basis_of(panel, inverse)
    trailing = trail(k1, permuted, hi, lo, inverse, own_all, other_all)
    upper_share = dot(inverse, share, NT, highest)

    pieces = sketch.shape[1]
    size = -(-sketch.shape[0] // lanes)
    padded = jnp.pad(sketch, ((0, size * lanes - sketch.shape[0]), (0, 0)))
    partner = partners(prow, pcol)
    own, sel, disp = wanted(prow, partner, c, columns)
    place = r * pieces + iota((pieces, 1), 0)
    pick = jnp.concatenate([jnp.where(place == sel, 1.0, 0.0), jnp.where(place == disp, 1.0, 0.0)], 1)
    part = dot(padded, pick, NN, highest).reshape(lanes, size, 2 * n)
    line = exchange(part, ROW).sum(axis=0)
    slots, inside_s = line[:, :n], line[:, n:]
    got = to_all(slots, "col")
    owner = [(prow >= s * columns) & (prow < (s + 1) * columns) for s in range(cols)]
    front = functools.reduce(lambda acc, s: jnp.where(owner[s], got[s], acc), range(cols), slots)
    back = jnp.where(c == 0, inside_s, jnp.where(own, got[0], 0.0))
    both = to_all(jnp.concatenate([front, back], 1), ROW).reshape(lanes * size, 2 * n)[: sketch.shape[0]]
    fronts, backs = both[:, :n], both[:, n:]
    glob = c * columns + r * pieces
    hit = jnp.where(glob + iota((pieces, 1), 0) == prow, 1.0, 0.0)
    lead = jnp.where((glob + iota((pieces, 1), 0) == iota((1, n), 1)), 1.0, 0.0)
    stays = (jnp.max(jnp.where(pcol == glob + iota((1, pieces), 1), 1, 0), axis=0, keepdims=True) == 0) & (
        glob + iota((1, pieces), 1) >= n
    )
    moved = jnp.where(stays, sketch, dot(backs, hit, NT, highest) + dot(fronts, lead, NT, highest))
    solved = dot(inverse, upper_share, TN, highest)
    new_sketch = moved - dot(fronts, solved, NN, highest)
    return (upper_share, trailing, new_sketch)


def solution(mesh):
    finer = Mesh(mesh.devices.reshape(4, 4, 2, mesh.shape["col"]), ("row_0", "row_1", "row_2", "col"))
    return jax.shard_map(
        per_device,
        mesh=finer,
        in_specs=(P(ROW, "col"), P(), P(None, COL_ROW)),
        out_specs=(P(None, COL_ROW), P(ROW, "col"), P(None, COL_ROW)),
        check_vma=False,
    )
```

profile of v0, /device:TPU:1, one launch (start us, length us, event | category | flops | bytes accessed | tf_op | source)
XLA Modules:
  0.0 268.6 jit_solution(7678529652800398070)
XLA Ops:
  0.7 1.5 copy.8.pcol_ref
  2.2 7.3 %extract.1 = (f32[640,256]{1,0:T(8,128)}, f32[640,256]{1,0:T(8,128)}) custom-call(s32[1]{0:T(128)} %bitcast.c_ref, s32[1,256]{1,0:T(1,128)} %bitcast.63, s32[256,1]{1,0:T(8,128)} %copy.8.pcol_ref, f32[640,2048]{1,0:T(8,128)} %a_ref.5), custom_call_target="tpu_custom_call" | custom-call | tf_op jit(solution)/shard_map/extract/pallas_call | solution.py:86
  9.5 9.0 %all-to-all-start = ((f32[8,80,256]{2,1,0:T(8,128)}), f32[8,80,256]{2,1,0:T(8,128)S(1)}, u32[]{:S(2)}, u32[]{:S(2)}) async-start(f32[8,80,256]{2,1,0:T(8,128)} %bitcast.59), calls=%async_computation | async-start | bytes 1310720 | tf_op jit(solution)/shard_map/all_to_all | solution.py:320
  19.9 1.1 reshape.135
  21.0 18.3 %all-to-all-done.r_ref = f32[8,80,256]{2,1,0:T(8,128)S(1)} async-done(((f32[8,80,256]{2,1,0:T(8,128)}), f32[8,80,256]{2,1,0:T(8,128)S(1)}, u32[]{:S(2)}, u32[]{:S(2)}) %all-to-all-start) | async-done | bytes 655392 | tf_op jit(solution)/shard_map/all_to_all | solution.py:320
  39.3 7.6 %all-to-all-start.6 = ((f32[32,9,512]{2,1,0:T(8,128)}), f32[32,9,512]{2,1,0:T(8,128)S(1)}, u32[]{:S(2)}, u32[]{:S(2)}) async-start(f32[32,9,512]{2,1,0:T(8,128)} %reshape.135), calls=%async_computation.6 | async-start | bytes 2097152 | tf_op jit(solution)/shard_map/all_to_all | solution.py:320
  46.9 2.0 holder.1
  48.9 15.0 %all-to-all-done.6 = f32[32,9,512]{2,1,0:T(8,128)S(1)} async-done(((f32[32,9,512]{2,1,0:T(8,128)}), f32[32,9,512]{2,1,0:T(8,128)S(1)}, u32[]{:S(2)}, u32[]{:S(2)}) %all-to-all-start.6) | async-done | bytes 589856 | tf_op jit(solution)/shard_map/all_to_all | solution.py:320
  63.9 3.5 %all-to-all-start.1 = ((f32[8,80,256]{2,1,0:T(8,128)}), f32[8,80,256]{2,1,0:T(8,128)S(1)}, u32[]{:S(2)}, u32[]{:S(2)}) async-start(f32[8,80,256]{2,1,0:T(8,128)} %holder.1), calls=%async_computation.1 | async-start | bytes 1310720 | tf_op jit(solution)/shard_map/all_to_all | solution.py:320
  67.5 20.6 %all-to-all-done.1 = f32[8,80,256]{2,1,0:T(8,128)S(1)} async-done(((f32[8,80,256]{2,1,0:T(8,128)}), f32[8,80,256]{2,1,0:T(8,128)S(1)}, u32[]{:S(2)}, u32[]{:S(2)}) %all-to-all-start.1) | async-done | bytes 655392 | tf_op jit(solution)/shard_map/all_to_all | solution.py:320
  88.8 3.4 %all-to-all-start.7 = ((f32[8,9,256]{2,1,0:T(8,128)}), f32[8,9,256]{2,1,0:T(8,128)S(1)}, u32[]{:S(2)}, u32[]{:S(2)}) async-start(f32[8,9,256]{2,1,0:T(8,128)} %broadcast_in_dim.163), calls=%async_computation.7 | async-start | bytes 262144 | tf_op jit(solution)/shard_map/all_to_all | solution.py:320
  92.8 3.8 %gram.1 = (f32[640,256]{1,0:T(8,128)}, f32[640,256]{1,0:T(8,128)}, f32[256,256]{1,0:T(8,128)}, f32[256,256]{1,0:T(8,128)}) custom-call(s32[1]{0:T(128)} %bitcast.c_ref, s32[1,256]{1,0:T(1,128)} %bitcast.65, f32[640,256]{1,0:T(8,128)} %bitcast.60, f32[640,256]{1,0:T(8,128)} %get-tuple-element.13.m_ref, f32[640,256]{1,0:T(8,128)} %get-tuple-element.14.d0_ref), custom_call_target="tpu_custom_call" | custom-call | tf_op jit(solution)/shard_map/gram/pallas_call | solution.py:136
  96.7 16.3 %product.1 = (f32[16,64,256]{2,1,0:T(8,128)}, f32[16,64,256]{2,1,0:T(8,128)}) custom-call(s32[2]{0:T(128)} %pad_add_fusion.ck_ref, s32[1,256]{1,0:T(1,128)} %bitcast.66, f32[640,2048]{1,0:T(8,128)} %a_ref.5, f32[640,256]{1,0:T(8,128)} %get-tuple-element.16.p_ref, f32[256,256]{1,0:T(8,128)} %get-tuple-element.15.g_ref, f32[256,256]{1,0:T(8,128)} %get-tuple-element.17.dp_ref), custom_call_target="tpu_custom_call" | custom-call | tf_op jit(solution)/shard_map/product/pallas_call | solution.py:175
  113.5 1.2 broadcast_in_dim.173
  114.6 3.8 %all-to-all-start.8 = ((f32[32,9,512]{2,1,0:T(8,128)}), f32[32,9,512]{2,1,0:T(8,128)S(1)}, u32[]{:S(2)}, u32[]{:S(2)}) async-start(f32[32,9,512]{2,1,0:T(8,128)} %broadcast_in_dim.173), calls=%async_computation.8 | async-start | bytes 2097152 | tf_op jit(solution)/shard_map/all_to_all | solution.py:320
  118.5 1.4 add.67
  119.8 15.7 %all-to-all-done.8 = f32[32,9,512]{2,1,0:T(8,128)S(1)} async-done(((f32[32,9,512]{2,1,0:T(8,128)}), f32[32,9,512]{2,1,0:T(8,128)S(1)}, u32[]{:S(2)}, u32[]{:S(2)}) %all-to-all-start.8) | async-done | bytes 589856 | tf_op jit(solution)/shard_map/all_to_all | solution.py:320
  135.5 20.0 %all_to_all.45 = f32[16,64,256]{2,1,0:T(8,128)S(1)} all-to-all(f32[16,64,256]{2,1,0:T(8,128)S(1)} %add.67), channel_id=1, replica_groups=mesh['row_0'=4,'row_1'=4,'row_2'=2,'col'=8] {'row_0','row_1'}, dimensions={0} | all-to-all | bytes 2097152 | tf_op jit(solution)/shard_map/all_to_all | solution.py:320
  155.5 4.8 %all-to-all-start.2 = ((f32[32,8,256]{2,1,0:T(8,128)}), f32[32,8,256]{2,1,0:T(8,128)S(1)}, u32[]{:S(2)}, u32[]{:S(2)}) async-start(f32[32,8,256]{2,1,0:T(8,128)} %bitcast.5), calls=%async_computation.2 | async-start | bytes 524288 | tf_op jit(solution)/shard_map/all_to_all | solution.py:320
  160.4 8.9 %all-to-all-done.2 = f32[32,8,256]{2,1,0:T(8,128)S(1)} async-done(((f32[32,8,256]{2,1,0:T(8,128)}), f32[32,8,256]{2,1,0:T(8,128)S(1)}, u32[]{:S(2)}, u32[]{:S(2)}) %all-to-all-start.2) | async-done | bytes 262176 | tf_op jit(solution)/shard_map/all_to_all | solution.py:320
  169.3 1.1 broadcast_in_dim.152
  170.4 3.7 %all-to-all-start.5 = ((f32[16,64,256]{2,1,0:T(8,128)}), f32[16,64,256]{2,1,0:T(8,128)S(1)}, u32[]{:S(2)}, u32[]{:S(2)}) async-start(f32[16,64,256]{2,1,0:T(8,128)} %broadcast_in_dim.152), calls=%async_computation.5 | async-start | bytes 2097152 | tf_op jit(solution)/shard_map/all_to_all | solution.py:320
  174.4 17.9 %all-to-all-done.5.mine_ref = f32[16,64,256]{2,1,0:T(8,128)S(1)} async-done(((f32[16,64,256]{2,1,0:T(8,128)}), f32[16,64,256]{2,1,0:T(8,128)S(1)}, u32[]{:S(2)}, u32[]{:S(2)}) %all-to-all-start.5) | async-done | bytes 1048608 | tf_op jit(solution)/shard_map/all_to_all | solution.py:320
  192.3 0.8 broadcast_in_dim.151
  193.1 4.5 %all-to-all-start.3 = ((f32[32,8,256]{2,1,0:T(8,128)}), f32[32,8,256]{2,1,0:T(8,128)S(1)}, u32[]{:S(2)}, u32[]{:S(2)}) async-start(f32[32,8,256]{2,1,0:T(8,128)} %broadcast_in_dim.151), calls=%async_computation.3 | async-start | bytes 524288 | tf_op jit(solution)/shard_map/all_to_all | solution.py:320
  199.1 14.4 %permute.1.a_ref = f32[640,2048]{1,0:T(8,128)} custom-call(s32[1]{0:T(128)} %bitcast.c_ref, s32[1,256]{1,0:T(1,128)} %bitcast.67, s32[256,1]{1,0:T(8,128)} %copy.8.pcol_ref, f32[640,2048]{1,0:T(8,128)} %a_ref.5, f32[640,256]{1,0:T(8,128)} %get-tuple-element.16.p_ref, f32[640,256]{1,0:T(8,128)} %get-tuple-element.20.d_ref), custom_call_target="tpu_custom_call" | custom-call | tf_op jit(solution)/shard_map/permute/pallas_call | solution.py:216
  214.2 27.2 %factor.1.inv_ref = f32[256,256]{1,0:T(8,128)} custom-call(f32[256,256]{1,0:T(8,128)} %bitcast.61), custom_call_target="tpu_custom_call" | custom-call | tf_op jit(solution)/shard_map/factor/pallas_call | solution.py:262
  241.4 2.8 %basis.1 = (bf16[640,256]{1,0:T(8,128)(2,1)}, bf16[640,256]{1,0:T(8,128)(2,1)}) custom-call(f32[640,256]{1,0:T(8,128)} %get-tuple-element.16.p_ref, f32[256,256]{1,0:T(8,128)} %factor.1.inv_ref), custom_call_target="tpu_custom_call" | custom-call | tf_op jit(solution)/shard_map/basis/pallas_call | solution.py:275
  244.2 1.3 fusion.33
  245.5 1.2 fusion.34
  246.7 1.1 convolution_subtract_fusion
  247.8 20.8 %trailing.1 = f32[640,2048]{1,0:T(8,128)} custom-call(s32[1]{0:T(128)} %bitcast.7.k_ref, f32[640,2048]{1,0:T(8,128)} %permute.1.a_ref, bf16[640,256]{1,0:T(8,128)(2,1)} %get-tuple-element.21.hi_ref, bf16[640,256]{1,0:T(8,128)(2,1)} %get-tuple-element.22.lo_ref, f32[256,256]{1,0:T(8,128)} %factor.1.inv_ref, f32[16,64,256]{2,1,0:T(8,128)} %copy-done, ...), custom_call_target="tpu_custom_call" | custom-call | tf_op jit(solution)/shard_map/trailing/pallas_call | solution.py:298
  (49 shorter events, 5.8 us)
Async XLA Ops:
  0.6 17.9 %copy-start.6 = (s32[256]{0:T(256)S(1)}, s32[256]{0:T(256)}, u32[]{:S(2)}) copy-start(s32[256]{0:T(256)} %param.4) | copy-start | bytes 3076
  0.6 18.6 %copy-start.4 = (f32[264,64]{0,1:T(8,128)S(1)}, f32[264,64]{0,1:T(8,128)}, u32[]{:S(2)}) copy-start(f32[264,64]{0,1:T(8,128)} %param.5) | copy-start | bytes 202756
  9.5 29.8 %all-to-all-start = ((f32[8,80,256]{2,1,0:T(8,128)}), f32[8,80,256]{2,1,0:T(8,128)S(1)}, u32[]{:S(2)}, u32[]{:S(2)}) async-start(f32[8,80,256]{2,1,0:T(8,128)} %bitcast.59), calls=%async_computation | async-start | bytes 1310720 | tf_op jit(solution)/shard_map/all_to_all | solution.py:320
  39.3 7.6 %copy-start.1 = (f32[8,80,256]{2,1,0:T(8,128)}, f32[8,80,256]{2,1,0:T(8,128)S(1)}, u32[]{:S(2)}) copy-start(f32[8,80,256]{2,1,0:T(8,128)S(1)} %all-to-all-done.r_ref) | copy-start | bytes 1966084
  39.3 24.6 %all-to-all-start.6 = ((f32[32,9,512]{2,1,0:T(8,128)}), f32[32,9,512]{2,1,0:T(8,128)S(1)}, u32[]{:S(2)}, u32[]{:S(2)}) async-start(f32[32,9,512]{2,1,0:T(8,128)} %reshape.135), calls=%async_computation.6 | async-start | bytes 2097152 | tf_op jit(solution)/shard_map/all_to_all | solution.py:320
  63.9 24.2 %all-to-all-start.1 = ((f32[8,80,256]{2,1,0:T(8,128)}), f32[8,80,256]{2,1,0:T(8,128)S(1)}, u32[]{:S(2)}, u32[]{:S(2)}) async-start(f32[8,80,256]{2,1,0:T(8,128)} %holder.1), calls=%async_computation.1 | async-start | bytes 1310720 | tf_op jit(solution)/shard_map/all_to_all | solution.py:320
  88.1 4.7 %copy-start.2 = (f32[8,80,256]{2,1,0:T(8,128)}, f32[8,80,256]{2,1,0:T(8,128)S(1)}, u32[]{:S(2)}) copy-start(f32[8,80,256]{2,1,0:T(8,128)S(1)} %all-to-all-done.1) | copy-start | bytes 1966084
  88.8 24.6 %all-to-all-start.7 = ((f32[8,9,256]{2,1,0:T(8,128)}), f32[8,9,256]{2,1,0:T(8,128)S(1)}, u32[]{:S(2)}, u32[]{:S(2)}) async-start(f32[8,9,256]{2,1,0:T(8,128)} %broadcast_in_dim.163), calls=%async_computation.7 | async-start | bytes 262144 | tf_op jit(solution)/shard_map/all_to_all | solution.py:320
  113.0 5.5 %collective-permute-start = (f32[16,64,256]{2,1,0:T(8,128)}, f32[16,64,256]{2,1,0:T(8,128)S(1)}, u32[]{:S(2)}, u32[]{:S(2)}) collective-permute-start(f32[16,64,256]{2,1,0:T(8,128)} %get-tuple-element.19), channel_id=1, source_target_pairs={{0,8},{8,0},{1,9},{9,1},{2,10},{10,2},{3,11},{11,3},{4,12},{12,4},... | collective-permute-start | bytes 3145736 | tf_op jit(solution)/shard_map/ppermute | solution.py:347
  114.6 20.8 %all-to-all-start.8 = ((f32[32,9,512]{2,1,0:T(8,128)}), f32[32,9,512]{2,1,0:T(8,128)S(1)}, u32[]{:S(2)}, u32[]{:S(2)}) async-start(f32[32,9,512]{2,1,0:T(8,128)} %broadcast_in_dim.173), calls=%async_computation.8 | async-start | bytes 2097152 | tf_op jit(solution)/shard_map/all_to_all | solution.py:320
  118.4 55.6 %copy-start.7 = (s32[256]{0:T(256)S(1)}, s32[256]{0:T(256)}, u32[]{:S(2)}) copy-start(s32[256]{0:T(256)} %param.4) | copy-start | bytes 3076
  155.5 13.8 %all-to-all-start.2 = ((f32[32,8,256]{2,1,0:T(8,128)}), f32[32,8,256]{2,1,0:T(8,128)S(1)}, u32[]{:S(2)}, u32[]{:S(2)}) async-start(f32[32,8,256]{2,1,0:T(8,128)} %bitcast.5), calls=%async_computation.2 | async-start | bytes 524288 | tf_op jit(solution)/shard_map/all_to_all | solution.py:320
  170.4 21.9 %all-to-all-start.5 = ((f32[16,64,256]{2,1,0:T(8,128)}), f32[16,64,256]{2,1,0:T(8,128)S(1)}, u32[]{:S(2)}, u32[]{:S(2)}) async-start(f32[16,64,256]{2,1,0:T(8,128)} %broadcast_in_dim.152), calls=%async_computation.5 | async-start | bytes 2097152 | tf_op jit(solution)/shard_map/all_to_all | solution.py:320
  192.3 21.2 %copy-start = (f32[16,64,256]{2,1,0:T(8,128)}, f32[16,64,256]{2,1,0:T(8,128)S(1)}, u32[]{:S(2)}) copy-start(f32[16,64,256]{2,1,0:T(8,128)S(1)} %all-to-all-done.5.mine_ref) | copy-start | bytes 3145732
  193.1 20.5 %all-to-all-start.3 = ((f32[32,8,256]{2,1,0:T(8,128)}), f32[32,8,256]{2,1,0:T(8,128)S(1)}, u32[]{:S(2)}, u32[]{:S(2)}) async-start(f32[32,8,256]{2,1,0:T(8,128)} %broadcast_in_dim.151), calls=%async_computation.3 | async-start | bytes 524288 | tf_op jit(solution)/shard_map/all_to_all | solution.py:320
  197.6 50.2 %collective-permute-start.1 = (f32[16,64,256]{2,1,0:T(8,128)S(1)}, f32[16,64,256]{2,1,0:T(8,128)}, u32[]{:S(2)}, u32[]{:S(2)}) collective-permute-start(f32[16,64,256]{2,1,0:T(8,128)S(1)} %all-to-all-done.5.mine_ref), channel_id=1, source_target_pairs={{0,8},{8,0},{1,9},{9,1},{2,10},{10,2},{3,11},{11,3},{4,12},{12,4},... | collective-permute-start | bytes 3145736 | tf_op jit(solution)/shard_map/ppermute | solution.py:352
  213.5 0.7 copy-start.3
  245.5 23.2 %copy-start.5 = (f32[256,64]{0,1:T(8,128)}, f32[256,64]{0,1:T(8,128)S(1)}, u32[]{:S(2)}) copy-start(f32[256,64]{0,1:T(8,128)S(1)} %fusion.33) | copy-start | bytes 196612
where the time goes:
time: 271 us; the launch traced here: 269 us
  waiting for transfers between devices  96.4 us (36%)
  Pallas kernels  94.7 us (35%)
  starting transfers between devices  41.3 us (15%)
  blocking collectives  20 us (7%)
  local copies, waits for them, and re-layouts  7.11 us (3%)
  matrix products  5.15 us (2%)
  other arithmetic  2.96 us (1%)
    all_to_all x8, waiting for transfers between devices, exchange(): return lax.all_to_all(pieces, axis, split_axis=0, concat_axis=0, tiled=True)  96.4 us
    all_to_all x8, starting transfers between devices, exchange(): return lax.all_to_all(pieces, axis, split_axis=0, concat_axis=0, tiled=True)  40.3 us
    pallas_call x1, Pallas kernels, factor(): pl.pallas_call(factor_kernel, out_shape=jax.ShapeDtypeStruct((n, n), f32)...  27.2 us
    pallas_call x1, Pallas kernels, trail(): pl.pallas_call(trailing_kernel, out_shape=jax.ShapeDtypeStruct(a.shape, f...  20.8 us
    all_to_all x1, blocking collectives, exchange(): return lax.all_to_all(pieces, axis, split_axis=0, concat_axis=0, tiled=True)  20 us
    pallas_call x1, Pallas kernels, product(): pl.pallas_call(functools.partial(product_kernel, columns), out_shape=(jax...  16.3 us
    pallas_call x1, Pallas kernels, permute(): pl.pallas_call(functools.partial(permute_kernel, columns), out_shape=jax....  14.4 us
    pallas_call x1, Pallas kernels, extract(): pl.pallas_call(extract_kernel, out_shape=(jax.ShapeDtypeStruct((rows, n),...  7.31 us
  transfers between devices with their start and end apart: 10, of which 6 were waited for; matrix products, arithmetic and copies ran while one was open for 4% of the time, Pallas kernels for 25%

commit v1 on v0

v1 whole, which is shorter than its diff:
```python
import functools

import jax
import jax.numpy as jnp
from jax import lax
from jax.experimental import pallas as pl
from jax.experimental.pallas import tpu as pltpu
from jax.sharding import Mesh
from jax.sharding import PartitionSpec as P


ROW = ("row_0", "row_1", "row_2")
CHIPS = ("row_0", "row_1")
COL_ROW = ("col", "row_0", "row_1", "row_2")

f32, bf16, i32 = jnp.float32, jnp.bfloat16, jnp.int32
highest = lax.Precision.HIGHEST
NN = (((1,), (0,)), ((), ()))
NT = (((1,), (1,)), ((), ()))
TN = (((0,), (0,)), ((), ()))


def iota(shape, dim):
    return lax.broadcasted_iota(i32, shape, dim)


def dot(a, b, dims=NN, precision=None):
    return lax.dot_general(a, b, dims, precision=precision, preferred_element_type=f32)


def split(a, pieces):
    out = []
    for _ in range(pieces - 1):
        top = a.astype(bf16)
        out.append(top)
        a = a - top.astype(f32)
    return (*out, a.astype(bf16))


def stacked(a):
    return jnp.concatenate(split(a, 2), axis=0)


def folded(top_bottom):
    rows = top_bottom.shape[0] // 2
    return top_bottom[:rows] + top_bottom[rows:]


def product3(left, right):
    hi, lo = split(right, 2)
    return folded(dot(left, hi)) + dot(left[: left.shape[0] // 2], lo)


def owned(place, c, columns):
    return (place >= c * columns) & (place < (c + 1) * columns)


def onehot_rows(pcol, start, width):
    lanes = pcol.shape[1]
    return jnp.concatenate(
        [
            jnp.where(pcol[:, : min(lanes, width - s)] == start + s + iota((1, min(lanes, width - s)), 1), 1.0, 0.0)
            for s in range(0, width, lanes)
        ],
        axis=1,
    )


def whole(shape):
    return pl.BlockSpec(shape, lambda *_: (0,) * len(shape))


def scalars(*values):
    return jnp.stack([jnp.asarray(v, i32) for v in values])


def prepare_kernel(columns, at_ref, prow_ref, sk_ref, partner_ref, pcol_ref, s_ref):
    n = prow_ref.shape[1]
    c, r = at_ref[0], at_ref[2]
    prow = prow_ref[...]
    across = jnp.broadcast_to(prow.astype(f32), (n, n))
    down = across.T.astype(i32)
    pcol_ref[...] = down[:, : pcol_ref.shape[1]]
    named = jnp.where(iota((n, n), 0) == prow, 1.0, 0.0).astype(bf16)
    free = 1.0 - dot(named, jnp.ones((n, n), bf16))
    upto = jnp.where(iota((n, n), 1) <= iota((n, n), 0), 1.0, 0.0).astype(bf16)
    count = dot(upto, free.astype(bf16))
    rank = jnp.sum(jnp.where((down < prow) & (down >= n), 1.0, 0.0), axis=0, keepdims=True)
    partner = jnp.sum(jnp.where(count <= rank, 1.0, 0.0), axis=0, keepdims=True).astype(i32)
    partner = jnp.where(prow >= n, partner, -1)
    partner_ref[...] = partner
    own = owned(prow, c, columns)
    sel = jnp.where(own, prow - c * columns, jnp.where(c == 0, partner, -1))
    disp = jnp.where(own & (c == 0), partner, -1)
    pieces, rows = sk_ref.shape
    lanes, size, _ = s_ref.shape
    place = r * pieces + iota((pieces, 1), 0)
    pick = jnp.concatenate([jnp.where(place == sel, 1.0, 0.0), jnp.where(place == disp, 1.0, 0.0)], axis=1)
    hi, lo = split(sk_ref[...], 2)
    pick = pick.astype(bf16)
    line = dot(hi, pick, TN) + dot(lo, pick, TN)
    for i in range(lanes):
        low, high = min(i * size, rows), min((i + 1) * size, rows)
        if high > low:
            s_ref[i, : high - low, :] = line[low:high, :]
        if high - low < size:
            s_ref[i, high - low :, :] = jnp.zeros((size - (high - low), 2 * n), f32)


def prepare(at, prow, sketch, columns, lanes):
    n = prow.shape[1]
    size = -(-sketch.shape[1] // lanes)
    outs = (((1, n), i32), ((n, 128), i32), ((lanes, size, 2 * n), f32))
    return pl.pallas_call(
        functools.partial(prepare_kernel, columns),
        out_shape=tuple(jax.ShapeDtypeStruct(s, t) for s, t in outs),
        grid_spec=pltpu.PrefetchScalarGridSpec(
            num_scalar_prefetch=1,
            grid=(1,),
            in_specs=[whole((1, n)), whole(sketch.shape)],
            out_specs=tuple(whole(s) for s, _ in outs),
        ),
        name="prepare",
    )(at, prow, sketch)


def extract_kernel(at_ref, prow_ref, partner_ref, a_ref, m_ref, e_ref):
    columns = a_ref.shape[1]
    n = prow_ref.shape[1]
    c = at_ref[0]

    @pl.when(pl.program_id(0) == 0)
    def _():
        prow = prow_ref[...]
        sel = jnp.where(owned(prow, c, columns), prow - c * columns, jnp.where(c == 0, partner_ref[...], -1))
        for s in range(0, columns, n):
            e_ref[s : s + n, :] = jnp.where(iota((n, n), 0) == sel - s, 1.0, 0.0).astype(bf16)

    m_ref[...] = folded(dot(stacked(a_ref[...]), e_ref[...]))


def extract(at, prow, partner, a):
    rows, columns = a.shape
    n = prow.shape[1]
    tm = 128
    return pl.pallas_call(
        extract_kernel,
        out_shape=jax.ShapeDtypeStruct((rows, n), f32),
        grid_spec=pltpu.PrefetchScalarGridSpec(
            num_scalar_prefetch=1,
            grid=(rows // tm,),
            in_specs=[whole((1, n)), whole((1, n)), pl.BlockSpec((tm, columns), lambda i, *_: (i, 0))],
            out_specs=pl.BlockSpec((tm, n), lambda i, *_: (i, 0)),
            scratch_shapes=[pltpu.VMEM((columns, n), bf16)],
        ),
        name="extract",
    )(at, prow, partner, a)


def inside_kernel(columns, at_ref, prow_ref, partner_ref, a_ref, d_ref):
    n = prow_ref.shape[1]
    c = at_ref[0]
    disp = jnp.where(owned(prow_ref[...], c, columns) & (c == 0), partner_ref[...], -1)
    d_ref[...] = folded(dot(stacked(a_ref[...]), jnp.where(iota((n, n), 0) == disp, 1.0, 0.0).astype(bf16)))


def inside_of(at, prow, partner, a):
    rows, columns = a.shape
    n = prow.shape[1]
    return pl.pallas_call(
        functools.partial(inside_kernel, columns),
        out_shape=jax.ShapeDtypeStruct((rows, n), f32),
        grid_spec=pltpu.PrefetchScalarGridSpec(
            num_scalar_prefetch=1,
            grid=(1,),
            in_specs=[whole((1, n)), whole((1, n)), whole((rows, n))],
            out_specs=whole((rows, n)),
        ),
        name="inside",
    )(at, prow, partner, a)


def padded_to(rows, multiple):
    return -(-rows // multiple) * multiple


def holder_kernel(columns, prow_ref, r_ref, line_ref, o_ref):
    peers, height, n = r_ref.shape
    size = line_ref.shape[0]
    prow = prow_ref[...]
    panel = r_ref[0]
    for s in range(1, peers):
        panel = jnp.where(owned(prow, s, columns), r_ref[s], panel)
    line = line_ref[:, :n]
    for s in range(peers):
        o_ref[s, :height] = jnp.where(owned(prow, s, columns), r_ref[0], panel) if s else panel
        o_ref[s, height : height + size] = line
        o_ref[s, height + size :] = jnp.zeros((o_ref.shape[1] - height - size, n), f32)


def holder(prow, received, line, columns):
    peers, height, n = received.shape
    return pl.pallas_call(
        functools.partial(holder_kernel, columns),
        out_shape=jax.ShapeDtypeStruct((peers, padded_to(height + line.shape[0], 8), n), f32),
        name="holder",
    )(prow, received, line)


def gram_kernel(columns, at_ref, prow_ref, x_ref, m_ref, d0_ref, line_ref, p_ref, d_ref, w_ref, g_ref, o_ref, x_s):
    c = at_ref[0]
    peers = x_ref.shape[0]
    rows, n = m_ref.shape
    height = rows // peers
    size = line_ref.shape[0]
    lanes, piece, _ = o_ref.shape
    prow = prow_ref[...]
    own = owned(prow, c, columns)
    for s in range(peers):
        x_s[s * height : (s + 1) * height, :] = x_ref[s, :height]
    x = x_s[...]
    panel = jnp.where(own, m_ref[...], x)
    moved = jnp.where(c == 0, d0_ref[...], jnp.where(own, x, 0.0))
    p_ref[...] = panel
    d_ref[...] = stacked(moved)
    turned = panel.T
    total = dot(turned, panel, NN, highest)
    g_ref[...] = total
    left = stacked(turned)
    w_ref[:, :rows] = left
    w_ref[:, rows:] = stacked(product3(left, moved))
    got = [x_ref[s, height : height + size] for s in range(peers)]
    front = got[0]
    for s in range(1, peers):
        front = jnp.where(owned(prow, s, columns), got[s], front)
    back = jnp.where(c == 0, line_ref[:, n:], got[0])
    part = n // lanes
    share = columns // lanes
    for i in range(lanes):
        o_ref[i, :part] = total[i * part : (i + 1) * part]
        o_ref[i, part : part + size] = jnp.where(owned(prow, c * lanes + i, share), back, front)
        o_ref[i, part + size :] = jnp.zeros((piece - part - size, n), f32)


def gram(at, prow, x, m, d0, line, columns, lanes):
    rows, n = m.shape
    piece = padded_to(n // lanes + line.shape[0], 8)
    outs = (
        ((rows, n), f32),
        ((2 * rows, n), bf16),
        ((2 * n, rows + n), bf16),
        ((n, n), f32),
        ((lanes, piece, n), f32),
    )
    return pl.pallas_call(
        functools.partial(gram_kernel, columns),
        out_shape=tuple(jax.ShapeDtypeStruct(s, t) for s, t in outs),
        grid_spec=pltpu.PrefetchScalarGridSpec(
            num_scalar_prefetch=1,
            grid=(1,),
            in_specs=[whole(v.shape) for v in (prow, x, m, d0, line)],
            out_specs=tuple(whole(s) for s, _ in outs),
            scratch_shapes=[pltpu.VMEM((rows, n), f32)],
        ),
        name="gram",
    )(at, prow, x, m, d0, line)


def half_kernel(part, size, keep_ref, sent_ref, got_ref, o_ref, line_ref):
    chips, half, lanes = keep_ref.shape
    peers, _, n = got_ref.shape
    o_ref[:, :half, :] = keep_ref[...] + sent_ref[...]
    total = got_ref[0, :part]
    for s in range(1, peers):
        total = total + got_ref[s, :part]
    for s in range(chips):
        for t in range(n // lanes):
            o_ref[s, half + t * part : half + (t + 1) * part, :] = total[:, t * lanes : (t + 1) * lanes]

    @pl.when(pl.program_id(0) == 0)
    def _():
        for s in range(peers):
            line_ref[s * size : (s + 1) * size, :] = got_ref[s, part : part + size]


def add_halves(keep, sent, got, size):
    chips, half, lanes = keep.shape
    peers, _, n = got.shape
    part = n // peers
    tall = half + part * (n // lanes)
    step = 4
    block = pl.BlockSpec((step, half, lanes), lambda b: (b, 0, 0))
    return pl.pallas_call(
        functools.partial(half_kernel, part, size),
        out_shape=(
            jax.ShapeDtypeStruct((chips, tall, lanes), f32),
            jax.ShapeDtypeStruct((peers * size, n), f32),
        ),
        grid=(chips // step,),
        in_specs=[block, block, whole(got.shape)],
        out_specs=(pl.BlockSpec((step, tall, lanes), lambda b: (b, 0, 0)), whole((peers * size, n))),
        name="half",
    )(keep, sent, got)


def total_kernel(r_ref, share_ref, o_ref):
    chips, half, _ = o_ref.shape
    extra = r_ref.shape[1] - half
    total = r_ref[0, :half]
    for s in range(1, chips):
        total = total + r_ref[s, :half]
    share_ref[:half, :] = total
    for s in range(chips):
        o_ref[s] = total
        share_ref[half + s * extra : half + (s + 1) * extra, :] = r_ref[s, half:]


def total_of(received, half):
    chips, tall, lanes = received.shape
    return pl.pallas_call(
        total_kernel,
        out_shape=(
            jax.ShapeDtypeStruct((half + chips * (tall - half), lanes), f32),
            jax.ShapeDtypeStruct((chips, half, lanes), f32),
        ),
        name="total",
    )(received)


def product_kernel(columns, at_ref, pcol_ref, a_ref, w_ref, g_ref, keep_ref, send_ref, r_ref):
    c, k = at_ref[0], at_ref[1]
    b = pl.program_id(0)
    rows, tn = a_ref.shape
    n = pcol_ref.shape[0]
    start = c * columns + b * tn
    onehot = onehot_rows(pcol_ref[...], start, tn)
    stays = (jnp.max(onehot, axis=0, keepdims=True) == 0) & (start + iota((1, tn), 1) >= n)
    hi, lo = split(jnp.where(stays, a_ref[...], 0.0), 2)
    w = w_ref[...]
    onehot = onehot.astype(bf16)
    r = folded(dot(w, jnp.concatenate([hi, onehot], axis=0))) + dot(w[:n, :rows], lo)
    r_ref[...] = r

    @pl.when((c == 0) & (b < n // tn))
    def _():
        r_ref[...] = g_ref[...]

    half = n // 2
    lanes = keep_ref.shape[2]
    for s in range(tn // lanes):
        cut = slice(s * lanes, (s + 1) * lanes)
        keep_ref[s] = r_ref[pl.ds(k * half, half), cut]
        send_ref[s] = r_ref[pl.ds((1 - k) * half, half), cut]


def product(at, pcol, a, w, g, chips):
    rows, columns = a.shape
    n = g.shape[0]
    tn = n
    lanes = columns // chips
    shape = (chips, n // 2, lanes)
    return pl.pallas_call(
        functools.partial(product_kernel, columns),
        out_shape=(jax.ShapeDtypeStruct(shape, f32),) * 2,
        grid_spec=pltpu.PrefetchScalarGridSpec(
            num_scalar_prefetch=1,
            grid=(columns // tn,),
            in_specs=[
                whole(pcol.shape),
                pl.BlockSpec((rows, tn), lambda b, *_: (0, b)),
                whole(w.shape),
                whole((n, n)),
            ],
            out_specs=(pl.BlockSpec((tn // lanes, n // 2, lanes), lambda b, *_: (b, 0, 0)),) * 2,
            scratch_shapes=[pltpu.VMEM((n, tn), f32)],
        ),
        name="product",
    )(at, pcol, a, w, g)


def permute_kernel(columns, at_ref, pcol_ref, a_ref, p_ref, d_ref, o_ref):
    c = at_ref[0]
    b = pl.program_id(0)
    tn = a_ref.shape[1]
    n = pcol_ref.shape[0]
    onehot = onehot_rows(pcol_ref[...], c * columns + b * tn, tn)
    here = jnp.max(onehot, axis=0, keepdims=True) > 0
    o_ref[...] = jnp.where(here, folded(dot(d_ref[...], onehot.astype(bf16))), a_ref[...])

    @pl.when((c == 0) & (b < n // tn))
    def _():
        o_ref[...] = p_ref[...]


def permute(at, pcol, a, p, d):
    rows, columns = a.shape
    n = p.shape[1]
    tn = n
    return pl.pallas_call(
        functools.partial(permute_kernel, columns),
        out_shape=jax.ShapeDtypeStruct(a.shape, f32),
        grid_spec=pltpu.PrefetchScalarGridSpec(
            num_scalar_prefetch=1,
            grid=(columns // tn,),
            in_specs=[
                whole(pcol.shape),
                pl.BlockSpec((rows, tn), lambda b, *_: (0, b)),
                whole((rows, n)),
                whole(d.shape),
            ],
            out_specs=pl.BlockSpec((rows, tn), lambda b, *_: (0, b)),
        ),
        name="permute",
    )(at, pcol, a, p, d)


def unit_inverse(block):
    nb = block.shape[0]
    wide = 2 * nb
    sub = 8
    eye = jnp.where(iota((nb, nb), 0) == iota((nb, nb), 1), 1.0, 0.0)
    full = jnp.concatenate([block, eye], axis=1)
    tiles = [full[i : i + sub] for i in range(0, nb, sub)]
    at = iota((sub, wide), 0)
    for i in range(len(tiles)):
        cols = [[jnp.broadcast_to(t[:, i * sub + q : i * sub + q + 1], (sub, wide)) for t in tiles[i:]] for q in range(sub)]
        for q in range(sub):
            pivot = cols[q][0][q : q + 1]
            rest = 1.0 / pivot
            mult = [m * rest for m in cols[q]]
            mult[0] = jnp.where(at > q, mult[0], 0.0)
            for later in cols[q + 1 :]:
                row = later[0][q : q + 1]
                for u, m in enumerate(mult):
                    later[u] = later[u] - m * row
            row = tiles[i][q : q + 1]
            for u, m in enumerate(mult):
                tiles[i + u] = tiles[i + u] - m * row
    done = jnp.concatenate(tiles, axis=0)
    diagonal = jnp.sum(jnp.where(iota((nb, wide), 0) == iota((nb, wide), 1), done, 0.0), axis=1, keepdims=True)
    return done[:, nb:] * lax.rsqrt(diagonal)


def factor_kernel(at_ref, mine_ref, other_ref, p_ref, inv_ref, il_ref, b_ref, t_ref):
    k = at_ref[1]
    n = p_ref.shape[1]
    lanes = mine_ref.shape[1]
    nb = 64
    half = n // 2
    width = n // lanes
    part = 8
    for s in range(half // part):
        for t in range(width):
            low = half + (s * width + t) * part
            cols = slice(t * lanes, (t + 1) * lanes)
            t_ref[pl.ds((2 * s + k) * part, part), cols] = mine_ref[low : low + part, :]
            t_ref[pl.ds((2 * s + 1 - k) * part, part), cols] = other_ref[low : low + part, :]
    t_ref[:, n:] = jnp.where(iota((n, n), 0) == iota((n, n), 1), 1.0, 0.0)
    for s in range(0, n, nb):
        inv = unit_inverse(t_ref[s : s + nb, s : s + nb])
        y = dot(inv, t_ref[s : s + nb, :], NN, highest)
        inv_ref[s : s + nb, :] = y[:, n:]
        if s + nb < n:
            t_ref[s + nb :, :] = t_ref[s + nb :, :] - dot(y[:, s + nb : n], y, TN, highest)
    inverse = inv_ref[...]
    il_ref[...] = stacked(inverse)
    b_ref[...] = stacked(dot(p_ref[...], inverse, NT, highest))


def factor(at, mine, other, p):
    rows, n = p.shape
    outs = (((n, n), f32), ((2 * n, n), bf16), ((2 * rows, n), bf16))
    return pl.pallas_call(
        factor_kernel,
        out_shape=tuple(jax.ShapeDtypeStruct(s, t) for s, t in outs),
        grid_spec=pltpu.PrefetchScalarGridSpec(
            num_scalar_prefetch=1,
            grid=(1,),
            in_specs=[whole(v.shape) for v in (mine, other, p)],
            out_specs=tuple(whole(s) for s, _ in outs),
            scratch_shapes=[pltpu.VMEM((n, 2 * n), f32)],
        ),
        name="factor",
    )(at, mine, other, p)


def share_kernel(columns, at_ref, prow_ref, mine_ref, other_ref, inv_ref, slots_ref, sk_ref, u_ref, o_ref, s_ref, t_ref):
    c, k, r = at_ref[0], at_ref[1], at_ref[2]
    n = inv_ref.shape[0]
    half = n // 2
    pieces, rows = sk_ref.shape
    s_ref[pl.ds(k * half, half), :] = mine_ref[:half]
    s_ref[pl.ds((1 - k) * half, half), :] = other_ref[:half]
    t_ref[...] = s_ref[...].T
    inverse = inv_ref[...]
    upper = dot(t_ref[pl.ds(k * pieces, pieces), :], inverse, NT, highest)
    u_ref[...] = upper
    solved = dot(upper, inverse, NN, highest)
    start = c * columns + r * pieces
    prow = prow_ref[...]
    place = start + iota((pieces, 1), 0)
    hit = jnp.where(place == prow, 1.0, 0.0)
    stays = (jnp.max(hit, axis=1, keepdims=True) == 0) & (place >= n)
    lead = jnp.where(place == iota((1, n), 1), 1.0, 0.0)
    old = sk_ref[...]
    slots = slots_ref[:rows]
    own = (prow >= start) & (prow < start + pieces)
    fronts = jnp.where(own, dot(old, hit, TN, highest), slots)
    back = dot(jnp.where(place >= n, hit, 0.0), slots, NT, highest)
    o_ref[...] = jnp.where(stays, old, 0.0) + back + dot(lead - solved, fronts, NT, highest)


def finish_share(at, prow, mine, other, inverse, slots, sketch, columns):
    n = inverse.shape[0]
    outs = ((sketch.shape[0], n), sketch.shape)
    return pl.pallas_call(
        functools.partial(share_kernel, columns),
        out_shape=tuple(jax.ShapeDtypeStruct(s, f32) for s in outs),
        grid_spec=pltpu.PrefetchScalarGridSpec(
            num_scalar_prefetch=1,
            grid=(1,),
            in_specs=[whole(v.shape) for v in (prow, mine, other, inverse, slots, sketch)],
            out_specs=tuple(whole(s) for s in outs),
            scratch_shapes=[pltpu.VMEM((n, mine.shape[1]), f32), pltpu.VMEM((mine.shape[1], n), f32)],
        ),
        name="share",
    )(at, prow, mine, other, inverse, slots, sketch)


def trailing_kernel(at_ref, a_ref, b_ref, inv_ref, mine_ref, other_ref, o_ref, s_ref):
    k = at_ref[1]
    parts, half, lanes = mine_ref.shape
    for s in range(parts):
        cut = slice(s * lanes, (s + 1) * lanes)
        s_ref[pl.ds(k * half, half), cut] = mine_ref[s]
        s_ref[pl.ds((1 - k) * half, half), cut] = other_ref[s]
    upper = product3(inv_ref[...], s_ref[...])
    o_ref[...] = a_ref[...] - product3(b_ref[...], upper)


def trail(at, a, b, inverse, mine, other):
    rows, columns = a.shape
    _, half, lanes = mine.shape
    n = 2 * half
    tn = n
    share = pl.BlockSpec((tn // lanes, half, lanes), lambda b, *_: (b, 0, 0))
    return pl.pallas_call(
        trailing_kernel,
        out_shape=jax.ShapeDtypeStruct(a.shape, f32),
        grid_spec=pltpu.PrefetchScalarGridSpec(
            num_scalar_prefetch=1,
            grid=(columns // tn,),
            in_specs=[pl.BlockSpec((rows, tn), lambda b, *_: (0, b)), whole(b.shape), whole(inverse.shape), share, share],
            out_specs=pl.BlockSpec((rows, tn), lambda b, *_: (0, b)),
            scratch_shapes=[pltpu.VMEM((n, tn), f32)],
        ),
        name="trailing",
    )(at, a, b, inverse, mine, other)


def exchange(pieces, axis):
    return lax.all_to_all(pieces, axis, split_axis=0, concat_axis=0, tiled=True)


def per_device(matrix, pivots, sketch):
    c = lax.axis_index("col")
    r = lax.axis_index(ROW)
    k = lax.axis_index("row_2")
    cols, lanes, chips = lax.axis_size("col"), lax.axis_size(ROW), lax.axis_size(CHIPS)
    rows, columns = matrix.shape
    n = pivots.shape[0]
    prow = pivots.reshape(1, n)
    at = scalars(c, k, r)
    swap = [(0, 1), (1, 0)]

    turned = sketch.T
    partner, pcol, part = prepare(at, prow, turned, columns, lanes)
    gathered = exchange(part, ROW)
    mine = extract(at, prow, partner, matrix)
    arrived = exchange(mine.reshape(cols, rows // cols, n), "col")
    line = gathered.sum(axis=0)
    inside = inside_of(at, prow, partner, matrix)
    message = holder(prow, arrived, line, columns)
    x = exchange(message, "col")
    panel, displaced, w, gram_part, message = gram(at, prow, x, mine, inside, line, columns, lanes)
    gram_pieces = exchange(message, ROW)
    keep, send = product(at, pcol, matrix, w, gram_part, chips)
    sent = lax.ppermute(send, "row_2", swap)
    half, slots = add_halves(keep, sent, gram_pieces, line.shape[0])
    summands = exchange(half, CHIPS)
    permuted = permute(at, pcol, matrix, panel, displaced)
    share, message = total_of(summands, n // 2)
    own_all = exchange(message, CHIPS)
    share_other = lax.ppermute(share, "row_2", swap)
    inverse, stack, basis = factor(at, share, share_other, panel)
    upper_share, new_sketch = finish_share(at, prow, share, share_other, inverse, slots, turned, columns)
    other_all = lax.ppermute(own_all, "row_2", swap)
    trailing = trail(at, permuted, basis, stack, own_all, other_all)
    return (upper_share.T, trailing, new_sketch.T)


def solution(mesh):
    finer = Mesh(mesh.devices.reshape(4, 4, 2, mesh.shape["col"]), ("row_0", "row_1", "row_2", "col"))
    return jax.shard_map(
        per_device,
        mesh=finer,
        in_specs=(P(ROW, "col"), P(), P(None, COL_ROW)),
        out_specs=(P(None, COL_ROW), P(ROW, "col"), P(None, COL_ROW)),
        check_vma=False,
    )
```

time: 271 us -> 217 us (0.80)
  waiting for transfers between devices: 96.4 us -> 51 us
  blocking collectives: 20 us -> 60.2 us
  Pallas kernels: 94.7 us -> 74.7 us
  starting transfers between devices: 41.3 us -> 23 us
  matrix products: 5.15 us -> 0 us
  local copies, waits for them, and re-layouts: 7.11 us -> 4.37 us
    all_to_all x8 -> x3, waiting for transfers between devices: 96.4 us -> 50.9 us  [exchange(): return lax.all_to_all(pieces, axis, split_axis=0, concat_axis=0, tiled=True)]
    all_to_all x1 -> x3, blocking collectives: 20 us -> 60.2 us  [exchange(): return lax.all_to_all(pieces, axis, split_axis=0, concat_axis=0, tiled=True)]
    all_to_all x8 -> x3, starting transfers between devices: 40.3 us -> 20.3 us  [exchange(): return lax.all_to_all(pieces, axis, split_axis=0, concat_axis=0, tiled=True)]
    pallas_call x1, Pallas kernels: 20.8 us -> 11.7 us  [trail(): pl.pallas_call(trailing_kernel, out_shape=jax.ShapeDtypeStruct(a.shape, f...]
    pallas_call x1, Pallas kernels: 16.3 us -> 9.86 us  [product(): pl.pallas_call(functools.partial(product_kernel, columns), out_shape=(jax...]
    dot_general x6 -> x0, matrix products: 5.15 us -> none  [dot(): lax.dot_general(a, b, dims, precision=precision, preferred_element_type=f32)]
    pallas_call x1, Pallas kernels: 14.4 us -> 9.44 us  [permute(): pl.pallas_call(functools.partial(permute_kernel, columns), out_shape=jax....]
    broadcast_in_dim x4 -> x0, local copies, waits for them, and re-layouts: 3.7 us -> none  [to_all(): jnp.broadcast_to(piece[None], (lax.axis_size(axis), *piece.shape))]
  transfers between devices with their start and end apart: 10 -> 6, of which waited for: 6 -> 3; matrix products, arithmetic and copies ran while one was open for 4% -> 0% of each run, Pallas kernels for 25% -> 17%
where the time goes in v1:
time: 217 us; the launch traced here: 215 us
  Pallas kernels  74.7 us (34%)
  blocking collectives  60.2 us (28%)
  waiting for transfers between devices  51 us (24%)
  starting transfers between devices  23 us (11%)
  local copies, waits for them, and re-layouts  4.37 us (2%)
    all_to_all x3, blocking collectives, exchange(): return lax.all_to_all(pieces, axis, split_axis=0, concat_axis=0, tiled=True)  60.2 us
    all_to_all x3, waiting for transfers between devices, exchange(): return lax.all_to_all(pieces, axis, split_axis=0, concat_axis=0, tiled=True)  50.9 us
    all_to_all x3, starting transfers between devices, exchange(): return lax.all_to_all(pieces, axis, split_axis=0, concat_axis=0, tiled=True)  20.3 us
    pallas_call x1, Pallas kernels, factor(): pl.pallas_call(factor_kernel, out_shape=tuple((jax.ShapeDtypeStruct(s, t)...  13.2 us
    pallas_call x1, Pallas kernels, trail(): pl.pallas_call(trailing_kernel, out_shape=jax.ShapeDtypeStruct(a.shape, f...  11.7 us
    pallas_call x1, Pallas kernels, product(): pl.pallas_call(functools.partial(product_kernel, columns), out_shape=(jax...  9.86 us
    pallas_call x1, Pallas kernels, permute(): pl.pallas_call(functools.partial(permute_kernel, columns), out_shape=jax....  9.44 us
    pallas_call x1, Pallas kernels, extract(): pl.pallas_call(extract_kernel, out_shape=jax.ShapeDtypeStruct((rows, n),...  6.68 us
  transfers between devices with their start and end apart: 6, of which 3 were waited for; matrix products, arithmetic and copies ran while one was open for 0% of the time, Pallas kernels for 17%

profile of v1, /device:TPU:1, one launch (start us, length us, event | category | flops | bytes accessed | tf_op | source)
XLA Modules:
  0.0 215.2 jit_solution(4068530188281885730)
XLA Ops:
  0.6 0.7 pad_add_fusion.at_ref
  1.3 3.2 %prepare.1 = (s32[1,256]{1,0:T(1,128)}, s32[256,128]{1,0:T(8,128)}, f32[32,9,512]{2,1,0:T(8,128)}) custom-call(s32[3]{0:T(128)} %pad_add_fusion.at_ref, s32[1,256]{1,0:T(1,128)} %bitcast.11, f32[64,264]{1,0:T(8,128)} %bitcast.9), custom_call_target="tpu_custom_call" | custom-call | tf_op jit(solution)/shard_map/prepare/pallas_call | solution.py:114
  4.5 8.6 %all-to-all-start.1 = ((f32[32,9,512]{2,1,0:T(8,128)}), f32[32,9,512]{2,1,0:T(8,128)S(1)}, u32[]{:S(2)}, u32[]{:S(2)}) async-start(f32[32,9,512]{2,1,0:T(8,128)} %get-tuple-element.24), calls=%async_computation.1 | async-start | bytes 2097152 | tf_op jit(solution)/shard_map/all_to_all | solution.py:562
  13.1 6.7 %extract.1.m_ref = f32[640,256]{1,0:T(8,128)} custom-call(s32[3]{0:T(128)} %pad_add_fusion.at_ref, s32[1,256]{1,0:T(1,128)} %bitcast.12, s32[1,256]{1,0:T(1,128)} %get-tuple-element.23.partner_ref, f32[640,2048]{1,0:T(8,128)} %a_ref.7), custom_call_target="tpu_custom_call" | custom-call | tf_op jit(solution)/shard_map/extract/pallas_call | solution.py:146
  19.8 10.4 %all-to-all-done.1 = f32[32,9,512]{2,1,0:T(8,128)S(1)} async-done(((f32[32,9,512]{2,1,0:T(8,128)}), f32[32,9,512]{2,1,0:T(8,128)S(1)}, u32[]{:S(2)}, u32[]{:S(2)}) %all-to-all-start.1) | async-done | bytes 589856 | tf_op jit(solution)/shard_map/all_to_all | solution.py:562
  30.2 8.2 %all-to-all-start = ((f32[8,80,256]{2,1,0:T(8,128)}), f32[8,80,256]{2,1,0:T(8,128)S(1)}, u32[]{:S(2)}, u32[]{:S(2)}) async-start(f32[8,80,256]{2,1,0:T(8,128)} %bitcast.8), calls=%async_computation | async-start | bytes 1310720 | tf_op jit(solution)/shard_map/all_to_all | solution.py:562
  38.4 0.7 reduce_sum.9.line_ref
  39.0 20.1 %all-to-all-done.r_ref = f32[8,80,256]{2,1,0:T(8,128)S(1)} async-done(((f32[8,80,256]{2,1,0:T(8,128)}), f32[8,80,256]{2,1,0:T(8,128)S(1)}, u32[]{:S(2)}, u32[]{:S(2)}) %all-to-all-start) | async-done | bytes 655392 | tf_op jit(solution)/shard_map/all_to_all | solution.py:562
  59.1 0.9 copy-done.2
  60.0 2.0 holder.1
  62.0 3.5 %all-to-all-start.2 = ((f32[8,96,256]{2,1,0:T(8,128)}), f32[8,96,256]{2,1,0:T(8,128)S(1)}, u32[]{:S(2)}, u32[]{:S(2)}) async-start(f32[8,96,256]{2,1,0:T(8,128)} %holder.1), calls=%async_computation.2 | async-start | bytes 1572864 | tf_op jit(solution)/shard_map/all_to_all | solution.py:562
  65.6 3.0 %inside.1.d0_ref = f32[640,256]{1,0:T(8,128)} custom-call(s32[3]{0:T(128)} %pad_add_fusion.at_ref, s32[1,256]{1,0:T(1,128)} %bitcast.14, s32[1,256]{1,0:T(1,128)} %get-tuple-element.23.partner_ref, f32[640,2048]{1,0:T(8,128)} %a_ref.7), custom_call_target="tpu_custom_call" | custom-call | tf_op jit(solution)/shard_map/inside/pallas_call | solution.py:170
  68.6 20.5 %all-to-all-done.2.x_ref = f32[8,96,256]{2,1,0:T(8,128)S(1)} async-done(((f32[8,96,256]{2,1,0:T(8,128)}), f32[8,96,256]{2,1,0:T(8,128)S(1)}, u32[]{:S(2)}, u32[]{:S(2)}) %all-to-all-start.2) | async-done | bytes 786464 | tf_op jit(solution)/shard_map/all_to_all | solution.py:562
  89.1 0.9 copy-done.1
  89.9 4.8 %gram.1 = (f32[640,256]{1,0:T(8,128)}, bf16[1280,256]{1,0:T(8,128)(2,1)}, bf16[512,896]{1,0:T(8,128)(2,1)}, f32[256,256]{1,0:T(8,128)}, f32[32,24,256]{2,1,0:T(8,128)}) custom-call(s32[3]{0:T(128)} %pad_add_fusion.at_ref, s32[1,256]{1,0:T(1,128)} %bitcast.15, f32[8,96,256]{2,1,0:T(8,128)} %copy-done.1, f32[640,256]{1,0:T(8,128)} %extract.1.m_ref, ...), custom_call_target="tpu_custom_call" | custom-call | tf_op jit(solution)/shard_map/gram/pallas_call | solution.py:255
  94.7 9.9 %product.1 = (f32[16,128,128]{2,1,0:T(8,128)}, f32[16,128,128]{2,1,0:T(8,128)}) custom-call(s32[3]{0:T(128)} %pad_add_fusion.at_ref, s32[256,128]{1,0:T(8,128)} %get-tuple-element.22.pcol_ref, f32[640,2048]{1,0:T(8,128)} %a_ref.7, bf16[512,896]{1,0:T(8,128)(2,1)} %get-tuple-element.25.w_ref, f32[256,256]{1,0:T(8,128)} %get-tuple-element.26.g_ref), custom_call_target="tpu_custom_call" | custom-call | tf_op jit(solution)/shard_map/product/pallas_call | solution.py:362
  104.6 0.5 collective-permute-start
  105.1 18.1 %all_to_all.30.got_ref = f32[32,24,256]{2,1,0:T(8,128)} all-to-all(f32[32,24,256]{2,1,0:T(8,128)S(1)} %copy-done.5), channel_id=1, replica_groups=mesh['row_0'=4,'row_1'=4,'row_2'=2,'col'=8] {'row_0','row_1','row_2'}, dimensions={0} | all-to-all | bytes 1572864 | tf_op jit(solution)/shard_map/all_to_all | solution.py:562
  123.2 0.0 collective-permute-done.sent_ref
  123.2 1.0 copy-done.3
  124.2 4.1 %half.1 = (f32[16,144,128]{2,1,0:T(8,128)}, f32[288,256]{1,0:T(8,128)}) custom-call(f32[16,128,128]{2,1,0:T(8,128)} %get-tuple-element.27.keep_ref, f32[16,128,128]{2,1,0:T(8,128)} %copy-done.3, f32[32,24,256]{2,1,0:T(8,128)} %all_to_all.30.got_ref), custom_call_target="tpu_custom_call" | custom-call | tf_op jit(solution)/shard_map/half/pallas_call | solution.py:293
  128.2 22.5 %all_to_all.31.r_ref = f32[16,144,128]{2,1,0:T(8,128)} all-to-all(f32[16,144,128]{2,1,0:T(8,128)} %get-tuple-element.30), channel_id=1, replica_groups=mesh['row_0'=4,'row_1'=4,'row_2'=2,'col'=8] {'row_0','row_1'}, dimensions={0} | all-to-all | bytes 2359296 | tf_op jit(solution)/shard_map/all_to_all | solution.py:562
  150.8 2.4 %total.1 = (f32[384,128]{1,0:T(8,128)}, f32[16,128,128]{2,1,0:T(8,128)}) custom-call(f32[16,144,128]{2,1,0:T(8,128)} %all_to_all.31.r_ref), custom_call_target="tpu_custom_call" | custom-call | tf_op jit(solution)/shard_map/total/pallas_call | solution.py:320
  153.2 19.5 %all_to_all.32.mine_ref = f32[16,128,128]{2,1,0:T(8,128)S(1)} all-to-all(f32[16,128,128]{2,1,0:T(8,128)} %get-tuple-element.39), channel_id=1, replica_groups=mesh['row_0'=4,'row_1'=4,'row_2'=2,'col'=8] {'row_0','row_1'}, dimensions={0} | all-to-all | bytes 2097152 | tf_op jit(solution)/shard_map/all_to_all | solution.py:562
  172.7 2.2 %collective-permute-start.2 = (f32[16,128,128]{2,1,0:T(8,128)S(1)}, f32[16,128,128]{2,1,0:T(8,128)S(1)}, u32[]{:S(2)}, u32[]{:S(2)}) collective-permute-start(f32[16,128,128]{2,1,0:T(8,128)S(1)} %all_to_all.32.mine_ref), channel_id=1, source_target_pairs={{0,8},{8,0},{1,9},{9,1},{2,10},{10,2},{3,11},{11,3},{4,12},{12,4},... | collective-permute-start | bytes 3145736 | tf_op jit(solution)/shard_map/ppermute | solution.py:597
  174.9 0.0 collective-permute-start.1
  174.9 9.4 %permute.1.a_ref = f32[640,2048]{1,0:T(8,128)} custom-call(s32[3]{0:T(128)} %pad_add_fusion.at_ref, s32[256,128]{1,0:T(8,128)} %get-tuple-element.22.pcol_ref, f32[640,2048]{1,0:T(8,128)} %a_ref.7, f32[640,256]{1,0:T(8,128)} %get-tuple-element.32.p_ref, bf16[1280,256]{1,0:T(8,128)(2,1)} %get-tuple-element.36.d_ref), custom_call_target="tpu_custom_call" | custom-call | tf_op jit(solution)/shard_map/permute/pallas_call | solution.py:399
  184.4 0.7 copy-done.6
  185.1 13.2 %factor.1 = (f32[256,256]{1,0:T(8,128)}, bf16[512,256]{1,0:T(8,128)(2,1)}, bf16[1280,256]{1,0:T(8,128)(2,1)}) custom-call(s32[3]{0:T(128)} %pad_add_fusion.at_ref, f32[384,128]{1,0:T(8,128)} %get-tuple-element.31.mine_ref, f32[384,128]{1,0:T(8,128)} %copy-done.6, f32[640,256]{1,0:T(8,128)} %get-tuple-element.32.p_ref), custom_call_target="tpu_custom_call" | custom-call | tf_op jit(solution)/shard_map/factor/pallas_call | solution.py:473
  198.3 4.2 %share.1 = (f32[64,256]{1,0:T(8,128)}, f32[64,264]{1,0:T(8,128)}) custom-call(s32[3]{0:T(128)} %pad_add_fusion.at_ref, s32[1,256]{1,0:T(1,128)} %bitcast.16, f32[384,128]{1,0:T(8,128)} %get-tuple-element.31.mine_ref, f32[384,128]{1,0:T(8,128)} %copy-done.6, f32[256,256]{1,0:T(8,128)} %get-tuple-element.33.inv_ref, f32[288,256]{1,0:T(8,128)} %get-tuple-element.34.slots_ref, ...), custom_call_target="tpu_custom_call" | custom-call | tf_op jit(solution)/shard_map/share/pallas_call | solution.py:516
  202.5 1.0 copy-done.4
  203.5 11.7 %trailing.1 = f32[640,2048]{1,0:T(8,128)} custom-call(s32[3]{0:T(128)} %pad_add_fusion.at_ref, f32[640,2048]{1,0:T(8,128)} %permute.1.a_ref, bf16[1280,256]{1,0:T(8,128)(2,1)} %get-tuple-element.37.b_ref, bf16[512,256]{1,0:T(8,128)(2,1)} %get-tuple-element.38.inv_ref, f32[16,128,128]{2,1,0:T(8,128)} %copy-done, f32[16,128,128]{2,1,0:T(8,128)} %copy-done.4), custom_call_target="tpu_custom_call" | custom-call | tf_op jit(solution)/shard_map/trailing/pallas_call | solution.py:547
  (11 shorter events, 0.0 us)
Async XLA Ops:
  4.5 25.6 %all-to-all-start.1 = ((f32[32,9,512]{2,1,0:T(8,128)}), f32[32,9,512]{2,1,0:T(8,128)S(1)}, u32[]{:S(2)}, u32[]{:S(2)}) async-start(f32[32,9,512]{2,1,0:T(8,128)} %get-tuple-element.24), calls=%async_computation.1 | async-start | bytes 2097152 | tf_op jit(solution)/shard_map/all_to_all | solution.py:562
  30.2 28.9 %all-to-all-start = ((f32[8,80,256]{2,1,0:T(8,128)}), f32[8,80,256]{2,1,0:T(8,128)S(1)}, u32[]{:S(2)}, u32[]{:S(2)}) async-start(f32[8,80,256]{2,1,0:T(8,128)} %bitcast.8), calls=%async_computation | async-start | bytes 1310720 | tf_op jit(solution)/shard_map/all_to_all | solution.py:562
  59.1 0.9 copy-start.2
  62.0 27.0 %all-to-all-start.2 = ((f32[8,96,256]{2,1,0:T(8,128)}), f32[8,96,256]{2,1,0:T(8,128)S(1)}, u32[]{:S(2)}, u32[]{:S(2)}) async-start(f32[8,96,256]{2,1,0:T(8,128)} %holder.1), calls=%async_computation.2 | async-start | bytes 1572864 | tf_op jit(solution)/shard_map/all_to_all | solution.py:562
  89.1 0.9 copy-start.1
  94.7 10.3 %copy-start.5 = (f32[32,24,256]{2,1,0:T(8,128)S(1)}, f32[32,24,256]{2,1,0:T(8,128)}, u32[]{:S(2)}) copy-start(f32[32,24,256]{2,1,0:T(8,128)} %get-tuple-element.29) | copy-start | bytes 2359300
  104.6 18.6 %collective-permute-start = (f32[16,128,128]{2,1,0:T(8,128)}, f32[16,128,128]{2,1,0:T(8,128)S(1)}, u32[]{:S(2)}, u32[]{:S(2)}) collective-permute-start(f32[16,128,128]{2,1,0:T(8,128)} %get-tuple-element.28), channel_id=1, source_target_pairs={{0,8},{8,0},{1,9},{9,1},{2,10},{10,2},{3,11},{11,3},{4,12},{12,4},... | collective-permute-start | bytes 3145736 | tf_op jit(solution)/shard_map/ppermute | solution.py:588
  123.2 1.0 copy-start.3
  172.7 11.6 %copy-start = (f32[16,128,128]{2,1,0:T(8,128)}, f32[16,128,128]{2,1,0:T(8,128)S(1)}, u32[]{:S(2)}) copy-start(f32[16,128,128]{2,1,0:T(8,128)S(1)} %all_to_all.32.mine_ref) | copy-start | bytes 3145732
  172.7 29.8 %collective-permute-start.2 = (f32[16,128,128]{2,1,0:T(8,128)S(1)}, f32[16,128,128]{2,1,0:T(8,128)S(1)}, u32[]{:S(2)}, u32[]{:S(2)}) collective-permute-start(f32[16,128,128]{2,1,0:T(8,128)S(1)} %all_to_all.32.mine_ref), channel_id=1, source_target_pairs={{0,8},{8,0},{1,9},{9,1},{2,10},{10,2},{3,11},{11,3},{4,12},{12,4},... | collective-permute-start | bytes 3145736 | tf_op jit(solution)/shard_map/ppermute | solution.py:597
  174.9 9.5 %collective-permute-start.1 = (f32[384,128]{1,0:T(8,128)}, f32[384,128]{1,0:T(8,128)S(1)}, u32[]{:S(2)}, u32[]{:S(2)}) collective-permute-start(f32[384,128]{1,0:T(8,128)} %get-tuple-element.31.mine_ref), channel_id=1, source_target_pairs={{0,8},{8,0},{1,9},{9,1},{2,10},{10,2},{3,11},{11,3},{4,12},{12,4},... | collective-permute-start | bytes 589832 | tf_op jit(solution)/shard_map/ppermute | solution.py:594
  184.4 0.7 copy-start.6
  202.5 1.0 copy-start.4

commit v2 on v1

v2 whole, which is shorter than its diff:
```python
import functools

import jax
import jax.numpy as jnp
from jax import lax
from jax.experimental import pallas as pl
from jax.experimental.pallas import tpu as pltpu
from jax.sharding import Mesh
from jax.sharding import PartitionSpec as P


ROW = ("row_0", "row_1", "row_2")
CHIPS = ("row_0", "row_1")
COL_ROW = ("col", "row_0", "row_1", "row_2")

f32, bf16, i32 = jnp.float32, jnp.bfloat16, jnp.int32
highest = lax.Precision.HIGHEST
NN = (((1,), (0,)), ((), ()))
NT = (((1,), (1,)), ((), ()))
TN = (((0,), (0,)), ((), ()))


def iota(shape, dim):
    return lax.broadcasted_iota(i32, shape, dim)


def dot(a, b, dims=NN, precision=None):
    return lax.dot_general(a, b, dims, precision=precision, preferred_element_type=f32)


def split(a, pieces):
    out = []
    for _ in range(pieces - 1):
        top = a.astype(bf16)
        out.append(top)
        a = a - top.astype(f32)
    return (*out, a.astype(bf16))


def stacked(a):
    return jnp.concatenate(split(a, 2), axis=0)


def folded(top_bottom):
    rows = top_bottom.shape[0] // 2
    return top_bottom[:rows] + top_bottom[rows:]


def product3(left, right):
    hi, lo = split(right, 2)
    return folded(dot(left, hi)) + dot(left[: left.shape[0] // 2], lo)


def abreast(a):
    return jnp.concatenate(split(a, 2), axis=1)


def twice(a):
    return jnp.concatenate([a, a], axis=0)


def owned(place, c, columns):
    return (place >= c * columns) & (place < (c + 1) * columns)


def onehot_rows(pcol, start, width):
    lanes = pcol.shape[1]
    return jnp.concatenate(
        [
            jnp.where(pcol[:, : min(lanes, width - s)] == start + s + iota((1, min(lanes, width - s)), 1), 1.0, 0.0)
            for s in range(0, width, lanes)
        ],
        axis=1,
    )


def in_vmem(value):
    return pltpu.with_memory_space_constraint(value, pltpu.VMEM)


def held():
    return pl.BlockSpec(memory_space=pltpu.VMEM)


def whole(shape):
    return pl.BlockSpec(shape, lambda *_: (0,) * len(shape))


def scalars(*values):
    return jnp.stack([jnp.asarray(v, i32) for v in values])


def columns_of(ref, buffer, sems, step):
    width = buffer.shape[2]
    cut = pl.ds(pl.multiple_of(step * width, width), width)
    return pltpu.make_async_copy(ref.at[:, cut], buffer.at[step], sems.at[step])


def columns_to(buffer, ref, sems, step):
    width = buffer.shape[2]
    cut = pl.ds(pl.multiple_of(step * width, width), width)
    return pltpu.make_async_copy(buffer.at[step], ref.at[:, cut], sems.at[step])


def each(count, body):
    def step(i, carry):
        body(i)
        return carry

    lax.fori_loop(0, count, step, 0)


def streams(shape, width):
    rows, columns = shape
    blocks = columns // width
    return [pltpu.VMEM((blocks, rows, width), f32), pltpu.SemaphoreType.DMA((blocks,))]


HBM = pl.BlockSpec(memory_space=pltpu.HBM)


def extract_kernel(at_ref, prow_ref, a_ref, m_ref, partner_ref, pcol_ref, a_buf, a_sem):
    n = prow_ref.shape[1]
    columns = a_ref.shape[1]
    blocks = a_buf.shape[0]
    c = at_ref[0]
    each(blocks, lambda b: columns_of(a_ref, a_buf, a_sem, b).start())
    prow = prow_ref[...]
    across = jnp.broadcast_to(prow.astype(f32), (n, n))
    down = across.T.astype(i32)
    pcol_ref[...] = down[:, : pcol_ref.shape[1]]
    named = jnp.where(iota((n, n), 0) == prow, 1.0, 0.0).astype(bf16)
    free = 1.0 - dot(named, jnp.ones((n, n), bf16))
    upto = jnp.where(iota((n, n), 1) <= iota((n, n), 0), 1.0, 0.0).astype(bf16)
    count = dot(upto, free.astype(bf16))
    rank = jnp.sum(jnp.where((down < prow) & (down >= n), 1.0, 0.0), axis=0, keepdims=True)
    partner = jnp.sum(jnp.where(count <= rank, 1.0, 0.0), axis=0, keepdims=True).astype(i32)
    partner = jnp.where(prow >= n, partner, -1)
    partner_ref[...] = partner
    sel = jnp.where(owned(prow, c, columns), prow - c * columns, jnp.where(c == 0, partner, -1))
    m_ref[...] = jnp.zeros(m_ref.shape, f32)

    def block(b):
        columns_of(a_ref, a_buf, a_sem, b).wait()
        onehot = jnp.where(iota((n, n), 0) == sel - b * n, 1.0, 0.0).astype(bf16)
        m_ref[...] += dot(abreast(a_buf[b]), twice(onehot))

    each(blocks, block)


def extract(at, prow, a):
    rows, _ = a.shape
    n = prow.shape[1]
    outs = (((rows, n), f32), ((1, n), i32), ((n, 128), i32))
    return pl.pallas_call(
        extract_kernel,
        out_shape=tuple(jax.ShapeDtypeStruct(s, t) for s, t in outs),
        grid_spec=pltpu.PrefetchScalarGridSpec(
            num_scalar_prefetch=1,
            grid=(1,),
            in_specs=[whole((1, n)), HBM],
            out_specs=tuple(whole(s) for s, _ in outs),
            scratch_shapes=streams(a.shape, n),
        ),
        name="extract",
    )(at, prow, a)


def pick_kernel(columns, at_ref, prow_ref, partner_ref, sk_ref, s_ref, i_ref):
    n = prow_ref.shape[1]
    c, r = at_ref[0], at_ref[2]
    prow = prow_ref[...]
    own = owned(prow, c, columns)
    partner = partner_ref[...]
    sel = jnp.where(own, prow - c * columns, jnp.where(c == 0, partner, -1))
    disp = jnp.where(own & (c == 0), partner, -1)
    pieces, rows = sk_ref.shape
    lanes, tall, _ = s_ref.shape
    size = -(-rows // lanes)
    place = r * pieces + iota((pieces, 1), 0)
    pick = jnp.concatenate([jnp.where(place == sel, 1.0, 0.0), jnp.where(place == disp, 1.0, 0.0)], axis=1)
    hi, lo = split(sk_ref[...], 2)
    pick = pick.astype(bf16)
    line = dot(hi, pick, TN) + dot(lo, pick, TN)
    for i in range(lanes):
        low, high = min(i * size, rows), min((i + 1) * size, rows)
        for ref, cols in ((s_ref, slice(0, n)), (i_ref, slice(n, 2 * n))):
            if high > low:
                ref[i, : high - low, :] = line[low:high, cols]
            ref[i, high - low :, :] = jnp.zeros((tall - (high - low), n), f32)


def pick_sketch(at, prow, partner, sketch, columns, lanes):
    n = prow.shape[1]
    size = padded_to(-(-sketch.shape[1] // lanes), 8)
    return pl.pallas_call(
        functools.partial(pick_kernel, columns),
        out_shape=(jax.ShapeDtypeStruct((lanes, size, n), f32),) * 2,
        grid_spec=pltpu.PrefetchScalarGridSpec(
            num_scalar_prefetch=1,
            grid=(1,),
            in_specs=[whole((1, n)), whole((1, n)), whole(sketch.shape)],
            out_specs=(whole((lanes, size, n)),) * 2,
        ),
        name="pick",
    )(at, prow, partner, sketch)


def inside_kernel(columns, at_ref, prow_ref, partner_ref, a_ref, d_ref):
    n = prow_ref.shape[1]
    c = at_ref[0]
    disp = jnp.where(owned(prow_ref[...], c, columns) & (c == 0), partner_ref[...], -1)
    d_ref[...] = folded(dot(stacked(a_ref[...]), jnp.where(iota((n, n), 0) == disp, 1.0, 0.0).astype(bf16)))


def inside_of(at, prow, partner, a):
    rows, columns = a.shape
    n = prow.shape[1]
    return pl.pallas_call(
        functools.partial(inside_kernel, columns),
        out_shape=jax.ShapeDtypeStruct((rows, n), f32),
        grid_spec=pltpu.PrefetchScalarGridSpec(
            num_scalar_prefetch=1,
            grid=(1,),
            in_specs=[whole((1, n)), whole((1, n)), whole((rows, n))],
            out_specs=whole((rows, n)),
        ),
        name="inside",
    )(at, prow, partner, a)


def padded_to(rows, multiple):
    return -(-rows // multiple) * multiple


def holder_kernel(columns, prow_ref, r_ref, line_ref, o_ref):
    peers, height, _ = r_ref.shape
    prow = prow_ref[...]
    panel = r_ref[0]
    for s in range(1, peers):
        panel = jnp.where(owned(prow, s, columns), r_ref[s], panel)
    for s in range(peers):
        o_ref[s, :height] = jnp.where(owned(prow, s, columns), r_ref[0], panel) if s else panel
        o_ref[s, height:] = line_ref[...]


def holder(prow, received, line, columns):
    peers, height, n = received.shape
    return pl.pallas_call(
        functools.partial(holder_kernel, columns),
        out_shape=jax.ShapeDtypeStruct((peers, height + line.shape[0], n), f32),
        in_specs=[held()] * 3,
        name="holder",
    )(prow, in_vmem(received), line)


def gram_kernel(columns, at_ref, prow_ref, x_ref, m_ref, d0_ref, line_ref, p_ref, d_ref, w_ref, g_ref, o_ref, x_s):
    c = at_ref[0]
    peers = x_ref.shape[0]
    rows, n = m_ref.shape
    height = rows // peers
    size = line_ref.shape[0]
    lanes = o_ref.shape[0]
    prow = prow_ref[...]
    own = owned(prow, c, columns)
    for s in range(peers):
        x_s[s * height : (s + 1) * height, :] = x_ref[s, :height]
    x = x_s[...]
    panel = jnp.where(own, m_ref[...], x)
    moved = jnp.where(c == 0, d0_ref[...], jnp.where(own, x, 0.0))
    p_ref[...] = panel
    d_ref[...] = abreast(moved)
    turned = panel.T
    total = dot(turned, panel, NN, highest)
    g_ref[...] = total
    left = stacked(turned)
    w_ref[:, :rows] = left
    w_ref[:, rows:] = stacked(product3(left, moved))
    got = [x_ref[s, height : height + size] for s in range(peers)]
    front = got[0]
    for s in range(1, peers):
        front = jnp.where(owned(prow, s, columns), got[s], front)
    back = jnp.where(c == 0, line_ref[...], got[0])
    part = n // lanes
    share = columns // lanes
    for i in range(lanes):
        o_ref[i, :part] = total[i * part : (i + 1) * part]
        o_ref[i, part:] = jnp.where(owned(prow, c * lanes + i, share), back, front)


def gram(at, prow, x, m, d0, line, columns, lanes):
    rows, n = m.shape
    piece = n // lanes + line.shape[0]
    outs = (
        ((rows, n), f32),
        ((rows, 2 * n), bf16),
        ((2 * n, rows + n), bf16),
        ((n, n), f32),
        ((lanes, piece, n), f32),
    )
    return pl.pallas_call(
        functools.partial(gram_kernel, columns),
        out_shape=tuple(jax.ShapeDtypeStruct(s, t) for s, t in outs),
        grid_spec=pltpu.PrefetchScalarGridSpec(
            num_scalar_prefetch=1,
            grid=(1,),
            in_specs=[held()] * 5,
            out_specs=tuple(whole(s) for s, _ in outs),
            scratch_shapes=[pltpu.VMEM((rows, n), f32)],
        ),
        name="gram",
    )(at, prow, in_vmem(x), m, d0, line)


def half_kernel(part, size, keep_ref, sent_ref, got_ref, o_ref, line_ref):
    chips, half, lanes = keep_ref.shape
    peers, _, n = got_ref.shape
    o_ref[:, :half, :] = keep_ref[...] + sent_ref[...]
    total = got_ref[0, :part]
    for s in range(1, peers):
        total = total + got_ref[s, :part]
    for s in range(chips):
        for t in range(n // lanes):
            o_ref[s, half + t * part : half + (t + 1) * part, :] = total[:, t * lanes : (t + 1) * lanes]

    for s in range(peers):
        line_ref[s * size : (s + 1) * size, :] = got_ref[s, part : part + size]


def add_halves(keep, sent, got, size):
    chips, half, lanes = keep.shape
    peers, _, n = got.shape
    part = n // peers
    tall = half + part * (n // lanes)
    return pl.pallas_call(
        functools.partial(half_kernel, part, size),
        out_shape=(
            jax.ShapeDtypeStruct((chips, tall, lanes), f32),
            jax.ShapeDtypeStruct((peers * size, n), f32),
        ),
        in_specs=[held()] * 3,
        name="half",
    )(keep, in_vmem(sent), in_vmem(got))


def total_kernel(r_ref, share_ref, o_ref):
    chips, half, _ = o_ref.shape
    extra = r_ref.shape[1] - half
    total = r_ref[0, :half]
    for s in range(1, chips):
        total = total + r_ref[s, :half]
    share_ref[:half, :] = total
    for s in range(chips):
        o_ref[s] = total
        share_ref[half + s * extra : half + (s + 1) * extra, :] = r_ref[s, half:]


def total_of(received, half):
    chips, tall, lanes = received.shape
    return pl.pallas_call(
        total_kernel,
        out_shape=(
            jax.ShapeDtypeStruct((half + chips * (tall - half), lanes), f32),
            jax.ShapeDtypeStruct((chips, half, lanes), f32),
        ),
        in_specs=[held()],
        name="total",
    )(in_vmem(received))


def product_kernel(at_ref, pcol_ref, a_ref, w_ref, g_ref, keep_ref, send_ref, r_ref, a_buf, a_sem, k_buf, k_sem, s_buf, s_sem):
    c, k = at_ref[0], at_ref[1]
    rows, columns = a_ref.shape
    blocks, _, tn = a_buf.shape
    n = pcol_ref.shape[0]
    half = n // 2
    lanes = keep_ref.shape[2]
    parts = tn // lanes
    each(blocks, lambda b: columns_of(a_ref, a_buf, a_sem, b).start())

    def out(buffer, ref, sems, b):
        return pltpu.make_async_copy(buffer.at[b], ref.at[pl.ds(b * parts, parts)], sems.at[b])

    def block(b):
        columns_of(a_ref, a_buf, a_sem, b).wait()
        start = c * columns + b * tn
        onehot = onehot_rows(pcol_ref[...], start, tn)
        stays = (jnp.max(onehot, axis=0, keepdims=True) == 0) & (start + iota((1, tn), 1) >= n)
        hi, lo = split(jnp.where(stays, a_buf[b], 0.0), 2)
        w = w_ref[...]
        onehot = onehot.astype(bf16)
        r_ref[...] = folded(dot(w, jnp.concatenate([hi, onehot], axis=0))) + dot(w[:n, :rows], lo)

        @pl.when((c == 0) & (b < n // tn))
        def _():
            r_ref[...] = g_ref[...]

        for s in range(parts):
            cut = slice(s * lanes, (s + 1) * lanes)
            k_buf[b, s] = r_ref[pl.ds(k * half, half), cut]
            s_buf[b, s] = r_ref[pl.ds((1 - k) * half, half), cut]
        out(k_buf, keep_ref, k_sem, b).start()
        out(s_buf, send_ref, s_sem, b).start()

    each(blocks, block)

    def finish(b):
        out(k_buf, keep_ref, k_sem, b).wait()
        out(s_buf, send_ref, s_sem, b).wait()

    each(blocks, finish)


def product(at, pcol, a, w, g, chips):
    _, columns = a.shape
    n = g.shape[0]
    lanes = columns // chips
    blocks = columns // n
    shape = (chips, n // 2, lanes)
    made = [pltpu.VMEM((blocks, chips // blocks, n // 2, lanes), f32), pltpu.SemaphoreType.DMA((blocks,))]
    return pl.pallas_call(
        product_kernel,
        out_shape=(jax.ShapeDtypeStruct(shape, f32),) * 2,
        grid_spec=pltpu.PrefetchScalarGridSpec(
            num_scalar_prefetch=1,
            grid=(1,),
            in_specs=[whole(pcol.shape), HBM, whole(w.shape), whole((n, n))],
            out_specs=(HBM,) * 2,
            scratch_shapes=[pltpu.VMEM((n, n), f32), *streams(a.shape, n), *made, *made],
        ),
        name="product",
    )(at, pcol, a, w, g)


def permute_kernel(at_ref, pcol_ref, a_ref, p_ref, d_ref, o_ref, a_buf, a_sem, o_buf, o_sem):
    c = at_ref[0]
    columns = a_ref.shape[1]
    blocks, _, tn = a_buf.shape
    n = pcol_ref.shape[0]
    each(blocks, lambda b: columns_of(a_ref, a_buf, a_sem, b).start())

    def block(b):
        columns_of(a_ref, a_buf, a_sem, b).wait()
        onehot = onehot_rows(pcol_ref[...], c * columns + b * tn, tn)
        here = jnp.max(onehot, axis=0, keepdims=True) > 0
        o_buf[b] = jnp.where(here, dot(d_ref[...], twice(onehot.astype(bf16))), a_buf[b])

        @pl.when((c == 0) & (b < n // tn))
        def _():
            o_buf[b] = p_ref[...]

        columns_to(o_buf, o_ref, o_sem, b).start()

    each(blocks, block)
    each(blocks, lambda b: columns_to(o_buf, o_ref, o_sem, b).wait())


def permute(at, pcol, a, p, d):
    rows, _ = a.shape
    n = p.shape[1]
    return pl.pallas_call(
        permute_kernel,
        out_shape=jax.ShapeDtypeStruct(a.shape, f32),
        grid_spec=pltpu.PrefetchScalarGridSpec(
            num_scalar_prefetch=1,
            grid=(1,),
            in_specs=[whole(pcol.shape), HBM, whole((rows, n)), whole(d.shape)],
            out_specs=HBM,
            scratch_shapes=[*streams(a.shape, n), *streams(a.shape, n)],
        ),
        name="permute",
    )(at, pcol, a, p, d)


def unit_inverse(block):
    nb = block.shape[0]
    wide = 2 * nb
    sub = 8
    eye = jnp.where(iota((nb, nb), 0) == iota((nb, nb), 1), 1.0, 0.0)
    full = jnp.concatenate([block, eye], axis=1)
    tiles = [full[i : i + sub] for i in range(0, nb, sub)]
    at = iota((sub, wide), 0)
    for i in range(len(tiles)):
        cols = [[jnp.broadcast_to(t[:, i * sub + q : i * sub + q + 1], (sub, wide)) for t in tiles[i:]] for q in range(sub)]
        for q in range(sub):
            pivot = cols[q][0][q : q + 1]
            rest = 1.0 / pivot
            mult = [m * rest for m in cols[q]]
            mult[0] = jnp.where(at > q, mult[0], 0.0)
            for later in cols[q + 1 :]:
                row = later[0][q : q + 1]
                for u, m in enumerate(mult):
                    later[u] = later[u] - m * row
            row = tiles[i][q : q + 1]
            for u, m in enumerate(mult):
                tiles[i + u] = tiles[i + u] - m * row
    done = jnp.concatenate(tiles, axis=0)
    diagonal = jnp.sum(jnp.where(iota((nb, wide), 0) == iota((nb, wide), 1), done, 0.0), axis=1, keepdims=True)
    return done[:, nb:] * lax.rsqrt(diagonal)


def factor_kernel(at_ref, mine_ref, other_ref, p_ref, inv_ref, b_ref, t_ref):
    k = at_ref[1]
    n = p_ref.shape[1]
    lanes = mine_ref.shape[1]
    nb = 64
    half = n // 2
    width = n // lanes
    part = 8
    for s in range(half // part):
        for t in range(width):
            low = half + (s * width + t) * part
            cols = slice(t * lanes, (t + 1) * lanes)
            t_ref[pl.ds((2 * s + k) * part, part), cols] = mine_ref[low : low + part, :]
            t_ref[pl.ds((2 * s + 1 - k) * part, part), cols] = other_ref[low : low + part, :]
    t_ref[:, n:] = jnp.where(iota((n, n), 0) == iota((n, n), 1), 1.0, 0.0)
    for s in range(0, n, nb):
        inv = unit_inverse(t_ref[s : s + nb, s : s + nb])
        y = dot(inv, t_ref[s : s + nb, :], NN, highest)
        inv_ref[s : s + nb, :] = y[:, n:]
        if s + nb < n:
            t_ref[s + nb :, :] = t_ref[s + nb :, :] - dot(y[:, s + nb : n], y, TN, highest)
    inverse = inv_ref[...]
    hi, lo = split(dot(p_ref[...], dot(inverse, inverse, TN, highest), NN, highest), 2)
    for s, part in enumerate((hi, hi, lo)):
        b_ref[:, s * n : (s + 1) * n] = part


def factor(at, mine, other, p):
    rows, n = p.shape
    outs = (((n, n), f32), ((rows, 3 * n), bf16))
    return pl.pallas_call(
        factor_kernel,
        out_shape=tuple(jax.ShapeDtypeStruct(s, t) for s, t in outs),
        grid_spec=pltpu.PrefetchScalarGridSpec(
            num_scalar_prefetch=1,
            grid=(1,),
            in_specs=[held()] * 3,
            out_specs=tuple(whole(s) for s, _ in outs),
            scratch_shapes=[pltpu.VMEM((n, 2 * n), f32)],
        ),
        name="factor",
    )(at, mine, in_vmem(other), p)


def sketch_kernel(columns, at_ref, prow_ref, slots_ref, sk_ref, f_ref, o_ref):
    n = prow_ref.shape[1]
    pieces, rows = sk_ref.shape
    start = at_ref[0] * columns + at_ref[2] * pieces
    prow = prow_ref[...]
    place = start + iota((pieces, 1), 0)
    hit = jnp.where(place == prow, 1.0, 0.0)
    stays = (jnp.max(hit, axis=1, keepdims=True) == 0) & (place >= n)
    old = sk_ref[...]
    slots = slots_ref[:rows]
    own = (prow >= start) & (prow < start + pieces)
    f_ref[...] = jnp.where(own, dot(old, hit, TN, highest), slots)
    o_ref[...] = jnp.where(stays, old, 0.0) + dot(jnp.where(place >= n, hit, 0.0), slots, NT, highest)


def swap_sketch(at, prow, slots, sketch, columns):
    n = prow.shape[1]
    outs = ((sketch.shape[1], n), sketch.shape)
    return pl.pallas_call(
        functools.partial(sketch_kernel, columns),
        out_shape=tuple(jax.ShapeDtypeStruct(s, f32) for s in outs),
        grid_spec=pltpu.PrefetchScalarGridSpec(
            num_scalar_prefetch=1,
            grid=(1,),
            in_specs=[whole(v.shape) for v in (prow, slots, sketch)],
            out_specs=tuple(whole(s) for s in outs),
        ),
        name="sketch",
    )(at, prow, slots, sketch)


def share_kernel(columns, at_ref, mine_ref, other_ref, inv_ref, fronts_ref, sk_ref, u_ref, o_ref, s_ref, t_ref):
    c, k, r = at_ref[0], at_ref[1], at_ref[2]
    n = inv_ref.shape[0]
    half = n // 2
    pieces, _ = sk_ref.shape
    s_ref[pl.ds(k * half, half), :] = mine_ref[:half]
    s_ref[pl.ds((1 - k) * half, half), :] = other_ref[:half]
    t_ref[...] = s_ref[...].T
    inverse = inv_ref[...]
    upper = dot(t_ref[pl.ds(k * pieces, pieces), :], inverse, NT, highest)
    u_ref[...] = upper
    solved = dot(upper, inverse, NN, highest)
    place = c * columns + r * pieces + iota((pieces, 1), 0)
    lead = jnp.where(place == iota((1, n), 1), 1.0, 0.0)
    o_ref[...] = sk_ref[...] + dot(lead - solved, fronts_ref[...], NT, highest)


def finish_share(at, mine, other, inverse, fronts, sketch, columns):
    n = inverse.shape[0]
    outs = ((sketch.shape[0], n), sketch.shape)
    return pl.pallas_call(
        functools.partial(share_kernel, columns),
        out_shape=tuple(jax.ShapeDtypeStruct(s, f32) for s in outs),
        grid_spec=pltpu.PrefetchScalarGridSpec(
            num_scalar_prefetch=1,
            grid=(1,),
            in_specs=[held()] * 5,
            out_specs=tuple(whole(s) for s in outs),
            scratch_shapes=[pltpu.VMEM((n, mine.shape[1]), f32), pltpu.VMEM((mine.shape[1], n), f32)],
        ),
        name="share",
    )(at, mine, in_vmem(other), inverse, in_vmem(fronts), in_vmem(sketch))


def trailing_kernel(at_ref, a_ref, b_ref, mine_ref, other_ref, o_ref, s_ref, a_buf, a_sem, o_buf, o_sem):
    k = at_ref[1]
    _, half, lanes = mine_ref.shape
    blocks, _, tn = a_buf.shape
    parts = tn // lanes
    each(blocks, lambda b: columns_of(a_ref, a_buf, a_sem, b).start())

    def block(b):
        for s in range(parts):
            cut = slice(s * lanes, (s + 1) * lanes)
            s_ref[pl.ds(k * half, half), cut] = mine_ref[b * parts + s]
            s_ref[pl.ds((1 - k) * half, half), cut] = other_ref[b * parts + s]
        hi, lo = split(s_ref[...], 2)
        columns_of(a_ref, a_buf, a_sem, b).wait()
        o_buf[b] = a_buf[b] - dot(b_ref[...], jnp.concatenate([hi, lo, hi], axis=0))
        columns_to(o_buf, o_ref, o_sem, b).start()

    each(blocks, block)
    each(blocks, lambda b: columns_to(o_buf, o_ref, o_sem, b).wait())


def trail(at, a, b, mine, other):
    n = 2 * mine.shape[1]
    return pl.pallas_call(
        trailing_kernel,
        out_shape=jax.ShapeDtypeStruct(a.shape, f32),
        grid_spec=pltpu.PrefetchScalarGridSpec(
            num_scalar_prefetch=1,
            grid=(1,),
            in_specs=[HBM, whole(b.shape), held(), held()],
            out_specs=HBM,
            scratch_shapes=[pltpu.VMEM((n, n), f32), *streams(a.shape, n), *streams(a.shape, n)],
        ),
        name="trailing",
    )(at, a, b, in_vmem(mine), in_vmem(other))


def exchange(pieces, axis):
    return lax.all_to_all(pieces, axis, split_axis=0, concat_axis=0, tiled=True)


def side_of(value, which, dim):
    return lax.dynamic_index_in_dim(value, which, dim, keepdims=False)


def halved(value, which, axis, swap, dim):
    size = value.shape[dim] // 2
    value = value.reshape(*value.shape[:dim], 2, size, *value.shape[dim + 1 :])
    return side_of(value, which, dim) + lax.ppermute(side_of(value, 1 - which, dim), axis, swap)


def sum_at_rows(value):
    y, x, k = (lax.axis_index(a) for a in ROW)
    value = value.reshape(4, 4, 2, *value.shape[1:])
    near, far = [(0, 1), (1, 0), (2, 3), (3, 2)], [(0, 3), (3, 0), (1, 2), (2, 1)]
    value = halved(value, k, "row_2", [(0, 1), (1, 0)], 2)[:, :, 0]
    value = halved(value, x >> 1, "row_1", far, 1)
    value = halved(value, x & 1, "row_1", near, 1)[:, 0]
    value = halved(value, y >> 1, "row_0", far, 0)
    return halved(value, y & 1, "row_0", near, 0)[0]


def per_device(matrix, pivots, sketch):
    c = lax.axis_index("col")
    r = lax.axis_index(ROW)
    k = lax.axis_index("row_2")
    cols, lanes, chips = lax.axis_size("col"), lax.axis_size(ROW), lax.axis_size(CHIPS)
    rows, columns = matrix.shape
    n = pivots.shape[0]
    prow = pivots.reshape(1, n)
    at = scalars(c, k, r)
    swap = [(0, 1), (1, 0)]

    turned = sketch.T
    mine, partner, pcol = extract(at, prow, matrix)
    arrived = exchange(mine.reshape(cols, rows // cols, n), "col")
    picks, insides = pick_sketch(at, prow, partner, turned, columns, lanes)
    line = sum_at_rows(picks)
    inside_line = sum_at_rows(insides)
    inside = inside_of(at, prow, partner, matrix)
    message = holder(prow, arrived, line, columns)
    x = exchange(message, "col")
    panel, displaced, w, gram_part, message = gram(at, prow, x, mine, inside, inside_line, columns, lanes)
    gram_pieces = exchange(message, ROW)
    keep, send = product(at, pcol, matrix, w, gram_part, chips)
    sent = lax.ppermute(send, "row_2", swap)
    half, slots = add_halves(keep, sent, gram_pieces, -(-sketch.shape[0] // lanes))
    summands = exchange(half, CHIPS)
    permuted = permute(at, pcol, matrix, panel, displaced)
    fronts, swapped = swap_sketch(at, prow, slots, turned, columns)
    share, message = total_of(summands, n // 2)
    own_all = exchange(message, CHIPS)
    share_other = lax.ppermute(share, "row_2", swap)
    inverse, basis = factor(at, share, share_other, panel)
    upper_share, new_sketch = finish_share(at, share, share_other, inverse, fronts, swapped, columns)
    other_all = lax.ppermute(own_all, "row_2", swap)
    trailing = trail(at, permuted, basis, own_all, other_all)
    return (upper_share.T, trailing, new_sketch.T)


def solution(mesh):
    finer = Mesh(mesh.devices.reshape(4, 4, 2, mesh.shape["col"]), ("row_0", "row_1", "row_2", "col"))
    return jax.shard_map(
        per_device,
        mesh=finer,
        in_specs=(P(ROW, "col"), P(), P(None, COL_ROW)),
        out_specs=(P(None, COL_ROW), P(ROW, "col"), P(None, COL_ROW)),
        check_vma=False,
    )
```

time: 217 us -> 194 us (0.89)
  waiting for transfers between devices: 51 us -> 31.4 us
  Pallas kernels: 74.7 us -> 66.1 us
  starting transfers between devices: 23 us -> 26.2 us
  other arithmetic: 1.34 us -> 3.86 us
    all_to_all x3 -> x2, waiting for transfers between devices: 50.9 us -> 21.5 us  [exchange(): return lax.all_to_all(pieces, axis, split_axis=0, concat_axis=0, tiled=True)]
    ppermute x0 -> x10, starting transfers between devices: none -> 11.7 us  [halved(): lax.ppermute(side_of(value, 1 - which, dim), axis, swap)]
    ppermute x0 -> x10, waiting for transfers between devices: none -> 9.96 us  [halved(): lax.ppermute(side_of(value, 1 - which, dim), axis, swap)]
    all_to_all x3 -> x2, starting transfers between devices: 20.3 us -> 11.8 us  [exchange(): return lax.all_to_all(pieces, axis, split_axis=0, concat_axis=0, tiled=True)]
    pallas_call x1, Pallas kernels: 11.7 us -> 7.74 us  [trail(): pl.pallas_call(trailing_kernel, out_shape=jax.ShapeDtypeStruct(a.shape, f...]
    unnamed x14 -> x6, local copies, waits for them, and re-layouts: 4.37 us -> 1.85 us
    pallas_call x4 -> x5, Pallas kernels: 29.2 us -> 27.9 us  [the longest x1 8.96 us: product(): pl.pallas_call(product_kernel, out_shape=(jax.ShapeDtypeStruct(shape, f32...]
  transfers between devices with their start and end apart: 6 -> 15, of which waited for: 3 -> 8; matrix products, arithmetic and copies ran while one was open for 0% -> 2% of each run, Pallas kernels for 17% -> 17%
where the time goes in v2:
time: 194 us; the launch traced here: 193 us
  Pallas kernels  66.1 us (34%)
  blocking collectives  60.3 us (31%)
  waiting for transfers between devices  31.4 us (16%)
  starting transfers between devices  26.2 us (14%)
  local copies, waits for them, and re-layouts  3.89 us (2%)
  other arithmetic  3.86 us (2%)
    all_to_all x3, blocking collectives, exchange(): return lax.all_to_all(pieces, axis, split_axis=0, concat_axis=0, tiled=True)  60.3 us
    all_to_all x2, waiting for transfers between devices, exchange(): return lax.all_to_all(pieces, axis, split_axis=0, concat_axis=0, tiled=True)  21.5 us
    pallas_call x1, Pallas kernels, factor(): pl.pallas_call(factor_kernel, out_shape=tuple((jax.ShapeDtypeStruct(s, t)...  13.8 us
    all_to_all x2, starting transfers between devices, exchange(): return lax.all_to_all(pieces, axis, split_axis=0, concat_axis=0, tiled=True)  11.8 us
    ppermute x10, starting transfers between devices, halved(): lax.ppermute(side_of(value, 1 - which, dim), axis, swap)  11.7 us
    ppermute x10, waiting for transfers between devices, halved(): lax.ppermute(side_of(value, 1 - which, dim), axis, swap)  9.96 us
    pallas_call x1, Pallas kernels, product(): pl.pallas_call(product_kernel, out_shape=(jax.ShapeDtypeStruct(shape, f32...  8.96 us
    pallas_call x1, Pallas kernels, trail(): pl.pallas_call(trailing_kernel, out_shape=jax.ShapeDtypeStruct(a.shape, f...  7.74 us
  transfers between devices with their start and end apart: 15, of which 8 were waited for; matrix products, arithmetic and copies ran while one was open for 2% of the time, Pallas kernels for 17%

profile of v2, /device:TPU:1, one launch (start us, length us, event | category | flops | bytes accessed | tf_op | source)
XLA Modules:
  0.0 192.7 jit_solution(8520499211579056607)
XLA Ops:
  1.2 6.1 %extract.1 = (f32[640,256]{1,0:T(8,128)}, s32[1,256]{1,0:T(1,128)}, s32[256,128]{1,0:T(8,128)}) custom-call(s32[3]{0:T(128)} %pad_add_fusion.at_ref, s32[1,256]{1,0:T(1,128)} %bitcast.57, f32[640,2048]{1,0:T(8,128)} %a_ref.7), custom_call_target="tpu_custom_call" | custom-call | tf_op jit(solution)/shard_map/extract/pallas_call | solution.py:155
  7.3 2.9 %pick.1 = (f32[32,16,256]{2,1,0:T(8,128)}, f32[32,16,256]{2,1,0:T(8,128)}) custom-call(s32[3]{0:T(128)} %pad_add_fusion.at_ref, s32[1,256]{1,0:T(1,128)} %bitcast.58, s32[1,256]{1,0:T(1,128)} %get-tuple-element.27.partner_ref, f32[64,264]{1,0:T(8,128)} %bitcast.51), custom_call_target="tpu_custom_call" | custom-call | tf_op jit(solution)/shard_map/pick/pallas_call | solution.py:196
  11.2 3.3 %collective-permute-start = (f32[4,4,1,16,256]{4,3,1,0,2:T(8,128)S(1)}, f32[4,4,1,16,256]{4,3,1,0,2:T(8,128)S(1)}, u32[]{:S(2)}, u32[]{:S(2)}) collective-permute-start(f32[4,4,1,16,256]{4,3,1,0,2:T(8,128)S(1)} %dynamic-slice_bitcast_fusion.1), channel_id=1, source_target_pairs={{0,8},{8,0},{1,9},{9,1},{2,10},{10,2},{3,11},{11,3},{4,12},{12,4},... | collective-permute-start | bytes 786440 | tf_op jit(solution)/shard_map/ppermute | solution.py:659
  14.5 1.2 collective-permute-done
  15.7 1.0 bitcast_add_fusion.1
  17.6 8.2 %all-to-all-start = ((f32[8,80,256]{2,1,0:T(8,128)}), f32[8,80,256]{2,1,0:T(8,128)S(1)}, u32[]{:S(2)}, u32[]{:S(2)}) async-start(f32[8,80,256]{2,1,0:T(8,128)} %bitcast.42), calls=%async_computation | async-start | bytes 1310720 | tf_op jit(solution)/shard_map/all_to_all | solution.py:649
  25.9 1.0 dynamic-slice_bitcast_fusion
  26.9 1.2 collective-permute-start.5
  29.1 2.8 %collective-permute-start.3 = (f32[2,16,256]{2,1,0:T(8,128)S(1)}, f32[2,16,256]{2,1,0:T(8,128)S(1)}, u32[]{:S(2)}, u32[]{:S(2)}) collective-permute-start(f32[2,16,256]{2,1,0:T(8,128)S(1)} %dynamic-slice_bitcast_fusion.5), channel_id=1, source_target_pairs={{0,192},{192,0},{64,128},{128,64},{1,193},{193,1},{65,129},{129,65... | collective-permute-start | bytes 98312 | tf_op jit(solution)/shard_map/ppermute | solution.py:659
  31.9 1.0 bitcast_add_fusion
  33.9 2.6 %collective-permute-done.4 = f32[1,16,256]{2,1,0:T(8,128)S(1)} collective-permute-done((f32[1,16,256]{2,1,0:T(8,128)S(1)}, f32[1,16,256]{2,1,0:T(8,128)S(1)}, u32[]{:S(2)}, u32[]{:S(2)}) %collective-permute-start.4) | collective-permute-done | bytes 16416 | tf_op jit(solution)/shard_map/ppermute | solution.py:659
  37.1 9.4 %all-to-all-done.r_ref = f32[8,80,256]{2,1,0:T(8,128)S(1)} async-done(((f32[8,80,256]{2,1,0:T(8,128)}), f32[8,80,256]{2,1,0:T(8,128)S(1)}, u32[]{:S(2)}, u32[]{:S(2)}) %all-to-all-start) | async-done | bytes 655392 | tf_op jit(solution)/shard_map/all_to_all | solution.py:649
  46.5 1.7 holder.1
  48.2 3.5 %all-to-all-start.1 = ((f32[8,96,256]{2,1,0:T(8,128)}), f32[8,96,256]{2,1,0:T(8,128)S(1)}, u32[]{:S(2)}, u32[]{:S(2)}) async-start(f32[8,96,256]{2,1,0:T(8,128)} %holder.1), calls=%async_computation.1 | async-start | bytes 1572864 | tf_op jit(solution)/shard_map/all_to_all | solution.py:649
  51.9 3.1 %collective-permute-done.7 = f32[4,1,16,256]{3,2,1,0:T(8,128)S(1)} collective-permute-done((f32[4,1,16,256]{3,2,1,0:T(8,128)S(1)}, f32[4,1,16,256]{3,2,1,0:T(8,128)S(1)}, u32[]{:S(2)}, u32[]{:S(2)}) %collective-permute-start.7) | collective-permute-done | bytes 65568 | tf_op jit(solution)/shard_map/ppermute | solution.py:659
  55.1 2.8 %collective-permute-start.8 = (f32[2,16,256]{2,1,0:T(8,128)S(1)}, f32[2,16,256]{2,1,0:T(8,128)S(1)}, u32[]{:S(2)}, u32[]{:S(2)}) collective-permute-start(f32[2,16,256]{2,1,0:T(8,128)S(1)} %dynamic-slice_bitcast_fusion.4), channel_id=1, source_target_pairs={{0,192},{192,0},{64,128},{128,64},{1,193},{193,1},{65,129},{129,65... | collective-permute-start | bytes 98312 | tf_op jit(solution)/shard_map/ppermute | solution.py:659
  57.9 1.6 collective-permute-done.8
  59.6 3.0 %inside.1.d0_ref = f32[640,256]{1,0:T(8,128)} custom-call(s32[3]{0:T(128)} %pad_add_fusion.at_ref, s32[1,256]{1,0:T(1,128)} %bitcast.60, s32[1,256]{1,0:T(1,128)} %get-tuple-element.27.partner_ref, f32[640,2048]{1,0:T(8,128)} %a_ref.7), custom_call_target="tpu_custom_call" | custom-call | tf_op jit(solution)/shard_map/inside/pallas_call | solution.py:219
  63.2 12.0 %all-to-all-done.1.x_ref = f32[8,96,256]{2,1,0:T(8,128)S(1)} async-done(((f32[8,96,256]{2,1,0:T(8,128)}), f32[8,96,256]{2,1,0:T(8,128)S(1)}, u32[]{:S(2)}, u32[]{:S(2)}) %all-to-all-start.1) | async-done | bytes 786464 | tf_op jit(solution)/shard_map/all_to_all | solution.py:649
  75.3 4.5 %gram.1 = (f32[640,256]{1,0:T(8,128)}, bf16[640,512]{1,0:T(8,128)(2,1)}, bf16[512,896]{1,0:T(8,128)(2,1)}, f32[256,256]{1,0:T(8,128)}, f32[32,24,256]{2,1,0:T(8,128)}) custom-call(s32[3]{0:T(128)} %pad_add_fusion.at_ref, s32[1,256]{1,0:T(1,128)} %bitcast.61, f32[8,96,256]{2,1,0:T(8,128)S(1)} %all-to-all-done.1.x_ref, f32[640,256]{1,0:T(8,128)} %get-tuple-element.26.m_ref, ...), custom_call_target="tpu_custom_call" | custom-call | tf_op jit(solution)/shard_map/gram/pallas_call | solution.py:301
  79.8 9.0 %product.1 = (f32[16,128,128]{2,1,0:T(8,128)}, f32[16,128,128]{2,1,0:T(8,128)}) custom-call(s32[3]{0:T(128)} %pad_add_fusion.at_ref, s32[256,128]{1,0:T(8,128)} %get-tuple-element.25.pcol_ref, f32[640,2048]{1,0:T(8,128)} %a_ref.7, bf16[512,896]{1,0:T(8,128)(2,1)} %get-tuple-element.30.w_ref, f32[256,256]{1,0:T(8,128)} %get-tuple-element.31.g_ref), custom_call_target="tpu_custom_call" | custom-call | tf_op jit(solution)/shard_map/product/pallas_call | solution.py:421
  89.3 19.0 %all_to_all.25.got_ref = f32[32,24,256]{2,1,0:T(8,128)S(1)} all-to-all(f32[32,24,256]{2,1,0:T(8,128)S(1)} %copy-done.2), channel_id=1, replica_groups=mesh['row_0'=4,'row_1'=4,'row_2'=2,'col'=8] {'row_0','row_1','row_2'}, dimensions={0} | all-to-all | bytes 1572864 | tf_op jit(solution)/shard_map/all_to_all | solution.py:649
  108.3 2.5 %half.1 = (f32[16,144,128]{2,1,0:T(8,128)}, f32[288,256]{1,0:T(8,128)}) custom-call(f32[16,128,128]{2,1,0:T(8,128)} %get-tuple-element.32.keep_ref, f32[16,128,128]{2,1,0:T(8,128)S(1)} %collective-permute-done.10.sent_ref, f32[32,24,256]{2,1,0:T(8,128)S(1)} %all_to_all.25.got_ref), custom_call_target="tpu_custom_call" | custom-call | tf_op jit(solution)/shard_map/half/pallas_call | solution.py:335
  110.8 21.8 %all_to_all.26.r_ref = f32[16,144,128]{2,1,0:T(8,128)S(1)} all-to-all(f32[16,144,128]{2,1,0:T(8,128)} %get-tuple-element.35), channel_id=1, replica_groups=mesh['row_0'=4,'row_1'=4,'row_2'=2,'col'=8] {'row_0','row_1'}, dimensions={0} | all-to-all | bytes 2359296 | tf_op jit(solution)/shard_map/all_to_all | solution.py:649
  132.6 1.2 total.1
  133.8 19.5 %all_to_all.27.mine_ref = f32[16,128,128]{2,1,0:T(8,128)S(1)} all-to-all(f32[16,128,128]{2,1,0:T(8,128)} %get-tuple-element.45), channel_id=1, replica_groups=mesh['row_0'=4,'row_1'=4,'row_2'=2,'col'=8] {'row_0','row_1'}, dimensions={0} | all-to-all | bytes 2097152 | tf_op jit(solution)/shard_map/all_to_all | solution.py:649
  153.3 2.2 %collective-permute-start.12 = (f32[16,128,128]{2,1,0:T(8,128)S(1)}, f32[16,128,128]{2,1,0:T(8,128)S(1)}, u32[]{:S(2)}, u32[]{:S(2)}) collective-permute-start(f32[16,128,128]{2,1,0:T(8,128)S(1)} %all_to_all.27.mine_ref), channel_id=1, source_target_pairs={{0,8},{8,0},{1,9},{9,1},{2,10},{10,2},{3,11},{11,3},{4,12},{12,4},... | collective-permute-start | bytes 3145736 | tf_op jit(solution)/shard_map/ppermute | solution.py:706
  155.5 6.9 %permute.1.a_ref = f32[640,2048]{1,0:T(8,128)} custom-call(s32[3]{0:T(128)} %pad_add_fusion.at_ref, s32[256,128]{1,0:T(8,128)} %get-tuple-element.25.pcol_ref, f32[640,2048]{1,0:T(8,128)} %a_ref.7, f32[640,256]{1,0:T(8,128)} %get-tuple-element.37.p_ref, bf16[640,512]{1,0:T(8,128)(2,1)} %get-tuple-element.43.d_ref), custom_call_target="tpu_custom_call" | custom-call | tf_op jit(solution)/shard_map/permute/pallas_call | solution.py:461
  162.4 3.0 %sketch.1 = (f32[264,256]{1,0:T(8,128)}, f32[64,264]{1,0:T(8,128)}) custom-call(s32[3]{0:T(128)} %pad_add_fusion.at_ref, s32[1,256]{1,0:T(1,128)} %bitcast.62, f32[288,256]{1,0:T(8,128)} %get-tuple-element.39.slots_ref, f32[64,264]{1,0:T(8,128)} %bitcast.52), custom_call_target="tpu_custom_call" | custom-call | tf_op jit(solution)/shard_map/sketch/pallas_call | solution.py:564
  165.5 13.8 %factor.1 = (f32[256,256]{1,0:T(8,128)}, bf16[640,768]{1,0:T(8,128)(2,1)}) custom-call(s32[3]{0:T(128)} %pad_add_fusion.at_ref, f32[384,128]{1,0:T(8,128)} %get-tuple-element.36.mine_ref, f32[384,128]{1,0:T(8,128)S(1)} %collective-permute-done.11.other_ref, f32[640,256]{1,0:T(8,128)} %get-tuple-element.37.p_ref), custom_call_target="tpu_custom_call" | custom-call | tf_op jit(solution)/shard_map/factor/pallas_call | solution.py:532
  181.2 3.7 %share.1 = (f32[64,256]{1,0:T(8,128)}, f32[64,264]{1,0:T(8,128)}) custom-call(s32[3]{0:T(128)} %pad_add_fusion.at_ref, f32[384,128]{1,0:T(8,128)} %get-tuple-element.36.mine_ref, f32[384,128]{1,0:T(8,128)S(1)} %collective-permute-done.11.other_ref, f32[256,256]{1,0:T(8,128)} %get-tuple-element.38.inv_ref, f32[264,256]{1,0:T(8,128)S(1)} %copy-done, ...), custom_call_target="tpu_custom_call" | custom-call | tf_op jit(solution)/shard_map/share/pallas_call | solution.py:597
  184.8 7.7 %trailing.1 = f32[640,2048]{1,0:T(8,128)} custom-call(s32[3]{0:T(128)} %pad_add_fusion.at_ref, f32[640,2048]{1,0:T(8,128)} %permute.1.a_ref, bf16[640,768]{1,0:T(8,128)(2,1)} %get-tuple-element.44.b_ref, f32[16,128,128]{2,1,0:T(8,128)S(1)} %all_to_all.27.mine_ref, f32[16,128,128]{2,1,0:T(8,128)S(1)} %collective-permute-done.12.other_ref), custom_call_target="tpu_custom_call" | custom-call | tf_op jit(solution)/shard_map/trailing/pallas_call | solution.py:634
  (41 shorter events, 8.5 us)
Async XLA Ops:
  11.2 4.4 %collective-permute-start = (f32[4,4,1,16,256]{4,3,1,0,2:T(8,128)S(1)}, f32[4,4,1,16,256]{4,3,1,0,2:T(8,128)S(1)}, u32[]{:S(2)}, u32[]{:S(2)}) collective-permute-start(f32[4,4,1,16,256]{4,3,1,0,2:T(8,128)S(1)} %dynamic-slice_bitcast_fusion.1), channel_id=1, source_target_pairs={{0,8},{8,0},{1,9},{9,1},{2,10},{10,2},{3,11},{11,3},{4,12},{12,4},... | collective-permute-start | bytes 786440 | tf_op jit(solution)/shard_map/ppermute | solution.py:659
  16.7 9.1 %collective-permute-start.1 = (f32[4,2,16,256]{3,2,1,0:T(8,128)S(1)}, f32[4,2,16,256]{3,2,1,0:T(8,128)S(1)}, u32[]{:S(2)}, u32[]{:S(2)}) collective-permute-start(f32[4,2,16,256]{3,2,1,0:T(8,128)S(1)} %dynamic-slice_bitcast_fusion.3), channel_id=1, source_target_pairs={{0,48},{48,0},{16,32},{32,16},{1,49},{49,1},{17,33},{33,17},{2,50}... | collective-permute-start | bytes 393224 | tf_op jit(solution)/shard_map/ppermute | solution.py:659
  17.6 29.0 %all-to-all-start = ((f32[8,80,256]{2,1,0:T(8,128)}), f32[8,80,256]{2,1,0:T(8,128)S(1)}, u32[]{:S(2)}, u32[]{:S(2)}) async-start(f32[8,80,256]{2,1,0:T(8,128)} %bitcast.42), calls=%async_computation | async-start | bytes 1310720 | tf_op jit(solution)/shard_map/all_to_all | solution.py:649
  25.8 3.2 %collective-permute-start.2 = (f32[4,1,16,256]{3,2,1,0:T(8,128)S(1)}, f32[4,1,16,256]{3,2,1,0:T(8,128)S(1)}, u32[]{:S(2)}, u32[]{:S(2)}) collective-permute-start(f32[4,1,16,256]{3,2,1,0:T(8,128)S(1)} %constant_dynamic-slice_fusion.3), channel_id=1, source_target_pairs={{0,16},{16,0},{32,48},{48,32},{1,17},{17,1},{33,49},{49,33},{2,18}... | collective-permute-start | bytes 196616 | tf_op jit(solution)/shard_map/ppermute | solution.py:659
  26.9 5.0 %collective-permute-start.5 = (f32[4,4,1,16,256]{4,3,1,0,2:T(8,128)S(1)}, f32[4,4,1,16,256]{4,3,1,0,2:T(8,128)S(1)}, u32[]{:S(2)}, u32[]{:S(2)}) collective-permute-start(f32[4,4,1,16,256]{4,3,1,0,2:T(8,128)S(1)} %dynamic-slice_bitcast_fusion), channel_id=1, source_target_pairs={{0,8},{8,0},{1,9},{9,1},{2,10},{10,2},{3,11},{11,3},{4,12},{12,4},... | collective-permute-start | bytes 786440 | tf_op jit(solution)/shard_map/ppermute | solution.py:659
  29.1 4.4 %collective-permute-start.3 = (f32[2,16,256]{2,1,0:T(8,128)S(1)}, f32[2,16,256]{2,1,0:T(8,128)S(1)}, u32[]{:S(2)}, u32[]{:S(2)}) collective-permute-start(f32[2,16,256]{2,1,0:T(8,128)S(1)} %dynamic-slice_bitcast_fusion.5), channel_id=1, source_target_pairs={{0,192},{192,0},{64,128},{128,64},{1,193},{193,1},{65,129},{129,65... | collective-permute-start | bytes 98312 | tf_op jit(solution)/shard_map/ppermute | solution.py:659
  33.5 3.0 %collective-permute-start.4 = (f32[1,16,256]{2,1,0:T(8,128)S(1)}, f32[1,16,256]{2,1,0:T(8,128)S(1)}, u32[]{:S(2)}, u32[]{:S(2)}) collective-permute-start(f32[1,16,256]{2,1,0:T(8,128)S(1)} %constant_dynamic-slice_fusion.2), channel_id=1, source_target_pairs={{0,64},{64,0},{128,192},{192,128},{1,65},{65,1},{129,193},{193,129... | collective-permute-start | bytes 49160 | tf_op jit(solution)/shard_map/ppermute | solution.py:659
  33.6 18.1 %collective-permute-start.6 = (f32[4,2,16,256]{3,2,1,0:T(8,128)S(1)}, f32[4,2,16,256]{3,2,1,0:T(8,128)S(1)}, u32[]{:S(2)}, u32[]{:S(2)}) collective-permute-start(f32[4,2,16,256]{3,2,1,0:T(8,128)S(1)} %dynamic-slice_bitcast_fusion.2), channel_id=1, source_target_pairs={{0,48},{48,0},{16,32},{32,16},{1,49},{49,1},{17,33},{33,17},{2,50}... | collective-permute-start | bytes 393224 | tf_op jit(solution)/shard_map/ppermute | solution.py:659
  48.2 27.0 %all-to-all-start.1 = ((f32[8,96,256]{2,1,0:T(8,128)}), f32[8,96,256]{2,1,0:T(8,128)S(1)}, u32[]{:S(2)}, u32[]{:S(2)}) async-start(f32[8,96,256]{2,1,0:T(8,128)} %holder.1), calls=%async_computation.1 | async-start | bytes 1572864 | tf_op jit(solution)/shard_map/all_to_all | solution.py:649
  51.8 3.2 %collective-permute-start.7 = (f32[4,1,16,256]{3,2,1,0:T(8,128)S(1)}, f32[4,1,16,256]{3,2,1,0:T(8,128)S(1)}, u32[]{:S(2)}, u32[]{:S(2)}) collective-permute-start(f32[4,1,16,256]{3,2,1,0:T(8,128)S(1)} %constant_dynamic-slice_fusion.1), channel_id=1, source_target_pairs={{0,16},{16,0},{32,48},{48,32},{1,17},{17,1},{33,49},{49,33},{2,18}... | collective-permute-start | bytes 196616 | tf_op jit(solution)/shard_map/ppermute | solution.py:659
  55.1 4.4 %collective-permute-start.8 = (f32[2,16,256]{2,1,0:T(8,128)S(1)}, f32[2,16,256]{2,1,0:T(8,128)S(1)}, u32[]{:S(2)}, u32[]{:S(2)}) collective-permute-start(f32[2,16,256]{2,1,0:T(8,128)S(1)} %dynamic-slice_bitcast_fusion.4), channel_id=1, source_target_pairs={{0,192},{192,0},{64,128},{128,64},{1,193},{193,1},{65,129},{129,65... | collective-permute-start | bytes 98312 | tf_op jit(solution)/shard_map/ppermute | solution.py:659
  59.5 3.1 %collective-permute-start.9 = (f32[1,16,256]{2,1,0:T(8,128)S(1)}, f32[1,16,256]{2,1,0:T(8,128)S(1)}, u32[]{:S(2)}, u32[]{:S(2)}) collective-permute-start(f32[1,16,256]{2,1,0:T(8,128)S(1)} %constant_dynamic-slice_fusion), channel_id=1, source_target_pairs={{0,64},{64,0},{128,192},{192,128},{1,65},{65,1},{129,193},{193,129... | collective-permute-start | bytes 49160 | tf_op jit(solution)/shard_map/ppermute | solution.py:659
  79.8 9.6 %copy-start.2 = (f32[32,24,256]{2,1,0:T(8,128)S(1)}, f32[32,24,256]{2,1,0:T(8,128)}, u32[]{:S(2)}) copy-start(f32[32,24,256]{2,1,0:T(8,128)} %get-tuple-element.34) | copy-start | bytes 2359300
  88.7 19.6 %collective-permute-start.10 = (f32[16,128,128]{2,1,0:T(8,128)}, f32[16,128,128]{2,1,0:T(8,128)S(1)}, u32[]{:S(2)}, u32[]{:S(2)}) collective-permute-start(f32[16,128,128]{2,1,0:T(8,128)} %get-tuple-element.33), channel_id=1, source_target_pairs={{0,8},{8,0},{1,9},{9,1},{2,10},{10,2},{3,11},{11,3},{4,12},{12,4},... | collective-permute-start | bytes 3145736 | tf_op jit(solution)/shard_map/ppermute | solution.py:696
  153.3 31.5 %collective-permute-start.12 = (f32[16,128,128]{2,1,0:T(8,128)S(1)}, f32[16,128,128]{2,1,0:T(8,128)S(1)}, u32[]{:S(2)}, u32[]{:S(2)}) collective-permute-start(f32[16,128,128]{2,1,0:T(8,128)S(1)} %all_to_all.27.mine_ref), channel_id=1, source_target_pairs={{0,8},{8,0},{1,9},{9,1},{2,10},{10,2},{3,11},{11,3},{4,12},{12,4},... | collective-permute-start | bytes 3145736 | tf_op jit(solution)/shard_map/ppermute | solution.py:706
  155.5 10.0 %collective-permute-start.11 = (f32[384,128]{1,0:T(8,128)}, f32[384,128]{1,0:T(8,128)S(1)}, u32[]{:S(2)}, u32[]{:S(2)}) collective-permute-start(f32[384,128]{1,0:T(8,128)} %get-tuple-element.36.mine_ref), channel_id=1, source_target_pairs={{0,8},{8,0},{1,9},{9,1},{2,10},{10,2},{3,11},{11,3},{4,12},{12,4},... | collective-permute-start | bytes 589832 | tf_op jit(solution)/shard_map/ppermute | solution.py:703
  179.3 1.0 copy-start
  180.3 0.9 copy-start.1

commit v3 on v2

--- a/solution.py
+++ b/solution.py
@@ -166,44 +166,41 @@
     )(at, prow, a)
 
 
-def pick_kernel(columns, at_ref, prow_ref, partner_ref, sk_ref, s_ref, i_ref):
+def pick_kernel(columns, at_ref, prow_ref, partner_ref, sk_ref, first_ref, s_ref):
     n = prow_ref.shape[1]
     c, r = at_ref[0], at_ref[2]
     prow = prow_ref[...]
-    own = owned(prow, c, columns)
     partner = partner_ref[...]
-    sel = jnp.where(own, prow - c * columns, jnp.where(c == 0, partner, -1))
-    disp = jnp.where(own & (c == 0), partner, -1)
+    sel = jnp.where(owned(prow, c, columns), prow - c * columns, jnp.where(c == 0, partner, -1))
+    disp = jnp.where(owned(prow, 0, columns) & (c == 1), partner, -1)
     pieces, rows = sk_ref.shape
     lanes, tall, _ = s_ref.shape
-    size = -(-rows // lanes)
+    body = 8
     place = r * pieces + iota((pieces, 1), 0)
-    pick = jnp.concatenate([jnp.where(place == sel, 1.0, 0.0), jnp.where(place == disp, 1.0, 0.0)], axis=1)
-    hi, lo = split(sk_ref[...], 2)
-    pick = pick.astype(bf16)
+    pick = jnp.concatenate([jnp.where(place == sel, 1.0, 0.0), jnp.where(place == disp, 1.0, 0.0)], axis=0).astype(bf16)
+    hi, lo = split(jnp.concatenate([sk_ref[...], first_ref[...]], axis=0), 2)
     line = dot(hi, pick, TN) + dot(lo, pick, TN)
+    left = rows - lanes * body
     for i in range(lanes):
-        low, high = min(i * size, rows), min((i + 1) * size, rows)
-        for ref, cols in ((s_ref, slice(0, n)), (i_ref, slice(n, 2 * n))):
-            if high > low:
-                ref[i, : high - low, :] = line[low:high, cols]
-            ref[i, high - low :, :] = jnp.zeros((tall - (high - low), n), f32)
-
-
-def pick_sketch(at, prow, partner, sketch, columns, lanes):
+        s_ref[i, :body, :] = line[i * body : (i + 1) * body]
+        s_ref[i, body:, :] = jnp.zeros((tall - body, n), f32)
+        if i < left:
+            s_ref[i, body : body + 1, :] = line[lanes * body + i : lanes * body + i + 1]
+
+
+def pick_sketch(at, prow, partner, sketch, first, columns, lanes):
     n = prow.shape[1]
-    size = padded_to(-(-sketch.shape[1] // lanes), 8)
     return pl.pallas_call(
         functools.partial(pick_kernel, columns),
-        out_shape=(jax.ShapeDtypeStruct((lanes, size, n), f32),) * 2,
-        grid_spec=pltpu.PrefetchScalarGridSpec(
-            num_scalar_prefetch=1,
-            grid=(1,),
-            in_specs=[whole((1, n)), whole((1, n)), whole(sketch.shape)],
-            out_specs=(whole((lanes, size, n)),) * 2,
+        out_shape=jax.ShapeDtypeStruct((lanes, 16, n), f32),
+        grid_spec=pltpu.PrefetchScalarGridSpec(
+            num_scalar_prefetch=1,
+            grid=(1,),
+            in_specs=[whole((1, n)), whole((1, n)), whole(sketch.shape), whole(sketch.shape)],
+            out_specs=whole((lanes, 16, n)),
         ),
         name="pick",
-    )(at, prow, partner, sketch)
+    )(at, prow, partner, sketch, first)
 
 
 def inside_kernel(columns, at_ref, prow_ref, partner_ref, a_ref, d_ref):
@@ -227,10 +224,6 @@
         ),
         name="inside",
     )(at, prow, partner, a)
-
-
-def padded_to(rows, multiple):
-    return -(-rows // multiple) * multiple
 
 
 def holder_kernel(columns, prow_ref, r_ref, line_ref, o_ref):
@@ -254,12 +247,12 @@
     )(prow, in_vmem(received), line)
 
 
-def gram_kernel(columns, at_ref, prow_ref, x_ref, m_ref, d0_ref, line_ref, p_ref, d_ref, w_ref, g_ref, o_ref, x_s):
+def gram_kernel(columns, at_ref, prow_ref, x_ref, m_ref, d0_ref, p_ref, d_ref, w_ref, g_ref, o_ref, x_s):
     c = at_ref[0]
     peers = x_ref.shape[0]
     rows, n = m_ref.shape
     height = rows // peers
-    size = line_ref.shape[0]
+    size = x_ref.shape[1] - height
     lanes = o_ref.shape[0]
     prow = prow_ref[...]
     own = owned(prow, c, columns)
@@ -280,7 +273,7 @@
     front = got[0]
     for s in range(1, peers):
         front = jnp.where(owned(prow, s, columns), got[s], front)
-    back = jnp.where(c == 0, line_ref[...], got[0])
+    back = jnp.where(c == 0, got[1], got[0])
     part = n // lanes
     share = columns // lanes
     for i in range(lanes):
@@ -288,9 +281,9 @@
         o_ref[i, part:] = jnp.where(owned(prow, c * lanes + i, share), back, front)
 
 
-def gram(at, prow, x, m, d0, line, columns, lanes):
+def gram(at, prow, x, m, d0, columns, lanes):
     rows, n = m.shape
-    piece = n // lanes + line.shape[0]
+    piece = n // lanes + x.shape[1] - rows // x.shape[0]
     outs = (
         ((rows, n), f32),
         ((rows, 2 * n), bf16),
@@ -304,15 +297,15 @@
         grid_spec=pltpu.PrefetchScalarGridSpec(
             num_scalar_prefetch=1,
             grid=(1,),
-            in_specs=[held()] * 5,
+            in_specs=[held()] * 4,
             out_specs=tuple(whole(s) for s, _ in outs),
             scratch_shapes=[pltpu.VMEM((rows, n), f32)],
         ),
         name="gram",
-    )(at, prow, in_vmem(x), m, d0, line)
-
-
-def half_kernel(part, size, keep_ref, sent_ref, got_ref, o_ref, line_ref):
+    )(at, prow, in_vmem(x), m, d0)
+
+
+def half_kernel(part, keep_ref, sent_ref, got_ref, o_ref, line_ref):
     chips, half, lanes = keep_ref.shape
     peers, _, n = got_ref.shape
     o_ref[:, :half, :] = keep_ref[...] + sent_ref[...]
@@ -324,19 +317,21 @@
             o_ref[s, half + t * part : half + (t + 1) * part, :] = total[:, t * lanes : (t + 1) * lanes]
 
     for s in range(peers):
-        line_ref[s * size : (s + 1) * size, :] = got_ref[s, part : part + size]
-
-
-def add_halves(keep, sent, got, size):
+        line_ref[s * 8 : (s + 1) * 8, :] = got_ref[s, part : part + 8]
+    for s in range(line_ref.shape[0] - 8 * peers):
+        line_ref[8 * peers + s : 8 * peers + s + 1, :] = got_ref[s, part + 8 : part + 9]
+
+
+def add_halves(keep, sent, got, rows):
     chips, half, lanes = keep.shape
     peers, _, n = got.shape
     part = n // peers
     tall = half + part * (n // lanes)
     return pl.pallas_call(
-        functools.partial(half_kernel, part, size),
+        functools.partial(half_kernel, part),
         out_shape=(
             jax.ShapeDtypeStruct((chips, tall, lanes), f32),
-            jax.ShapeDtypeStruct((peers * size, n), f32),
+            jax.ShapeDtypeStruct((rows, n), f32),
         ),
         in_specs=[held()] * 3,
         name="half",
@@ -545,14 +540,14 @@
 
 def sketch_kernel(columns, at_ref, prow_ref, slots_ref, sk_ref, f_ref, o_ref):
     n = prow_ref.shape[1]
-    pieces, rows = sk_ref.shape
+    pieces, _ = sk_ref.shape
     start = at_ref[0] * columns + at_ref[2] * pieces
     prow = prow_ref[...]
     place = start + iota((pieces, 1), 0)
     hit = jnp.where(place == prow, 1.0, 0.0)
     stays = (jnp.max(hit, axis=1, keepdims=True) == 0) & (place >= n)
     old = sk_ref[...]
-    slots = slots_ref[:rows]
+    slots = slots_ref[...]
     own = (prow >= start) & (prow < start + pieces)
     f_ref[...] = jnp.where(own, dot(old, hit, TN, highest), slots)
     o_ref[...] = jnp.where(stays, old, 0.0) + dot(jnp.where(place >= n, hit, 0.0), slots, NT, highest)
@@ -682,19 +677,19 @@
     swap = [(0, 1), (1, 0)]
 
     turned = sketch.T
+    first = lax.ppermute(turned, "col", [(i, (i + 1) % cols) for i in range(cols)])
     mine, partner, pcol = extract(at, prow, matrix)
     arrived = exchange(mine.reshape(cols, rows // cols, n), "col")
-    picks, insides = pick_sketch(at, prow, partner, turned, columns, lanes)
+    picks = pick_sketch(at, prow, partner, turned, first, columns, lanes)
     line = sum_at_rows(picks)
-    inside_line = sum_at_rows(insides)
     inside = inside_of(at, prow, partner, matrix)
     message = holder(prow, arrived, line, columns)
     x = exchange(message, "col")
-    panel, displaced, w, gram_part, message = gram(at, prow, x, mine, inside, inside_line, columns, lanes)
+    panel, displaced, w, gram_part, message = gram(at, prow, x, mine, inside, columns, lanes)
     gram_pieces = exchange(message, ROW)
     keep, send = product(at, pcol, matrix, w, gram_part, chips)
     sent = lax.ppermute(send, "row_2", swap)
-    half, slots = add_halves(keep, sent, gram_pieces, -(-sketch.shape[0] // lanes))
+    half, slots = add_halves(keep, sent, gram_pieces, sketch.shape[0])
     summands = exchange(half, CHIPS)
     permuted = permute(at, pcol, matrix, panel, displaced)
     fronts, swapped = swap_sketch(at, prow, slots, turned, columns)

time: 194 us -> 195 us (level)
  waiting for transfers between devices: 31.4 us -> 38.7 us
  starting transfers between devices: 26.2 us -> 22.7 us
    all_to_all x2, waiting for transfers between devices: 21.5 us -> 30 us  [exchange(): return lax.all_to_all(pieces, axis, split_axis=0, concat_axis=0, tiled=True)]
    ppermute x10 -> x5, starting transfers between devices: 11.7 us -> 6.76 us  [halved(): lax.ppermute(side_of(value, 1 - which, dim), axis, swap)]
    ppermute x0 -> x1, starting transfers between devices: none -> 2.53 us  [per_device(): lax.ppermute(turned, 'col', [(i, (i + 1) % cols) for i in range(cols)])]
    ppermute x10 -> x5, waiting for transfers between devices: 9.96 us -> 8.72 us  [halved(): lax.ppermute(side_of(value, 1 - which, dim), axis, swap)]
  transfers between devices with their start and end apart: 15 -> 11, of which waited for: 8 -> 6; matrix products, arithmetic and copies ran while one was open for 2% -> 1% of each run, Pallas kernels for 17% -> 19%
where the time goes in v3:
time: 195 us; the launch traced here: 194 us
  Pallas kernels  65.8 us (34%)
  blocking collectives  60.3 us (31%)
  waiting for transfers between devices  38.7 us (20%)
  starting transfers between devices  22.7 us (12%)
  local copies, waits for them, and re-layouts  3.5 us (2%)
  other arithmetic  2.24 us (1%)
    all_to_all x3, blocking collectives, exchange(): return lax.all_to_all(pieces, axis, split_axis=0, concat_axis=0, tiled=True)  60.3 us
    all_to_all x2, waiting for transfers between devices, exchange(): return lax.all_to_all(pieces, axis, split_axis=0, concat_axis=0, tiled=True)  30 us
    pallas_call x1, Pallas kernels, factor(): pl.pallas_call(factor_kernel, out_shape=tuple((jax.ShapeDtypeStruct(s, t)...  13.9 us
    all_to_all x2, starting transfers between devices, exchange(): return lax.all_to_all(pieces, axis, split_axis=0, concat_axis=0, tiled=True)  10.7 us
    pallas_call x1, Pallas kernels, product(): pl.pallas_call(product_kernel, out_shape=(jax.ShapeDtypeStruct(shape, f32...  8.96 us
    ppermute x5, waiting for transfers between devices, halved(): lax.ppermute(side_of(value, 1 - which, dim), axis, swap)  8.72 us
    pallas_call x1, Pallas kernels, trail(): pl.pallas_call(trailing_kernel, out_shape=jax.ShapeDtypeStruct(a.shape, f...  7.74 us
    pallas_call x1, Pallas kernels, permute(): pl.pallas_call(permute_kernel, out_shape=jax.ShapeDtypeStruct(a.shape, f3...  6.89 us
  transfers between devices with their start and end apart: 11, of which 6 were waited for; matrix products, arithmetic and copies ran while one was open for 1% of the time, Pallas kernels for 19%

profile of v3, /device:TPU:1, one launch (start us, length us, event | category | flops | bytes accessed | tf_op | source)
XLA Modules:
  0.0 194.3 jit_solution(2983878386492093640)
XLA Ops:
  0.6 2.5 %collective-permute-start = (f32[64,264]{1,0:T(8,128)}, f32[64,264]{1,0:T(8,128)S(1)}, u32[]{:S(2)}, u32[]{:S(2)}) collective-permute-start(f32[64,264]{1,0:T(8,128)} %bitcast.30), channel_id=1, source_target_pairs={{0,1},{1,2},{2,3},{3,4},{4,5},{5,6},{6,7},{7,0},{8,9},{9,10},{10,1... | collective-permute-start | bytes 202760 | tf_op jit(solution)/shard_map/ppermute | solution.py:680
  3.8 6.2 %extract.1 = (f32[640,256]{1,0:T(8,128)}, s32[1,256]{1,0:T(1,128)}, s32[256,128]{1,0:T(8,128)}) custom-call(s32[3]{0:T(128)} %pad_add_fusion.at_ref, s32[1,256]{1,0:T(1,128)} %bitcast.35, f32[640,2048]{1,0:T(8,128)} %a_ref.7), custom_call_target="tpu_custom_call" | custom-call | tf_op jit(solution)/shard_map/extract/pallas_call | solution.py:155
  10.6 2.7 %pick.1 = f32[32,16,256]{2,1,0:T(8,128)} custom-call(s32[3]{0:T(128)} %pad_add_fusion.at_ref, s32[1,256]{1,0:T(1,128)} %bitcast.36, s32[1,256]{1,0:T(1,128)} %get-tuple-element.25.partner_ref, f32[64,264]{1,0:T(8,128)} %bitcast.31, f32[64,264]{1,0:T(8,128)} %copy-done.3), custom_call_target="tpu_custom_call" | custom-call | tf_op jit(solution)/shard_map/pick/pallas_call | solution.py:193
  13.3 1.0 dynamic-slice_bitcast_fusion
  14.3 1.2 collective-permute-start.1
  15.4 1.2 collective-permute-done.1
  16.6 1.0 bitcast_add_fusion
  17.6 2.6 %collective-permute-start.2 = (f32[4,2,16,256]{3,2,1,0:T(8,128)S(1)}, f32[4,2,16,256]{3,2,1,0:T(8,128)S(1)}, u32[]{:S(2)}, u32[]{:S(2)}) collective-permute-start(f32[4,2,16,256]{3,2,1,0:T(8,128)S(1)} %dynamic-slice_bitcast_fusion.1), channel_id=1, source_target_pairs={{0,48},{48,0},{16,32},{32,16},{1,49},{49,1},{17,33},{33,17},{2,50}... | collective-permute-start | bytes 393224 | tf_op jit(solution)/shard_map/ppermute | solution.py:654
  20.2 7.1 %all-to-all-start = ((f32[8,80,256]{2,1,0:T(8,128)}), f32[8,80,256]{2,1,0:T(8,128)S(1)}, u32[]{:S(2)}, u32[]{:S(2)}) async-start(f32[8,80,256]{2,1,0:T(8,128)} %bitcast.25), calls=%async_computation | async-start | bytes 1310720 | tf_op jit(solution)/shard_map/all_to_all | solution.py:644
  27.5 3.1 %collective-permute-done.3 = f32[4,1,16,256]{3,2,1,0:T(8,128)S(1)} collective-permute-done((f32[4,1,16,256]{3,2,1,0:T(8,128)S(1)}, f32[4,1,16,256]{3,2,1,0:T(8,128)S(1)}, u32[]{:S(2)}, u32[]{:S(2)}) %collective-permute-start.3) | collective-permute-done | bytes 65568 | tf_op jit(solution)/shard_map/ppermute | solution.py:654
  30.6 2.8 %collective-permute-start.4 = (f32[2,16,256]{2,1,0:T(8,128)S(1)}, f32[2,16,256]{2,1,0:T(8,128)S(1)}, u32[]{:S(2)}, u32[]{:S(2)}) collective-permute-start(f32[2,16,256]{2,1,0:T(8,128)S(1)} %dynamic-slice_bitcast_fusion.2), channel_id=1, source_target_pairs={{0,192},{192,0},{64,128},{128,64},{1,193},{193,1},{65,129},{129,65... | collective-permute-start | bytes 98312 | tf_op jit(solution)/shard_map/ppermute | solution.py:654
  33.4 1.6 collective-permute-done.4
  35.1 2.9 %collective-permute-done.5 = f32[1,16,256]{2,1,0:T(8,128)S(1)} collective-permute-done((f32[1,16,256]{2,1,0:T(8,128)S(1)}, f32[1,16,256]{2,1,0:T(8,128)S(1)}, u32[]{:S(2)}, u32[]{:S(2)}) %collective-permute-start.5) | collective-permute-done | bytes 16416 | tf_op jit(solution)/shard_map/ppermute | solution.py:654
  38.6 9.5 %all-to-all-done.r_ref = f32[8,80,256]{2,1,0:T(8,128)S(1)} async-done(((f32[8,80,256]{2,1,0:T(8,128)}), f32[8,80,256]{2,1,0:T(8,128)S(1)}, u32[]{:S(2)}, u32[]{:S(2)}) %all-to-all-start) | async-done | bytes 655392 | tf_op jit(solution)/shard_map/all_to_all | solution.py:644
  48.1 1.7 holder.1
  49.8 3.5 %all-to-all-start.1 = ((f32[8,96,256]{2,1,0:T(8,128)}), f32[8,96,256]{2,1,0:T(8,128)S(1)}, u32[]{:S(2)}, u32[]{:S(2)}) async-start(f32[8,96,256]{2,1,0:T(8,128)} %holder.1), calls=%async_computation.1 | async-start | bytes 1572864 | tf_op jit(solution)/shard_map/all_to_all | solution.py:644
  53.3 3.0 %inside.1.d0_ref = f32[640,256]{1,0:T(8,128)} custom-call(s32[3]{0:T(128)} %pad_add_fusion.at_ref, s32[1,256]{1,0:T(1,128)} %bitcast.38, s32[1,256]{1,0:T(1,128)} %get-tuple-element.25.partner_ref, f32[640,2048]{1,0:T(8,128)} %a_ref.7), custom_call_target="tpu_custom_call" | custom-call | tf_op jit(solution)/shard_map/inside/pallas_call | solution.py:216
  56.3 20.5 %all-to-all-done.1.x_ref = f32[8,96,256]{2,1,0:T(8,128)S(1)} async-done(((f32[8,96,256]{2,1,0:T(8,128)}), f32[8,96,256]{2,1,0:T(8,128)S(1)}, u32[]{:S(2)}, u32[]{:S(2)}) %all-to-all-start.1) | async-done | bytes 786464 | tf_op jit(solution)/shard_map/all_to_all | solution.py:644
  76.8 4.5 %gram.1 = (f32[640,256]{1,0:T(8,128)}, bf16[640,512]{1,0:T(8,128)(2,1)}, bf16[512,896]{1,0:T(8,128)(2,1)}, f32[256,256]{1,0:T(8,128)}, f32[32,24,256]{2,1,0:T(8,128)}) custom-call(s32[3]{0:T(128)} %pad_add_fusion.at_ref, s32[1,256]{1,0:T(1,128)} %bitcast.39, f32[8,96,256]{2,1,0:T(8,128)S(1)} %all-to-all-done.1.x_ref, f32[640,256]{1,0:T(8,128)} %get-tuple-element.24.m_ref, ...), custom_call_target="tpu_custom_call" | custom-call | tf_op jit(solution)/shard_map/gram/pallas_call | solution.py:294
  81.4 9.0 %product.1 = (f32[16,128,128]{2,1,0:T(8,128)}, f32[16,128,128]{2,1,0:T(8,128)}) custom-call(s32[3]{0:T(128)} %pad_add_fusion.at_ref, s32[256,128]{1,0:T(8,128)} %get-tuple-element.23.pcol_ref, f32[640,2048]{1,0:T(8,128)} %a_ref.7, bf16[512,896]{1,0:T(8,128)(2,1)} %get-tuple-element.26.w_ref, f32[256,256]{1,0:T(8,128)} %get-tuple-element.27.g_ref), custom_call_target="tpu_custom_call" | custom-call | tf_op jit(solution)/shard_map/product/pallas_call | solution.py:416
  90.9 19.0 %all_to_all.25.got_ref = f32[32,24,256]{2,1,0:T(8,128)S(1)} all-to-all(f32[32,24,256]{2,1,0:T(8,128)S(1)} %copy-done.2), channel_id=1, replica_groups=mesh['row_0'=4,'row_1'=4,'row_2'=2,'col'=8] {'row_0','row_1','row_2'}, dimensions={0} | all-to-all | bytes 1572864 | tf_op jit(solution)/shard_map/all_to_all | solution.py:644
  109.9 2.5 %half.1 = (f32[16,144,128]{2,1,0:T(8,128)}, f32[264,256]{1,0:T(8,128)}) custom-call(f32[16,128,128]{2,1,0:T(8,128)} %get-tuple-element.28.keep_ref, f32[16,128,128]{2,1,0:T(8,128)S(1)} %collective-permute-done.6.sent_ref, f32[32,24,256]{2,1,0:T(8,128)S(1)} %all_to_all.25.got_ref), custom_call_target="tpu_custom_call" | custom-call | tf_op jit(solution)/shard_map/half/pallas_call | solution.py:330
  112.4 21.8 %all_to_all.26.r_ref = f32[16,144,128]{2,1,0:T(8,128)S(1)} all-to-all(f32[16,144,128]{2,1,0:T(8,128)} %get-tuple-element.31), channel_id=1, replica_groups=mesh['row_0'=4,'row_1'=4,'row_2'=2,'col'=8] {'row_0','row_1'}, dimensions={0} | all-to-all | bytes 2359296 | tf_op jit(solution)/shard_map/all_to_all | solution.py:644
  134.2 1.2 total.1
  135.3 19.5 %all_to_all.27.mine_ref = f32[16,128,128]{2,1,0:T(8,128)S(1)} all-to-all(f32[16,128,128]{2,1,0:T(8,128)} %get-tuple-element.41), channel_id=1, replica_groups=mesh['row_0'=4,'row_1'=4,'row_2'=2,'col'=8] {'row_0','row_1'}, dimensions={0} | all-to-all | bytes 2097152 | tf_op jit(solution)/shard_map/all_to_all | solution.py:644
  154.9 2.2 %collective-permute-start.8 = (f32[16,128,128]{2,1,0:T(8,128)S(1)}, f32[16,128,128]{2,1,0:T(8,128)S(1)}, u32[]{:S(2)}, u32[]{:S(2)}) collective-permute-start(f32[16,128,128]{2,1,0:T(8,128)S(1)} %all_to_all.27.mine_ref), channel_id=1, source_target_pairs={{0,8},{8,0},{1,9},{9,1},{2,10},{10,2},{3,11},{11,3},{4,12},{12,4},... | collective-permute-start | bytes 3145736 | tf_op jit(solution)/shard_map/ppermute | solution.py:701
  157.1 6.9 %permute.1.a_ref = f32[640,2048]{1,0:T(8,128)} custom-call(s32[3]{0:T(128)} %pad_add_fusion.at_ref, s32[256,128]{1,0:T(8,128)} %get-tuple-element.23.pcol_ref, f32[640,2048]{1,0:T(8,128)} %a_ref.7, f32[640,256]{1,0:T(8,128)} %get-tuple-element.33.p_ref, bf16[640,512]{1,0:T(8,128)(2,1)} %get-tuple-element.39.d_ref), custom_call_target="tpu_custom_call" | custom-call | tf_op jit(solution)/shard_map/permute/pallas_call | solution.py:456
  164.0 3.0 %sketch.1 = (f32[264,256]{1,0:T(8,128)}, f32[64,264]{1,0:T(8,128)}) custom-call(s32[3]{0:T(128)} %pad_add_fusion.at_ref, s32[1,256]{1,0:T(1,128)} %bitcast.40, f32[264,256]{1,0:T(8,128)} %get-tuple-element.35.slots_ref, f32[64,264]{1,0:T(8,128)} %bitcast.32), custom_call_target="tpu_custom_call" | custom-call | tf_op jit(solution)/shard_map/sketch/pallas_call | solution.py:559
  167.0 13.9 %factor.1 = (f32[256,256]{1,0:T(8,128)}, bf16[640,768]{1,0:T(8,128)(2,1)}) custom-call(s32[3]{0:T(128)} %pad_add_fusion.at_ref, f32[384,128]{1,0:T(8,128)} %get-tuple-element.32.mine_ref, f32[384,128]{1,0:T(8,128)S(1)} %collective-permute-done.7.other_ref, f32[640,256]{1,0:T(8,128)} %get-tuple-element.33.p_ref), custom_call_target="tpu_custom_call" | custom-call | tf_op jit(solution)/shard_map/factor/pallas_call | solution.py:527
  180.9 1.0 copy-done
  182.7 3.7 %share.1 = (f32[64,256]{1,0:T(8,128)}, f32[64,264]{1,0:T(8,128)}) custom-call(s32[3]{0:T(128)} %pad_add_fusion.at_ref, f32[384,128]{1,0:T(8,128)} %get-tuple-element.32.mine_ref, f32[384,128]{1,0:T(8,128)S(1)} %collective-permute-done.7.other_ref, f32[256,256]{1,0:T(8,128)} %get-tuple-element.34.inv_ref, f32[264,256]{1,0:T(8,128)S(1)} %copy-done, ...), custom_call_target="tpu_custom_call" | custom-call | tf_op jit(solution)/shard_map/share/pallas_call | solution.py:592
  186.4 7.7 %trailing.1 = f32[640,2048]{1,0:T(8,128)} custom-call(s32[3]{0:T(128)} %pad_add_fusion.at_ref, f32[640,2048]{1,0:T(8,128)} %permute.1.a_ref, bf16[640,768]{1,0:T(8,128)(2,1)} %get-tuple-element.40.b_ref, f32[16,128,128]{2,1,0:T(8,128)S(1)} %all_to_all.27.mine_ref, f32[16,128,128]{2,1,0:T(8,128)S(1)} %collective-permute-done.8.other_ref), custom_call_target="tpu_custom_call" | custom-call | tf_op jit(solution)/shard_map/trailing/pallas_call | solution.py:629
  (25 shorter events, 3.6 us)
Async XLA Ops:
  0.6 9.3 %collective-permute-start = (f32[64,264]{1,0:T(8,128)}, f32[64,264]{1,0:T(8,128)S(1)}, u32[]{:S(2)}, u32[]{:S(2)}) collective-permute-start(f32[64,264]{1,0:T(8,128)} %bitcast.30), channel_id=1, source_target_pairs={{0,1},{1,2},{2,3},{3,4},{4,5},{5,6},{6,7},{7,0},{8,9},{9,10},{10,1... | collective-permute-start | bytes 202760 | tf_op jit(solution)/shard_map/ppermute | solution.py:680
  10.0 0.6 copy-start.3
  14.3 2.4 %collective-permute-start.1 = (f32[4,4,1,16,256]{4,3,1,0,2:T(8,128)S(1)}, f32[4,4,1,16,256]{4,3,1,0,2:T(8,128)S(1)}, u32[]{:S(2)}, u32[]{:S(2)}) collective-permute-start(f32[4,4,1,16,256]{4,3,1,0,2:T(8,128)S(1)} %dynamic-slice_bitcast_fusion), channel_id=1, source_target_pairs={{0,8},{8,0},{1,9},{9,1},{2,10},{10,2},{3,11},{11,3},{4,12},{12,4},... | collective-permute-start | bytes 786440 | tf_op jit(solution)/shard_map/ppermute | solution.py:654
  17.6 9.7 %collective-permute-start.2 = (f32[4,2,16,256]{3,2,1,0:T(8,128)S(1)}, f32[4,2,16,256]{3,2,1,0:T(8,128)S(1)}, u32[]{:S(2)}, u32[]{:S(2)}) collective-permute-start(f32[4,2,16,256]{3,2,1,0:T(8,128)S(1)} %dynamic-slice_bitcast_fusion.1), channel_id=1, source_target_pairs={{0,48},{48,0},{16,32},{32,16},{1,49},{49,1},{17,33},{33,17},{2,50}... | collective-permute-start | bytes 393224 | tf_op jit(solution)/shard_map/ppermute | solution.py:654
  20.2 27.9 %all-to-all-start = ((f32[8,80,256]{2,1,0:T(8,128)}), f32[8,80,256]{2,1,0:T(8,128)S(1)}, u32[]{:S(2)}, u32[]{:S(2)}) async-start(f32[8,80,256]{2,1,0:T(8,128)} %bitcast.25), calls=%async_computation | async-start | bytes 1310720 | tf_op jit(solution)/shard_map/all_to_all | solution.py:644
  27.4 3.2 %collective-permute-start.3 = (f32[4,1,16,256]{3,2,1,0:T(8,128)S(1)}, f32[4,1,16,256]{3,2,1,0:T(8,128)S(1)}, u32[]{:S(2)}, u32[]{:S(2)}) collective-permute-start(f32[4,1,16,256]{3,2,1,0:T(8,128)S(1)} %constant_dynamic-slice_fusion.1), channel_id=1, source_target_pairs={{0,16},{16,0},{32,48},{48,32},{1,17},{17,1},{33,49},{49,33},{2,18}... | collective-permute-start | bytes 196616 | tf_op jit(solution)/shard_map/ppermute | solution.py:654
  30.6 4.4 %collective-permute-start.4 = (f32[2,16,256]{2,1,0:T(8,128)S(1)}, f32[2,16,256]{2,1,0:T(8,128)S(1)}, u32[]{:S(2)}, u32[]{:S(2)}) collective-permute-start(f32[2,16,256]{2,1,0:T(8,128)S(1)} %dynamic-slice_bitcast_fusion.2), channel_id=1, source_target_pairs={{0,192},{192,0},{64,128},{128,64},{1,193},{193,1},{65,129},{129,65... | collective-permute-start | bytes 98312 | tf_op jit(solution)/shard_map/ppermute | solution.py:654
  35.0 3.0 %collective-permute-start.5 = (f32[1,16,256]{2,1,0:T(8,128)S(1)}, f32[1,16,256]{2,1,0:T(8,128)S(1)}, u32[]{:S(2)}, u32[]{:S(2)}) collective-permute-start(f32[1,16,256]{2,1,0:T(8,128)S(1)} %constant_dynamic-slice_fusion), channel_id=1, source_target_pairs={{0,64},{64,0},{128,192},{192,128},{1,65},{65,1},{129,193},{193,129... | collective-permute-start | bytes 49160 | tf_op jit(solution)/shard_map/ppermute | solution.py:654
  49.8 27.0 %all-to-all-start.1 = ((f32[8,96,256]{2,1,0:T(8,128)}), f32[8,96,256]{2,1,0:T(8,128)S(1)}, u32[]{:S(2)}, u32[]{:S(2)}) async-start(f32[8,96,256]{2,1,0:T(8,128)} %holder.1), calls=%async_computation.1 | async-start | bytes 1572864 | tf_op jit(solution)/shard_map/all_to_all | solution.py:644
  81.4 9.6 %copy-start.2 = (f32[32,24,256]{2,1,0:T(8,128)S(1)}, f32[32,24,256]{2,1,0:T(8,128)}, u32[]{:S(2)}) copy-start(f32[32,24,256]{2,1,0:T(8,128)} %get-tuple-element.30) | copy-start | bytes 2359300
  90.3 19.6 %collective-permute-start.6 = (f32[16,128,128]{2,1,0:T(8,128)}, f32[16,128,128]{2,1,0:T(8,128)S(1)}, u32[]{:S(2)}, u32[]{:S(2)}) collective-permute-start(f32[16,128,128]{2,1,0:T(8,128)} %get-tuple-element.29), channel_id=1, source_target_pairs={{0,8},{8,0},{1,9},{9,1},{2,10},{10,2},{3,11},{11,3},{4,12},{12,4},... | collective-permute-start | bytes 3145736 | tf_op jit(solution)/shard_map/ppermute | solution.py:691
  154.9 31.5 %collective-permute-start.8 = (f32[16,128,128]{2,1,0:T(8,128)S(1)}, f32[16,128,128]{2,1,0:T(8,128)S(1)}, u32[]{:S(2)}, u32[]{:S(2)}) collective-permute-start(f32[16,128,128]{2,1,0:T(8,128)S(1)} %all_to_all.27.mine_ref), channel_id=1, source_target_pairs={{0,8},{8,0},{1,9},{9,1},{2,10},{10,2},{3,11},{11,3},{4,12},{12,4},... | collective-permute-start | bytes 3145736 | tf_op jit(solution)/shard_map/ppermute | solution.py:701
  157.1 9.9 %collective-permute-start.7 = (f32[384,128]{1,0:T(8,128)}, f32[384,128]{1,0:T(8,128)S(1)}, u32[]{:S(2)}, u32[]{:S(2)}) collective-permute-start(f32[384,128]{1,0:T(8,128)} %get-tuple-element.32.mine_ref), channel_id=1, source_target_pairs={{0,8},{8,0},{1,9},{9,1},{2,10},{10,2},{3,11},{11,3},{4,12},{12,4},... | collective-permute-start | bytes 589832 | tf_op jit(solution)/shard_map/ppermute | solution.py:698
  180.9 1.0 copy-start
  181.8 0.9 copy-start.1

commit v4 on v3

--- a/solution.py
+++ b/solution.py
@@ -226,83 +226,89 @@
     )(at, prow, partner, a)
 
 
-def holder_kernel(columns, prow_ref, r_ref, line_ref, o_ref):
-    peers, height, _ = r_ref.shape
+def holder_kernel(columns, prow_ref, r_ref, o_ref):
+    peers, _, _ = r_ref.shape
     prow = prow_ref[...]
     panel = r_ref[0]
     for s in range(1, peers):
         panel = jnp.where(owned(prow, s, columns), r_ref[s], panel)
     for s in range(peers):
-        o_ref[s, :height] = jnp.where(owned(prow, s, columns), r_ref[0], panel) if s else panel
-        o_ref[s, height:] = line_ref[...]
-
-
-def holder(prow, received, line, columns):
-    peers, height, n = received.shape
+        o_ref[s] = jnp.where(owned(prow, s, columns), r_ref[0], panel) if s else panel
+
+
+def holder(prow, received, columns):
     return pl.pallas_call(
         functools.partial(holder_kernel, columns),
-        out_shape=jax.ShapeDtypeStruct((peers, height + line.shape[0], n), f32),
-        in_specs=[held()] * 3,
+        out_shape=jax.ShapeDtypeStruct(received.shape, f32),
+        in_specs=[held()] * 2,
         name="holder",
-    )(prow, in_vmem(received), line)
-
-
-def gram_kernel(columns, at_ref, prow_ref, x_ref, m_ref, d0_ref, p_ref, d_ref, w_ref, g_ref, o_ref, x_s):
+    )(prow, in_vmem(received))
+
+
+def gram_kernel(columns, at_ref, prow_ref, x_ref, m_ref, d0_ref, p_ref, d_ref, w_ref, g_ref):
     c = at_ref[0]
-    peers = x_ref.shape[0]
-    rows, n = m_ref.shape
-    height = rows // peers
-    size = x_ref.shape[1] - height
-    lanes = o_ref.shape[0]
+    rows, _ = m_ref.shape
     prow = prow_ref[...]
     own = owned(prow, c, columns)
-    for s in range(peers):
-        x_s[s * height : (s + 1) * height, :] = x_ref[s, :height]
-    x = x_s[...]
+    x = x_ref[...]
     panel = jnp.where(own, m_ref[...], x)
     moved = jnp.where(c == 0, d0_ref[...], jnp.where(own, x, 0.0))
     p_ref[...] = panel
     d_ref[...] = abreast(moved)
     turned = panel.T
-    total = dot(turned, panel, NN, highest)
-    g_ref[...] = total
+    g_ref[...] = dot(turned, panel, NN, highest)
     left = stacked(turned)
     w_ref[:, :rows] = left
     w_ref[:, rows:] = stacked(product3(left, moved))
-    got = [x_ref[s, height : height + size] for s in range(peers)]
-    front = got[0]
+
+
+def gram(at, prow, x, m, d0, columns):
+    rows, n = m.shape
+    outs = (((rows, n), f32), ((rows, 2 * n), bf16), ((2 * n, rows + n), bf16), ((n, n), f32))
+    return pl.pallas_call(
+        functools.partial(gram_kernel, columns),
+        out_shape=tuple(jax.ShapeDtypeStruct(s, t) for s, t in outs),
+        grid_spec=pltpu.PrefetchScalarGridSpec(
+            num_scalar_prefetch=1,
+            grid=(1,),
+            in_specs=[held()] * 4,
+            out_specs=tuple(whole(s) for s, _ in outs),
+        ),
+        name="gram",
+    )(at, prow, in_vmem(x), m, d0)
+
+
+def message_kernel(columns, at_ref, prow_ref, g_ref, got_ref, o_ref):
+    c = at_ref[0]
+    peers = got_ref.shape[0]
+    lanes = o_ref.shape[0]
+    n = g_ref.shape[0]
+    prow = prow_ref[...]
+    front = got_ref[0]
     for s in range(1, peers):
-        front = jnp.where(owned(prow, s, columns), got[s], front)
-    back = jnp.where(c == 0, got[1], got[0])
+        front = jnp.where(owned(prow, s, columns), got_ref[s], front)
+    back = jnp.where(c == 0, got_ref[1], got_ref[0])
     part = n // lanes
     share = columns // lanes
     for i in range(lanes):
-        o_ref[i, :part] = total[i * part : (i + 1) * part]
+        o_ref[i, :part] = g_ref[i * part : (i + 1) * part]
         o_ref[i, part:] = jnp.where(owned(prow, c * lanes + i, share), back, front)
 
 
-def gram(at, prow, x, m, d0, columns, lanes):
-    rows, n = m.shape
-    piece = n // lanes + x.shape[1] - rows // x.shape[0]
-    outs = (
-        ((rows, n), f32),
-        ((rows, 2 * n), bf16),
-        ((2 * n, rows + n), bf16),
-        ((n, n), f32),
-        ((lanes, piece, n), f32),
-    )
-    return pl.pallas_call(
-        functools.partial(gram_kernel, columns),
-        out_shape=tuple(jax.ShapeDtypeStruct(s, t) for s, t in outs),
-        grid_spec=pltpu.PrefetchScalarGridSpec(
-            num_scalar_prefetch=1,
-            grid=(1,),
-            in_specs=[held()] * 4,
-            out_specs=tuple(whole(s) for s, _ in outs),
-            scratch_shapes=[pltpu.VMEM((rows, n), f32)],
-        ),
-        name="gram",
-    )(at, prow, in_vmem(x), m, d0)
+def message_of(at, prow, g, got, columns, lanes):
+    n = g.shape[0]
+    out = (lanes, n // lanes + got.shape[1], n)
+    return pl.pallas_call(
+        functools.partial(message_kernel, columns),
+        out_shape=jax.ShapeDtypeStruct(out, f32),
+        grid_spec=pltpu.PrefetchScalarGridSpec(
+            num_scalar_prefetch=1,
+            grid=(1,),
+            in_specs=[held()] * 3,
+            out_specs=whole(out),
+        ),
+        name="message",
+    )(at, prow, g, in_vmem(got))
 
 
 def half_kernel(part, keep_ref, sent_ref, got_ref, o_ref, line_ref):
@@ -644,6 +650,10 @@
     return lax.all_to_all(pieces, axis, split_axis=0, concat_axis=0, tiled=True)
 
 
+def to_all(piece, axis):
+    return exchange(jnp.broadcast_to(piece[None], (lax.axis_size(axis), *piece.shape)), axis)
+
+
 def side_of(value, which, dim):
     return lax.dynamic_index_in_dim(value, which, dim, keepdims=False)
 
@@ -683,9 +693,11 @@
     picks = pick_sketch(at, prow, partner, turned, first, columns, lanes)
     line = sum_at_rows(picks)
     inside = inside_of(at, prow, partner, matrix)
-    message = holder(prow, arrived, line, columns)
-    x = exchange(message, "col")
-    panel, displaced, w, gram_part, message = gram(at, prow, x, mine, inside, columns, lanes)
+    message = holder(prow, arrived, columns)
+    x = exchange(message, "col").reshape(rows, n)
+    got = to_all(line, "col")
+    panel, displaced, w, gram_part = gram(at, prow, x, mine, inside, columns)
+    message = message_of(at, prow, gram_part, got, columns, lanes)
     gram_pieces = exchange(message, ROW)
     keep, send = product(at, pcol, matrix, w, gram_part, chips)
     sent = lax.ppermute(send, "row_2", swap)

time: 195 us -> 206 us (1.056)
  blocking collectives: 60.3 us -> 72.9 us
  waiting for transfers between devices: 38.7 us -> 31 us
  starting transfers between devices: 22.7 us -> 27.2 us
  Pallas kernels: 65.8 us -> 67.9 us
    all_to_all x2, waiting for transfers between devices: 30 us -> 9.92 us  [exchange(): return lax.all_to_all(pieces, axis, split_axis=0, concat_axis=0, tiled=True)]
    ppermute x1, waiting for transfers between devices: 0.01 us -> 15.2 us  [per_device(): lax.ppermute(turned, 'col', [(i, (i + 1) % cols) for i in range(cols)])]
    all_to_all x3 -> x4, blocking collectives: 60.3 us -> 72.9 us  [exchange(): return lax.all_to_all(pieces, axis, split_axis=0, concat_axis=0, tiled=True)]
    all_to_all x2, starting transfers between devices: 10.7 us -> 14 us  [exchange(): return lax.all_to_all(pieces, axis, split_axis=0, concat_axis=0, tiled=True)]
    ppermute x5, waiting for transfers between devices: 8.72 us -> 5.86 us  [halved(): lax.ppermute(side_of(value, 1 - which, dim), axis, swap)]
    pallas_call x0 -> x1, Pallas kernels: none -> 2.59 us  [message_of(): pl.pallas_call(functools.partial(message_kernel, columns), out_shape=jax....]
    ppermute x5, starting transfers between devices: 6.76 us -> 8.96 us  [halved(): lax.ppermute(side_of(value, 1 - which, dim), axis, swap)]
  transfers between devices with their start and end apart: 11 -> 11, of which waited for: 6 -> 5; matrix products, arithmetic and copies ran while one was open for 1% -> 1% of each run, Pallas kernels for 19% -> 25%
where the time goes in v4:
time: 206 us; the launch traced here: 205 us
  blocking collectives  72.9 us (35%)
  Pallas kernels  67.9 us (33%)
  waiting for transfers between devices  31 us (15%)
  starting transfers between devices  27.2 us (13%)
  local copies, waits for them, and re-layouts  3.54 us (2%)
    all_to_all x4, blocking collectives, exchange(): return lax.all_to_all(pieces, axis, split_axis=0, concat_axis=0, tiled=True)  72.9 us
    ppermute x1, waiting for transfers between devices, per_device(): lax.ppermute(turned, 'col', [(i, (i + 1) % cols) for i in range(cols)])  15.2 us
    all_to_all x2, starting transfers between devices, exchange(): return lax.all_to_all(pieces, axis, split_axis=0, concat_axis=0, tiled=True)  14 us
    pallas_call x1, Pallas kernels, factor(): pl.pallas_call(factor_kernel, out_shape=tuple((jax.ShapeDtypeStruct(s, t)...  13.8 us
    all_to_all x2, waiting for transfers between devices, exchange(): return lax.all_to_all(pieces, axis, split_axis=0, concat_axis=0, tiled=True)  9.92 us
    ppermute x5, starting transfers between devices, halved(): lax.ppermute(side_of(value, 1 - which, dim), axis, swap)  8.96 us
    pallas_call x1, Pallas kernels, product(): pl.pallas_call(product_kernel, out_shape=(jax.ShapeDtypeStruct(shape, f32...  8.83 us
    pallas_call x1, Pallas kernels, trail(): pl.pallas_call(trailing_kernel, out_shape=jax.ShapeDtypeStruct(a.shape, f...  7.74 us
  transfers between devices with their start and end apart: 11, of which 5 were waited for; matrix products, arithmetic and copies ran while one was open for 1% of the time, Pallas kernels for 25%

profile of v4, /device:TPU:1, one launch (start us, length us, event | category | flops | bytes accessed | tf_op | source)
XLA Modules:
  0.0 205.1 jit_solution(2005947615329512075)
XLA Ops:
  1.3 6.1 %extract.1 = (f32[640,256]{1,0:T(8,128)}, s32[1,256]{1,0:T(1,128)}, s32[256,128]{1,0:T(8,128)}) custom-call(s32[3]{0:T(128)} %pad_add_fusion.at_ref, s32[1,256]{1,0:T(1,128)} %bitcast.38, f32[640,2048]{1,0:T(8,128)} %a_ref.7), custom_call_target="tpu_custom_call" | custom-call | tf_op jit(solution)/shard_map/extract/pallas_call | solution.py:155
  7.4 9.1 %all-to-all-start = ((f32[8,80,256]{2,1,0:T(8,128)}), f32[8,80,256]{2,1,0:T(8,128)S(1)}, u32[]{:S(2)}, u32[]{:S(2)}) async-start(f32[8,80,256]{2,1,0:T(8,128)} %bitcast.28), calls=%async_computation | async-start | bytes 1310720 | tf_op jit(solution)/shard_map/all_to_all | solution.py:650
  16.4 1.5 collective-permute-start.1
  17.9 15.2 %collective-permute-done.1.first_ref = f32[64,264]{1,0:T(8,128)S(1)} collective-permute-done((f32[64,264]{1,0:T(8,128)S(1)}, f32[64,264]{1,0:T(8,128)S(1)}, u32[]{:S(2)}, u32[]{:S(2)}) %collective-permute-start.1) | collective-permute-done | bytes 67616 | tf_op jit(solution)/shard_map/ppermute | solution.py:690
  33.8 2.7 %pick.1 = f32[32,16,256]{2,1,0:T(8,128)} custom-call(s32[3]{0:T(128)} %pad_add_fusion.at_ref, s32[1,256]{1,0:T(1,128)} %bitcast.39, s32[1,256]{1,0:T(1,128)} %get-tuple-element.24.partner_ref, f32[64,264]{1,0:T(8,128)} %bitcast.32, f32[64,264]{1,0:T(8,128)} %copy-done.3), custom_call_target="tpu_custom_call" | custom-call | tf_op jit(solution)/shard_map/pick/pallas_call | solution.py:193
  36.5 1.0 dynamic-slice_bitcast_fusion
  37.4 3.4 %collective-permute-start.2 = (f32[4,4,1,16,256]{4,3,1,0,2:T(8,128)S(1)}, f32[4,4,1,16,256]{4,3,1,0,2:T(8,128)S(1)}, u32[]{:S(2)}, u32[]{:S(2)}) collective-permute-start(f32[4,4,1,16,256]{4,3,1,0,2:T(8,128)S(1)} %dynamic-slice_bitcast_fusion), channel_id=1, source_target_pairs={{0,8},{8,0},{1,9},{9,1},{2,10},{10,2},{3,11},{11,3},{4,12},{12,4},... | collective-permute-start | bytes 786440 | tf_op jit(solution)/shard_map/ppermute | solution.py:664
  40.9 1.2 collective-permute-done.2
  42.0 1.0 bitcast_add_fusion
  43.1 2.5 %collective-permute-start.3 = (f32[4,2,16,256]{3,2,0,1:T(8,128)S(1)}, f32[4,2,16,256]{3,2,0,1:T(8,128)S(1)}, u32[]{:S(2)}, u32[]{:S(2)}) collective-permute-start(f32[4,2,16,256]{3,2,0,1:T(8,128)S(1)} %bitcast.37), channel_id=1, source_target_pairs={{0,48},{48,0},{16,32},{32,16},{1,49},{49,1},{17,33},{33,17},{2,50}... | collective-permute-start | bytes 393224 | tf_op jit(solution)/shard_map/ppermute | solution.py:664
  45.6 1.6 holder.1
  47.2 4.9 %all-to-all-start.1 = ((f32[8,80,256]{2,1,0:T(8,128)}), f32[8,80,256]{2,1,0:T(8,128)S(1)}, u32[]{:S(2)}, u32[]{:S(2)}) async-start(f32[8,80,256]{2,1,0:T(8,128)} %holder.1), calls=%async_computation.1 | async-start | bytes 1310720 | tf_op jit(solution)/shard_map/all_to_all | solution.py:650
  52.3 3.1 %collective-permute-done.4 = f32[4,1,16,256]{3,2,0,1:T(8,128)S(1)} collective-permute-done((f32[4,1,16,256]{3,2,0,1:T(8,128)S(1)}, f32[4,1,16,256]{3,2,0,1:T(8,128)S(1)}, u32[]{:S(2)}, u32[]{:S(2)}) %collective-permute-start.4) | collective-permute-done | bytes 65568 | tf_op jit(solution)/shard_map/ppermute | solution.py:664
  55.4 2.8 %collective-permute-start.5 = (f32[2,16,256]{2,1,0:T(8,128)S(1)}, f32[2,16,256]{2,1,0:T(8,128)S(1)}, u32[]{:S(2)}, u32[]{:S(2)}) collective-permute-start(f32[2,16,256]{2,1,0:T(8,128)S(1)} %dynamic-slice_bitcast_fusion.1), channel_id=1, source_target_pairs={{0,192},{192,0},{64,128},{128,64},{1,193},{193,1},{65,129},{129,65... | collective-permute-start | bytes 98312 | tf_op jit(solution)/shard_map/ppermute | solution.py:664
  58.3 1.6 collective-permute-done.5
  60.0 3.0 %inside.1.d0_ref = f32[640,256]{1,0:T(8,128)} custom-call(s32[3]{0:T(128)} %pad_add_fusion.at_ref, s32[1,256]{1,0:T(1,128)} %bitcast.41, s32[1,256]{1,0:T(1,128)} %get-tuple-element.24.partner_ref, f32[640,2048]{1,0:T(8,128)} %a_ref.7), custom_call_target="tpu_custom_call" | custom-call | tf_op jit(solution)/shard_map/inside/pallas_call | solution.py:216
  63.0 9.9 %all-to-all-done.1 = f32[8,80,256]{2,1,0:T(8,128)S(1)} async-done(((f32[8,80,256]{2,1,0:T(8,128)}), f32[8,80,256]{2,1,0:T(8,128)S(1)}, u32[]{:S(2)}, u32[]{:S(2)}) %all-to-all-start.1) | async-done | bytes 655392 | tf_op jit(solution)/shard_map/all_to_all | solution.py:650
  72.9 4.2 %gram.1 = (f32[640,256]{1,0:T(8,128)}, bf16[640,512]{1,0:T(8,128)(2,1)}, bf16[512,896]{1,0:T(8,128)(2,1)}, f32[256,256]{1,0:T(8,128)}) custom-call(s32[3]{0:T(128)} %pad_add_fusion.at_ref, s32[1,256]{1,0:T(1,128)} %bitcast.42, f32[640,256]{1,0:T(8,128)S(1)} %bitcast.27, f32[640,256]{1,0:T(8,128)} %get-tuple-element.23.m_ref, f32[640,256]{1,0:T(8,128)} %inside.1.d0_ref), custom_call_target="tpu_custom_call" | custom-call | tf_op jit(solution)/shard_map/gram/pallas_call | solution.py:268
  77.1 8.8 %product.1 = (f32[16,128,128]{2,1,0:T(8,128)}, f32[16,128,128]{2,1,0:T(8,128)}) custom-call(s32[3]{0:T(128)} %pad_add_fusion.at_ref, s32[256,128]{1,0:T(8,128)} %get-tuple-element.22.pcol_ref, f32[640,2048]{1,0:T(8,128)} %a_ref.7, bf16[512,896]{1,0:T(8,128)(2,1)} %get-tuple-element.25.w_ref, f32[256,256]{1,0:T(8,128)} %get-tuple-element.26.g_ref), custom_call_target="tpu_custom_call" | custom-call | tf_op jit(solution)/shard_map/product/pallas_call | solution.py:422
  86.5 11.8 %all_to_all.30.got_ref = f32[8,16,256]{2,1,0:T(8,128)S(1)} all-to-all(f32[8,16,256]{2,1,0:T(8,128)S(1)} %broadcast_in_dim.8), channel_id=1, replica_groups=mesh['row_0'=4,'row_1'=4,'row_2'=2,'col'=8] {'col'}, dimensions={0} | all-to-all | bytes 262144 | tf_op jit(solution)/shard_map/all_to_all | solution.py:650
  98.4 2.6 %message.1 = f32[32,24,256]{2,1,0:T(8,128)} custom-call(s32[3]{0:T(128)} %pad_add_fusion.at_ref, s32[1,256]{1,0:T(1,128)} %bitcast.43, f32[256,256]{1,0:T(8,128)} %get-tuple-element.26.g_ref, f32[8,16,256]{2,1,0:T(8,128)S(1)} %all_to_all.30.got_ref), custom_call_target="tpu_custom_call" | custom-call | tf_op jit(solution)/shard_map/message/pallas_call | solution.py:301
  101.0 19.7 %all_to_all.31.got_ref = f32[32,24,256]{2,1,0:T(8,128)S(1)} all-to-all(f32[32,24,256]{2,1,0:T(8,128)} %message.1), channel_id=1, replica_groups=mesh['row_0'=4,'row_1'=4,'row_2'=2,'col'=8] {'row_0','row_1','row_2'}, dimensions={0} | all-to-all | bytes 1572864 | tf_op jit(solution)/shard_map/all_to_all | solution.py:650
  120.7 2.5 %half.1 = (f32[16,144,128]{2,1,0:T(8,128)}, f32[264,256]{1,0:T(8,128)}) custom-call(f32[16,128,128]{2,1,0:T(8,128)} %get-tuple-element.27.keep_ref, f32[16,128,128]{2,1,0:T(8,128)S(1)} %collective-permute-done.sent_ref, f32[32,24,256]{2,1,0:T(8,128)S(1)} %all_to_all.31.got_ref), custom_call_target="tpu_custom_call" | custom-call | tf_op jit(solution)/shard_map/half/pallas_call | solution.py:336
  123.1 21.8 %all_to_all.32.r_ref = f32[16,144,128]{2,1,0:T(8,128)S(1)} all-to-all(f32[16,144,128]{2,1,0:T(8,128)} %get-tuple-element.29), channel_id=1, replica_groups=mesh['row_0'=4,'row_1'=4,'row_2'=2,'col'=8] {'row_0','row_1'}, dimensions={0} | all-to-all | bytes 2359296 | tf_op jit(solution)/shard_map/all_to_all | solution.py:650
  144.9 1.2 total.1
  146.1 19.5 %all_to_all.33.mine_ref = f32[16,128,128]{2,1,0:T(8,128)S(1)} all-to-all(f32[16,128,128]{2,1,0:T(8,128)} %get-tuple-element.39), channel_id=1, replica_groups=mesh['row_0'=4,'row_1'=4,'row_2'=2,'col'=8] {'row_0','row_1'}, dimensions={0} | all-to-all | bytes 2097152 | tf_op jit(solution)/shard_map/all_to_all | solution.py:650
  165.6 2.2 %collective-permute-start.8 = (f32[16,128,128]{2,1,0:T(8,128)S(1)}, f32[16,128,128]{2,1,0:T(8,128)S(1)}, u32[]{:S(2)}, u32[]{:S(2)}) collective-permute-start(f32[16,128,128]{2,1,0:T(8,128)S(1)} %all_to_all.33.mine_ref), channel_id=1, source_target_pairs={{0,8},{8,0},{1,9},{9,1},{2,10},{10,2},{3,11},{11,3},{4,12},{12,4},... | collective-permute-start | bytes 3145736 | tf_op jit(solution)/shard_map/ppermute | solution.py:713
  167.8 7.0 %permute.1.a_ref = f32[640,2048]{1,0:T(8,128)} custom-call(s32[3]{0:T(128)} %pad_add_fusion.at_ref, s32[256,128]{1,0:T(8,128)} %get-tuple-element.22.pcol_ref, f32[640,2048]{1,0:T(8,128)} %a_ref.7, f32[640,256]{1,0:T(8,128)} %get-tuple-element.31.p_ref, bf16[640,512]{1,0:T(8,128)(2,1)} %get-tuple-element.37.d_ref), custom_call_target="tpu_custom_call" | custom-call | tf_op jit(solution)/shard_map/permute/pallas_call | solution.py:462
  174.8 3.0 %sketch.1 = (f32[264,256]{1,0:T(8,128)}, f32[64,264]{1,0:T(8,128)}) custom-call(s32[3]{0:T(128)} %pad_add_fusion.at_ref, s32[1,256]{1,0:T(1,128)} %bitcast.44, f32[264,256]{1,0:T(8,128)} %get-tuple-element.33.slots_ref, f32[64,264]{1,0:T(8,128)} %bitcast.33), custom_call_target="tpu_custom_call" | custom-call | tf_op jit(solution)/shard_map/sketch/pallas_call | solution.py:565
  177.8 13.8 %factor.1 = (f32[256,256]{1,0:T(8,128)}, bf16[640,768]{1,0:T(8,128)(2,1)}) custom-call(s32[3]{0:T(128)} %pad_add_fusion.at_ref, f32[384,128]{1,0:T(8,128)} %get-tuple-element.30.mine_ref, f32[384,128]{1,0:T(8,128)S(1)} %collective-permute-done.7.other_ref, f32[640,256]{1,0:T(8,128)} %get-tuple-element.31.p_ref), custom_call_target="tpu_custom_call" | custom-call | tf_op jit(solution)/shard_map/factor/pallas_call | solution.py:533
  193.5 3.7 %share.1 = (f32[64,256]{1,0:T(8,128)}, f32[64,264]{1,0:T(8,128)}) custom-call(s32[3]{0:T(128)} %pad_add_fusion.at_ref, f32[384,128]{1,0:T(8,128)} %get-tuple-element.30.mine_ref, f32[384,128]{1,0:T(8,128)S(1)} %collective-permute-done.7.other_ref, f32[256,256]{1,0:T(8,128)} %get-tuple-element.32.inv_ref, f32[264,256]{1,0:T(8,128)S(1)} %copy-done, ...), custom_call_target="tpu_custom_call" | custom-call | tf_op jit(solution)/shard_map/share/pallas_call | solution.py:598
  197.2 7.7 %trailing.1 = f32[640,2048]{1,0:T(8,128)} custom-call(s32[3]{0:T(128)} %pad_add_fusion.at_ref, f32[640,2048]{1,0:T(8,128)} %permute.1.a_ref, bf16[640,768]{1,0:T(8,128)(2,1)} %get-tuple-element.38.b_ref, f32[16,128,128]{2,1,0:T(8,128)S(1)} %all_to_all.33.mine_ref, f32[16,128,128]{2,1,0:T(8,128)S(1)} %collective-permute-done.8.other_ref), custom_call_target="tpu_custom_call" | custom-call | tf_op jit(solution)/shard_map/trailing/pallas_call | solution.py:635
  (29 shorter events, 4.0 us)
Async XLA Ops:
  0.6 15.8 %copy-start.2 = (f32[264,64]{0,1:T(8,128)S(1)}, f32[264,64]{0,1:T(8,128)}, u32[]{:S(2)}) copy-start(f32[264,64]{0,1:T(8,128)} %param.5) | copy-start | bytes 202756
  7.4 38.2 %all-to-all-start = ((f32[8,80,256]{2,1,0:T(8,128)}), f32[8,80,256]{2,1,0:T(8,128)S(1)}, u32[]{:S(2)}, u32[]{:S(2)}) async-start(f32[8,80,256]{2,1,0:T(8,128)} %bitcast.28), calls=%async_computation | async-start | bytes 1310720 | tf_op jit(solution)/shard_map/all_to_all | solution.py:650
  16.4 16.7 %collective-permute-start.1 = (f32[64,264]{1,0:T(8,128)S(1)}, f32[64,264]{1,0:T(8,128)S(1)}, u32[]{:S(2)}, u32[]{:S(2)}) collective-permute-start(f32[64,264]{1,0:T(8,128)S(1)} %bitcast.34), channel_id=1, source_target_pairs={{0,1},{1,2},{2,3},{3,4},{4,5},{5,6},{6,7},{7,0},{8,9},{9,10},{10,1... | collective-permute-start | bytes 202760 | tf_op jit(solution)/shard_map/ppermute | solution.py:690
  33.1 0.6 copy-start.3
  37.4 4.6 %collective-permute-start.2 = (f32[4,4,1,16,256]{4,3,1,0,2:T(8,128)S(1)}, f32[4,4,1,16,256]{4,3,1,0,2:T(8,128)S(1)}, u32[]{:S(2)}, u32[]{:S(2)}) collective-permute-start(f32[4,4,1,16,256]{4,3,1,0,2:T(8,128)S(1)} %dynamic-slice_bitcast_fusion), channel_id=1, source_target_pairs={{0,8},{8,0},{1,9},{9,1},{2,10},{10,2},{3,11},{11,3},{4,12},{12,4},... | collective-permute-start | bytes 786440 | tf_op jit(solution)/shard_map/ppermute | solution.py:664
  43.1 9.1 %collective-permute-start.3 = (f32[4,2,16,256]{3,2,0,1:T(8,128)S(1)}, f32[4,2,16,256]{3,2,0,1:T(8,128)S(1)}, u32[]{:S(2)}, u32[]{:S(2)}) collective-permute-start(f32[4,2,16,256]{3,2,0,1:T(8,128)S(1)} %bitcast.37), channel_id=1, source_target_pairs={{0,48},{48,0},{16,32},{32,16},{1,49},{49,1},{17,33},{33,17},{2,50}... | collective-permute-start | bytes 393224 | tf_op jit(solution)/shard_map/ppermute | solution.py:664
  47.2 25.7 %all-to-all-start.1 = ((f32[8,80,256]{2,1,0:T(8,128)}), f32[8,80,256]{2,1,0:T(8,128)S(1)}, u32[]{:S(2)}, u32[]{:S(2)}) async-start(f32[8,80,256]{2,1,0:T(8,128)} %holder.1), calls=%async_computation.1 | async-start | bytes 1310720 | tf_op jit(solution)/shard_map/all_to_all | solution.py:650
  52.2 3.2 %collective-permute-start.4 = (f32[4,1,16,256]{3,2,0,1:T(8,128)S(1)}, f32[4,1,16,256]{3,2,0,1:T(8,128)S(1)}, u32[]{:S(2)}, u32[]{:S(2)}) collective-permute-start(f32[4,1,16,256]{3,2,0,1:T(8,128)S(1)} %constant_dynamic-slice_fusion.1), channel_id=1, source_target_pairs={{0,16},{16,0},{32,48},{48,32},{1,17},{17,1},{33,49},{49,33},{2,18}... | collective-permute-start | bytes 196616 | tf_op jit(solution)/shard_map/ppermute | solution.py:664
  55.4 4.4 %collective-permute-start.5 = (f32[2,16,256]{2,1,0:T(8,128)S(1)}, f32[2,16,256]{2,1,0:T(8,128)S(1)}, u32[]{:S(2)}, u32[]{:S(2)}) collective-permute-start(f32[2,16,256]{2,1,0:T(8,128)S(1)} %dynamic-slice_bitcast_fusion.1), channel_id=1, source_target_pairs={{0,192},{192,0},{64,128},{128,64},{1,193},{193,1},{65,129},{129,65... | collective-permute-start | bytes 98312 | tf_op jit(solution)/shard_map/ppermute | solution.py:664
  59.9 26.6 %collective-permute-start.6 = (f32[1,16,256]{2,1,0:T(8,128)S(1)}, f32[1,16,256]{2,1,0:T(8,128)S(1)}, u32[]{:S(2)}, u32[]{:S(2)}) collective-permute-start(f32[1,16,256]{2,1,0:T(8,128)S(1)} %constant_dynamic-slice_fusion), channel_id=1, source_target_pairs={{0,64},{64,0},{128,192},{192,128},{1,65},{65,1},{129,193},{193,129... | collective-permute-start | bytes 49160 | tf_op jit(solution)/shard_map/ppermute | solution.py:664
  85.9 34.7 %collective-permute-start = (f32[16,128,128]{2,1,0:T(8,128)}, f32[16,128,128]{2,1,0:T(8,128)S(1)}, u32[]{:S(2)}, u32[]{:S(2)}) collective-permute-start(f32[16,128,128]{2,1,0:T(8,128)} %get-tuple-element.28), channel_id=1, source_target_pairs={{0,8},{8,0},{1,9},{9,1},{2,10},{10,2},{3,11},{11,3},{4,12},{12,4},... | collective-permute-start | bytes 3145736 | tf_op jit(solution)/shard_map/ppermute | solution.py:703
  165.6 31.6 %collective-permute-start.8 = (f32[16,128,128]{2,1,0:T(8,128)S(1)}, f32[16,128,128]{2,1,0:T(8,128)S(1)}, u32[]{:S(2)}, u32[]{:S(2)}) collective-permute-start(f32[16,128,128]{2,1,0:T(8,128)S(1)} %all_to_all.33.mine_ref), channel_id=1, source_target_pairs={{0,8},{8,0},{1,9},{9,1},{2,10},{10,2},{3,11},{11,3},{4,12},{12,4},... | collective-permute-start | bytes 3145736 | tf_op jit(solution)/shard_map/ppermute | solution.py:713
  167.8 10.0 %collective-permute-start.7 = (f32[384,128]{1,0:T(8,128)}, f32[384,128]{1,0:T(8,128)S(1)}, u32[]{:S(2)}, u32[]{:S(2)}) collective-permute-start(f32[384,128]{1,0:T(8,128)} %get-tuple-element.30.mine_ref), channel_id=1, source_target_pairs={{0,8},{8,0},{1,9},{9,1},{2,10},{10,2},{3,11},{11,3},{4,12},{12,4},... | collective-permute-start | bytes 589832 | tf_op jit(solution)/shard_map/ppermute | solution.py:710
  191.7 1.0 copy-start
  192.6 0.9 copy-start.1
